TPU v7x, 32 devices: a whole 2x2x4 slice. The times are simulated.
32 devices in a mesh: fsdp: 4 (over z), context: 4 (over y, x), tensor: 2 (over core).
Axes of the slice: x: 2, y: 2, z: 4, core: 2. Of those that a mesh axis runs over, the one named last changes fastest.
Arguments:
- tokens: float32 [12, 1408, 1024], P('fsdp', 'context'), may hold values from -6 to 6
- cotangent: float32 [12, 1408, 1024], P('fsdp', 'context'), may hold values from -6 to 6
- gains: float32 [4, 1024], replicated, may hold values from 0.5 to 1.5
- w_qkv: bfloat16 [1024, 3, 1024], P('fsdp', None, 'tensor'), may hold values from -0.1875 to 0.1875
- w_out: bfloat16 [1024, 1024], P('tensor', 'fsdp'), may hold values from -4 to 4
- w_up: bfloat16 [1024, 4096], P('fsdp', 'tensor'), may hold values from -0.1875 to 0.1875
- w_down: bfloat16 [4096, 1024], P('tensor', 'fsdp'), may hold values from -0.09375 to 0.09375
- key_mask: int32 [12, 1408], P('fsdp', 'context'), may hold values from 0 to 1, as said below
- owner: int32 [12], replicated, may hold values from 0 to 11, each once
- stat_left: float32 [12, 2, 512, 1024], P('context', 'tensor', 'fsdp'), may hold values from -120 to 640
- stat_right: float32 [12, 2, 512, 1024], P('context', 'tensor', 'fsdp'), may hold values from -120 to 640
- root_left: float32 [12, 2, 512, 1024], P('context', 'tensor', 'fsdp'), may hold values from -3 to 24
- root_right: float32 [12, 1024, 1024], P('context'), may hold values from -0.3 to 1.6
- master: float32 [12, 2, 512, 1024], P('context', 'tensor', 'fsdp'), may hold values from -6 to 6
- gain_state: float32 [4, 1024], P(None, ('fsdp', 'context')), may hold values from 0.5 to 4
Outputs:
- output: float32 [12, 1408, 1024], P('fsdp', 'context')
- grad_tokens: float32 [12, 1408, 1024], P('fsdp', 'context')
- grad_blocks: float32 [12, 2, 512, 1024], P('context', 'tensor', 'fsdp')
- stat_left_new: float32 [12, 2, 512, 1024], P('context', 'tensor', 'fsdp')
- stat_right_new: float32 [12, 2, 512, 1024], P('context', 'tensor', 'fsdp')
- weight_new: float32 [12, 2, 512, 1024], P('context', 'tensor', 'fsdp')
- gain_grad: float32 [4, 1024], P(None, ('fsdp', 'context'))
- gain_state_new: float32 [4, 1024], P(None, ('fsdp', 'context'))
- gain_new: float32 [4, 1024], P(None, ('fsdp', 'context'))
Inputs may be any that keep to these rules, and one draw needn't show every extreme that they name: `key_mask`: each image's real tokens are its first p * p + 1 positions, for a whole p from 28 to 37; some image has p = 37.
All inputs are finite; a program needn't handle non-finite values.
Results may differ from a plain program's by a relative error of at most 0.012.
Values may be sent and summed in bfloat16 or wider, within the bound.
A program may use at most 256 MiB of HBM per device.

v0:
```python
import jax
import jax.numpy as jnp
from jax import lax
from jax.sharding import PartitionSpec as P

D = 1024
HD = 64
SEQ = 1408
NBLK = 12


def norm_fwd(field_in, gain_vec):
    centred = field_in - jnp.mean(field_in, axis=-1, keepdims=True)
    inv_std = lax.rsqrt(jnp.mean(centred * centred, axis=-1, keepdims=True) + 1e-06)
    normed = centred * inv_std
    return (normed, inv_std, normed * gain_vec)


def norm_back(grad_out, gain_vec, normed, inv_std):
    scaled = grad_out * gain_vec
    inner_sum = (
        scaled
        - jnp.mean(scaled, axis=-1, keepdims=True)
        - normed * jnp.mean(scaled * normed, axis=-1, keepdims=True)
    )
    return (inner_sum * inv_std, jnp.sum(grad_out * normed, axis=(0, 1)))


def gelu_parts(field_in):
    normal_cdf = 0.5 * (1.0 + lax.erf(field_in * 0.7071067811865476))
    normal_pdf = jnp.exp(-0.5 * field_in * field_in) * 0.3989422804014327
    return (field_in * normal_cdf, normal_cdf + field_in * normal_pdf)


def split_heads(field_in):
    shaped = field_in.reshape(field_in.shape[0], field_in.shape[1], field_in.shape[2] // HD, HD)
    return jnp.moveaxis(shaped, 2, 0)


def join_heads(field_in):
    moved_axes = jnp.moveaxis(field_in, 0, 2)
    return moved_axes.reshape(moved_axes.shape[0], moved_axes.shape[1], -1)


def per_device(
    tokens,
    cotangent,
    gains,
    w_qkv,
    w_out,
    w_up,
    w_down,
    key_mask,
    owner,
    stat_left,
    stat_right,
    root_left,
    root_right,
    master,
    gain_state,
):
    images = tokens.shape[0]
    local_len = tokens.shape[1]
    tok_rows = images * local_len
    score_scale = HD ** (-0.5)
    qkv_full, out_full, up_full, down_full = (
        lax.all_gather(w_qkv, "fsdp", axis=0, tiled=True),
        lax.all_gather(w_out, "fsdp", axis=1, tiled=True),
        lax.all_gather(w_up, "fsdp", axis=0, tiled=True),
        lax.all_gather(w_down, "fsdp", axis=1, tiled=True),
    )
    half_width = qkv_full.shape[2]
    hidden = up_full.shape[1]
    up_blocks = hidden // half_width
    normed1, inv_std1, pre_norm1 = norm_fwd(tokens, gains[0])
    normed1_low = pre_norm1.astype(jnp.bfloat16)
    qkv = jnp.einsum(
        "isd,djh->isjh", normed1_low, qkv_full, preferred_element_type=jnp.float32
    ).astype(jnp.bfloat16)
    kv_local = qkv[:, :, 1:]
    key_flag = key_mask.astype(jnp.bfloat16)
    keys_vals, key_live = (
        lax.all_gather(kv_local, "context", axis=1, tiled=True),
        lax.all_gather(key_flag, "context", axis=1, tiled=True),
    )

    def head_forward(operands):
        queries, key_rows, value_rows = operands
        scores = (
            jnp.einsum("iqd,ikd->iqk", queries, key_rows, preferred_element_type=jnp.float32)
            * score_scale
        )
        scores = jnp.where(key_live[:, None, :] > 0, scores, -1e30)
        peak_val = jnp.max(scores, axis=-1, keepdims=True)
        expo_val = jnp.exp(scores - peak_val)
        totals = jnp.sum(expo_val, axis=-1, keepdims=True)
        prob_low = (expo_val / totals).astype(jnp.bfloat16)
        mixed = jnp.einsum("iqk,ikd->iqd", prob_low, value_rows, preferred_element_type=jnp.float32)
        return (mixed, peak_val + jnp.log(totals))

    query_heads = split_heads(qkv[:, :, 0])
    head_out, log_total = lax.map(
        head_forward,
        (query_heads, split_heads(keys_vals[:, :, 0]), split_heads(keys_vals[:, :, 1])),
    )
    attended = join_heads(head_out).astype(jnp.bfloat16)
    branch_attn = lax.psum(
        jnp.einsum("ish,hd->isd", attended, out_full, preferred_element_type=jnp.float32), "tensor"
    )
    middle = tokens + gains[2] * branch_attn
    normed2, inv_std2, pre_norm2 = norm_fwd(middle, gains[1])
    normed2_low = pre_norm2.astype(jnp.bfloat16)
    pre_act = jnp.einsum("isd,df->isf", normed2_low, up_full, preferred_element_type=jnp.float32)
    act_val, act_slope = gelu_parts(pre_act)
    act_low = act_val.astype(jnp.bfloat16)
    branch_mlp = lax.psum(
        jnp.einsum("isf,fd->isd", act_low, down_full, preferred_element_type=jnp.float32), "tensor"
    )
    output = middle + gains[3] * branch_mlp
    qkv_full, out_full, up_full, down_full = (
        lax.all_gather(w_qkv, "fsdp", axis=0, tiled=True),
        lax.all_gather(w_out, "fsdp", axis=1, tiled=True),
        lax.all_gather(w_up, "fsdp", axis=0, tiled=True),
        lax.all_gather(w_down, "fsdp", axis=1, tiled=True),
    )
    grad_mlp = (gains[3] * cotangent).astype(jnp.bfloat16)
    grad_hidden = jnp.einsum("isd,fd->isf", grad_mlp, down_full, preferred_element_type=jnp.float32)
    grad_pre = (grad_hidden * act_slope).astype(jnp.bfloat16)
    grad_n2 = lax.psum(
        jnp.einsum("isf,df->isd", grad_pre, up_full, preferred_element_type=jnp.float32), "tensor"
    )
    middle_part, grad_gain2 = norm_back(grad_n2, gains[1], normed2, inv_std2)
    grad_middle = cotangent + middle_part
    grad_branch = (gains[2] * grad_middle).astype(jnp.bfloat16)
    grad_att = jnp.einsum(
        "isd,hd->ish", grad_branch, out_full, preferred_element_type=jnp.float32
    ).astype(jnp.bfloat16)
    keys_vals, key_live = (
        lax.all_gather(kv_local, "context", axis=1, tiled=True),
        lax.all_gather(key_flag, "context", axis=1, tiled=True),
    )
    grad_heads_all = split_heads(grad_att)
    key_heads = split_heads(keys_vals[:, :, 0])
    value_heads = split_heads(keys_vals[:, :, 1])

    def head_backward(operands):
        queries, key_rows, value_rows, head_total, grad_heads = operands
        scores = (
            jnp.einsum("iqd,ikd->iqk", queries, key_rows, preferred_element_type=jnp.float32)
            * score_scale
        )
        scores = jnp.where(key_live[:, None, :] > 0, scores, -1e30)
        prob_full = jnp.exp(scores - head_total)
        grad_prob = jnp.einsum(
            "iqd,ikd->iqk", grad_heads, value_rows, preferred_element_type=jnp.float32
        )
        row_delta = jnp.sum(prob_full * grad_prob, axis=-1, keepdims=True)
        grad_score = (prob_full * (grad_prob - row_delta)).astype(jnp.bfloat16)
        grad_query = (
            jnp.einsum("iqk,ikd->iqd", grad_score, key_rows, preferred_element_type=jnp.float32)
            * score_scale
        )
        grad_key = (
            jnp.einsum("iqk,iqd->ikd", grad_score, queries, preferred_element_type=jnp.float32)
            * score_scale
        )
        grad_value = jnp.einsum(
            "iqk,iqd->ikd",
            prob_full.astype(jnp.bfloat16),
            grad_heads,
            preferred_element_type=jnp.float32,
        )
        return (grad_query, grad_key, grad_value)

    grad_query, grad_key, grad_value = lax.map(
        head_backward, (query_heads, key_heads, value_heads, log_total, grad_heads_all)
    )
    key_terms = jnp.stack([join_heads(grad_key), join_heads(grad_value)], axis=2)
    key_grads = lax.psum_scatter(key_terms, "context", scatter_dimension=1, tiled=True)
    grad_qkv = jnp.concatenate([join_heads(grad_query)[:, :, None], key_grads], axis=2).astype(
        jnp.bfloat16
    )
    grad_n1 = lax.psum(
        jnp.einsum("isjh,djh->isd", grad_qkv, qkv_full, preferred_element_type=jnp.float32),
        "tensor",
    )
    input_part, grad_gain1 = norm_back(grad_n1, gains[0], normed1, inv_std1)
    grad_tokens = grad_middle + input_part
    grad_gain3 = jnp.sum(grad_middle * branch_attn, axis=(0, 1))
    grad_gain4 = jnp.sum(cotangent * branch_mlp, axis=(0, 1))
    gain_terms = jnp.stack([grad_gain1, grad_gain2, grad_gain3, grad_gain4], axis=0)
    term_qkv = jnp.einsum(
        "tjh,td->jhd",
        grad_qkv.reshape(tok_rows, 3, half_width),
        normed1_low.reshape(tok_rows, D),
        preferred_element_type=jnp.float32,
    )
    term_out = jnp.einsum(
        "th,td->hd",
        attended.reshape(tok_rows, half_width),
        grad_branch.reshape(tok_rows, D),
        preferred_element_type=jnp.float32,
    )[None]
    term_up = jnp.einsum(
        "tjh,td->jhd",
        grad_pre.reshape(tok_rows, up_blocks, half_width),
        normed2_low.reshape(tok_rows, D),
        preferred_element_type=jnp.float32,
    )
    term_down = jnp.einsum(
        "tjh,td->jhd",
        act_low.reshape(tok_rows, up_blocks, half_width),
        grad_mlp.reshape(tok_rows, D),
        preferred_element_type=jnp.float32,
    )
    block_terms = jnp.concatenate([term_qkv, term_out, term_up, term_down], axis=0)
    fsdp_count = lax.axis_size("fsdp")
    context_count = lax.axis_size("context")
    slot_count = NBLK // context_count
    row_count = half_width // fsdp_count
    onehot = (owner[:, None] == jnp.arange(NBLK, dtype=jnp.int32)[None, :]).astype(jnp.int32)
    block_of = jnp.sum(onehot * jnp.arange(NBLK, dtype=jnp.int32)[:, None], axis=0)
    shaped_terms = block_terms.reshape(NBLK, fsdp_count, row_count, D)
    placed = shaped_terms[
        block_of.reshape(context_count, slot_count)[None, :, :],
        jnp.arange(fsdp_count)[:, None, None],
    ]
    placed = placed.reshape(-1, D)
    summed, gain_grad = (
        lax.psum_scatter(placed, ("fsdp", "context"), scatter_dimension=0, tiled=True),
        lax.psum_scatter(gain_terms, ("fsdp", "context"), scatter_dimension=1, tiled=True),
    )
    grad_mine = summed.reshape(slot_count, row_count, D)
    grad_half = lax.all_gather(grad_mine, "fsdp", axis=1, tiled=True)
    grad_full = lax.all_gather(grad_half[:, None], "tensor", axis=1, tiled=True).reshape(
        slot_count, D, D
    )
    row_offset = lax.axis_index("tensor") * half_width + lax.axis_index("fsdp") * row_count
    tokens_all = images * fsdp_count * SEQ
    highest = lax.Precision.HIGHEST
    left_new = 0.5 * stat_left[:, 0] + 0.5 / tokens_all * jnp.einsum(
        "sra,sba->srb", grad_mine, grad_full, precision=highest
    )
    grad_cols = lax.dynamic_slice_in_dim(grad_full, row_offset, row_count, 2)
    right_new = 0.5 * stat_right[:, 0] + 0.5 / tokens_all * jnp.einsum(
        "sar,sab->srb", grad_cols, grad_full, precision=highest
    )
    inner_prod = jnp.einsum("sra,sab->srb", root_left[:, 0], grad_full, precision=highest)
    update = jnp.einsum("srb,sbc->src", inner_prod, root_right, precision=highest)
    square_sum = lax.psum(jnp.sum(update * update, axis=(1, 2)), ("fsdp", "tensor"))
    factor = 1.0 * lax.rsqrt(square_sum / (D * D) + 1e-06)
    weight_new = master[:, 0] - factor[:, None, None] * update
    share_width = gain_grad.shape[1]
    gain_index = lax.axis_index(("fsdp", "context"))
    gain_mine = lax.dynamic_slice_in_dim(gains, gain_index * share_width, share_width, 1)
    state_new = 0.5 * gain_state + 0.5 * gain_grad * gain_grad / tokens_all
    gain_new = gain_mine - 0.1 * gain_grad * lax.rsqrt(tokens_all * state_new)
    return (
        output,
        grad_tokens,
        grad_mine[:, None],
        left_new[:, None],
        right_new[:, None],
        weight_new[:, None],
        gain_grad,
        state_new,
        gain_new,
    )


def solution(mesh):
    return jax.shard_map(
        per_device,
        mesh=mesh,
        in_specs=(
            P("fsdp", "context", None),
            P("fsdp", "context", None),
            P(),
            P("fsdp", None, "tensor"),
            P("tensor", "fsdp"),
            P("fsdp", "tensor"),
            P("tensor", "fsdp"),
            P("fsdp", "context"),
            P(),
            P("context", "tensor", "fsdp", None),
            P("context", "tensor", "fsdp", None),
            P("context", "tensor", "fsdp", None),
            P("context", None, None),
            P("context", "tensor", "fsdp", None),
            P(None, ("fsdp", "context")),
        ),
        out_specs=(
            P("fsdp", "context", None),
            P("fsdp", "context", None),
            P("context", "tensor", "fsdp", None),
            P("context", "tensor", "fsdp", None),
            P("context", "tensor", "fsdp", None),
            P("context", "tensor", "fsdp", None),
            P(None, ("fsdp", "context")),
            P(None, ("fsdp", "context")),
            P(None, ("fsdp", "context")),
        ),
        check_vma=False,
    )
```

profile of v0, /device:TPU:0, one launch (start us, length us, event | category | flops | bytes accessed | tf_op | source)
XLA Modules:
  0.0 1557.2 jit_solution(10948431820645879818)
XLA Ops:
  13.4 62.4 %all-gather.10.cloned.1.call-done = bf16[1024,3,512]{2,0,1:T(8,128)(2,1)} async-done(((bf16[256,3,512]{2,0,1:T(8,128)(2,1)}), bf16[1024,3,512]{2,0,1:T(8,128)(2,1)}) %all-gather.10.cloned.1.call-update) | async-done | bytes 3145744 | tf_op jit(solution)/shard_map/all_gather | solution.py:67
  75.8 6.8 fusion.71
  86.7 8.1 all-gather.1
  97.7 76.8 %all-gather.12.cloned.1.call-done = bf16[3,1408,2,512]{3,1,2,0:T(8,128)(2,1)} async-done(((bf16[3,352,2,512]{3,1,2,0:T(8,128)(2,1)}), bf16[3,1408,2,512]{3,1,2,0:T(8,128)(2,1)}) %all-gather.12.cloned.1.call-update) | async-done | bytes 8650768 | tf_op jit(solution)/shard_map/all_gather | solution.py:83
  174.5 6.2 fusion.107
  180.7 6.5 copy.141
  187.2 4.6 copy.144
  191.8 6.5 copy.142
  198.3 4.6 copy.145
  204.1 55.3 %while.26 = (s32[]{:T(128)}, bf16[8,3,352,64]{2,3,1,0:T(8,128)(2,1)}, f32[8,3,352,1]{2,1,3,0:T(4,128)S(1)}, bf16[3,1408]{1,0:T(4,128)(2,1)S(1)}, bf16[8,3,352,64...) while((s32[]{:T(128)}, ...), condition=%wide.region_5.6_spmd, body=%wide.region_2.5_spmd.sunk | while | flops 398478432 | bytes 19434328 | solution.py:102
  261.8 4.9 fusion.94
  272.3 23.2 %all-reduce.5.cloned.1.call-done = f32[3,352,1024]{2,1,0:T(8,128)} async-done(((f32[3,352,1024]{2,1,0:T(8,128)}), f32[3,352,1024]{2,1,0:T(8,128)}) %all-reduce.5.cloned.1.call-update) | async-done | bytes 4325392 | tf_op jit(solution)/shard_map/psum | solution.py:107
  303.7 75.3 %all-gather.16.cloned.1.call-done = bf16[1024,2048]{1,0:T(8,128)(2,1)} async-done(((bf16[256,2048]{1,0:T(8,128)(2,1)}), bf16[1024,2048]{1,0:T(8,128)(2,1)}) %all-gather.16.cloned.1.call-update) | async-done | bytes 4194320 | tf_op jit(solution)/shard_map/all_gather | solution.py:69
  379.0 10.5 multiply_convert_fusion.1
  389.5 70.2 %all-gather.18.cloned.1.call-done = bf16[2048,1024]{1,0:T(8,128)(2,1)} async-done(((bf16[2048,256]{1,0:T(8,128)(2,1)}), bf16[2048,1024]{1,0:T(8,128)(2,1)}) %all-gather.18.cloned.1.call-update) | async-done | bytes 4194320 | tf_op jit(solution)/shard_map/all_gather | solution.py:70
  459.6 10.6 fusion.53
  472.3 6.3 fusion.63
  478.9 26.6 %all-reduce.7.cloned.1.call-done = f32[3,352,1024]{2,1,0:T(8,128)} async-done(((f32[3,352,1024]{2,1,0:T(8,128)}), f32[3,352,1024]{2,1,0:T(8,128)}) %all-reduce.7.cloned.1.call-update) | async-done | bytes 4325392 | tf_op jit(solution)/shard_map/psum | solution.py:129
  505.5 5.9 multiply_reduce_fusion.3
  511.5 6.4 multiply_reduce_fusion.2
  525.8 101.5 %while.27 = (s32[]{:T(128)}, bf16[8,3,352,64]{2,3,1,0:T(8,128)(2,1)}, f32[8,3,1408,64]{2,3,0,1:T(8,128)}, f32[8,3,1408,64]{2,3,0,1:T(8,128)}, bf16[3,1408]{1,0:T...) while((s32[]{:T(128)}, ...), condition=%wide.region_15.16_spmd, body=%wide.region_13.15_spmd.sunk | while | flops 965305472 | bytes 49321456 | solution.py:175
  627.3 9.1 copy.156
  636.4 9.1 copy.157
  645.5 12.7 pad_maximum_fusion.1
  659.2 10.0 reshape.167
  669.2 10.0 reshape.169
  679.2 10.5 fusion.57
  689.7 8.2 fusion.54
  703.1 5.4 fusion.81
  708.4 109.2 %reduce-scatter.6.cloned.1.call-done = f32[3,352,2,512]{3,1,2,0:T(8,128)} async-done(((f32[3,1408,2,512]{3,1,2,0:T(8,128)}), f32[3,352,2,512]{3,1,2,0:T(8,128)}) %reduce-scatter.6.cloned.1.call-update) | async-done | bytes 4325392 | tf_op jit(solution)/shard_map/reduce_scatter | solution.py:179
  820.4 8.4 fusion.80
  828.9 9.0 pad_maximum_fusion
  837.9 19.2 %gather_fusion = f32[48,128,1024]{2,1,0:T(8,128)} fusion(f32[12,4,128,1024]{3,2,1,0:T(8,128)} %pad_maximum_fusion, s32[48]{0:T(128)S(1)} %reshape.174), kind=kCustom, calls=%fused_computation | custom fusion | bytes 50332032 | tf_op jit(solution)/shard_map/gather | solution.py:224
  857.2 10.3 fusion.61
  867.6 5.3 fusion.74
  873.0 346.0 %reduce-scatter.8.cloned.1.call-done = f32[384,1024]{1,0:T(8,128)} async-done(((f32[6144,1024]{1,0:T(8,128)}), f32[384,1024]{1,0:T(8,128)}) %reduce-scatter.8.cloned.1.call-update) | async-done | bytes 1572880 | tf_op jit(solution)/shard_map/reduce_scatter | solution.py:230
  1219.0 41.5 %all-reduce.9.cloned.1.call-done = (f32[3,352,1024]{2,1,0:T(8,128)}, f32[3,352,1024]{2,1,0:T(8,128)}) async-done(((f32[3,352,1024]{2,1,0:T(8,128)}, f32[3,352,1024]{2,1,0:T(8,128)}), (f32[3,352,1024]{2,1,0:T(8,128)}, f32[3,352,1024]{2,1,0:T(8,128)})) %all-reduce.9.cloned.1.call-update) | async-done | bytes 8650768 | tf_op jit(solution)/shard_map/psum | solution.py:116
  1260.5 5.3 multiply_reduce_fusion.4
  1265.9 7.0 multiply_reduce_fusion.1
  1274.0 105.2 %all-gather.20.cloned.1.call-done = f32[3,512,1024]{2,1,0:T(8,128)} async-done(((f32[3,128,1024]{2,1,0:T(8,128)}), f32[3,512,1024]{2,1,0:T(8,128)}) %all-gather.20.cloned.1.call-update) | async-done | bytes 6291472 | tf_op jit(solution)/shard_map/all_gather | solution.py:234
  1379.4 7.1 multiply_add_fusion
  1386.5 70.3 %reduce-scatter.10.cloned.1.call-done = f32[64,4]{1,0:T(8,128)} async-done(((f32[1024,4]{1,0:T(8,128)}), f32[64,4]{1,0:T(8,128)}) %reduce-scatter.10.cloned.1.call-update) | async-done | bytes 1040
  1459.0 20.7 %all-gather.22.cloned.1.call-done = f32[3,1024,1024]{2,1,0:T(8,128)} async-done(((f32[3,512,1024]{2,1,0:T(8,128)}), f32[3,1024,1024]{2,1,0:T(8,128)}) %all-gather.22.cloned.1.call-update) | async-done | bytes 12582928 | tf_op jit(solution)/shard_map/all_gather | solution.py:235
  1479.7 10.1 fusion.84
  1489.8 10.7 multiply_reduce_fusion.11
  1500.5 17.3 %psum.39 = f32[3]{0:T(128)S(1)} all-reduce(f32[3]{0:T(128)S(1)} %get-tuple-element.281), channel_id=1, replica_groups=mesh['fsdp'=4,'context'=4,'tensor'=2] {'fsdp','tensor'}, use_global_device_ids=true, to_apply=%region_23.24 | all-reduce | flops 3 | bytes 24 | tf_op jit(solution)/shard_map/psum | solution.py:250
  1520.9 17.4 %fusion.88 = f32[3,1,128,1024]{3,2,1,0:T(8,128)} fusion(f32[3,1,128,1024]{3,2,1,0:T(8,128)S(1)} %copy-done.14, f32[3,128,1024]{2,1,0:T(8,128)S(1)} %bitcast.291, f32[3,1024,1024]{2,1,0:T(8,128)} %all-gather.22.cloned.1.call-done), kind=kOutput, calls=%fused_computation.123 | convolution fusion | flops 4833017856 | bytes 17301504 | tf_op jit(solution)/shard_map/sra,sba->srb/dot_general | solution.py:241
  1538.3 12.0 fusion.87
  (255 shorter events, 212.3 us)
Async XLA Ops:
  7.2 1472.5 %copy-start = (f32[3,1,128,1024]{3,2,1,0:T(8,128)S(1)}, f32[3,1,128,1024]{3,2,1,0:T(8,128)}, u32[]{:S(2)}) copy-start(f32[3,1,128,1024]{3,2,1,0:T(8,128)} %param.30) | copy-start | bytes 4718596
  7.2 68.6 %all-gather.10.cloned.1.call-start = ((), (), s32[]{:S(2)}) async-start(), calls=%async_computation.3 | async-start | bytes 3932160 | tf_op jit(solution)/shard_map/all_gather | solution.py:67
  7.9 5.4 copy-start.26
  7.9 166.6 %all-gather.12.cloned.1.call-start = ((), (), s32[]{:S(2)}) async-start(), calls=%async_computation.4 | async-start | bytes 10813440 | tf_op jit(solution)/shard_map/all_gather | solution.py:83
  10.5 72.1 %copy-start.18 = (f32[3,352]{1,0:T(4,128)}, f32[3,352]{1,0:T(4,128)S(1)}, u32[]{:S(2)}) copy-start(f32[3,352]{1,0:T(4,128)S(1)} %broadcast_multiply_fusion.5) | copy-start | bytes 12676
  13.3 69.3 %copy-start.20 = (f32[3,352]{1,0:T(4,128)}, f32[3,352]{1,0:T(4,128)S(1)}, u32[]{:S(2)}) copy-start(f32[3,352]{1,0:T(4,128)S(1)} %add_rsqrt_fusion.1) | copy-start | bytes 12676
  13.4 69.3 %copy-start.22 = (f32[1,1024]{1,0:T(1,128)}, f32[1,1024]{1,0:T(1,128)S(1)}, u32[]{:S(2)}) copy-start(f32[1,1024]{1,0:T(1,128)S(1)} %get-tuple-element.276) | copy-start | bytes 12292
  13.4 254.8 %copy-start.24 = (f32[1,1024]{1,0:T(1,128)}, f32[1,1024]{1,0:T(1,128)S(1)}, u32[]{:S(2)}) copy-start(f32[1,1024]{1,0:T(1,128)S(1)} %get-tuple-element.275) | copy-start | bytes 12292
  84.4 2.3 copy-start.30
  85.9 9.1 slice-start.4
  85.9 175.9 %all-gather.14.cloned.1.call-start = ((), (), s32[]{:S(2)}) async-start(), calls=%async_computation.5 | async-start | bytes 1310720 | tf_op jit(solution)/shard_map/all_gather | solution.py:68
  86.6 208.9 %all-reduce.5.cloned.1.call-start = ((), (), s32[]{:S(2)}) async-start(), calls=%async_computation.6 | async-start | bytes 8650752 | tf_op jit(solution)/shard_map/psum | solution.py:107
  266.8 112.2 %all-gather.16.cloned.1.call-start = ((), (), s32[]{:S(2)}) async-start(), calls=%async_computation.7 | async-start | bytes 5242880 | tf_op jit(solution)/shard_map/all_gather | solution.py:69
  267.4 192.3 %all-gather.18.cloned.1.call-start = ((), (), s32[]{:S(2)}) async-start(), calls=%async_computation.8 | async-start | bytes 5242880 | tf_op jit(solution)/shard_map/all_gather | solution.py:70
  267.9 237.6 %all-reduce.7.cloned.1.call-start = ((), (), s32[]{:S(2)}) async-start(), calls=%async_computation.9 | async-start | bytes 8650752 | tf_op jit(solution)/shard_map/psum | solution.py:129
  459.6 12.6 copy-start.32
  478.6 339.0 %reduce-scatter.6.cloned.1.call-start = ((), (), s32[]{:S(2)}) async-start(), calls=%async_computation.10 | async-start | bytes 21626880 | tf_op jit(solution)/shard_map/reduce_scatter | solution.py:179
  505.5 5.9 copy-start.3
  511.5 8.5 copy-start.17
  658.3 560.7 %reduce-scatter.8.cloned.1.call-start = ((), (), s32[]{:S(2)}) async-start(), calls=%async_computation.11 | async-start | bytes 26738688 | tf_op jit(solution)/shard_map/reduce_scatter | solution.py:230
  679.2 10.5 copy-start.7
  679.2 10.5 copy-start.12
  697.9 5.2 copy-start.4
  708.4 111.9 %copy-start.16 = (bf16[3,352,1,512]{3,1,2,0:T(8,128)(2,1)S(1)}, bf16[3,352,1,512]{3,1,2,0:T(8,128)(2,1)}, u32[]{:S(2)}) copy-start(bf16[3,352,1,512]{3,1,2,0:T(8,128)(2,1)} %copy.158) | copy-start | bytes 3244036
  708.4 111.9 %copy-start.19 = (f32[3,352]{1,0:T(4,128)S(1)}, f32[3,352]{1,0:T(4,128)}, u32[]{:S(2)}) copy-start(f32[3,352]{1,0:T(4,128)} %copy-done.18) | copy-start | bytes 12676
  708.4 111.9 %copy-start.21 = (f32[3,352]{1,0:T(4,128)S(1)}, f32[3,352]{1,0:T(4,128)}, u32[]{:S(2)}) copy-start(f32[3,352]{1,0:T(4,128)} %copy-done.20) | copy-start | bytes 12676
  708.4 111.9 %copy-start.23 = (f32[1,1024]{1,0:T(1,128)S(1)}, f32[1,1024]{1,0:T(1,128)}, u32[]{:S(2)}) copy-start(f32[1,1024]{1,0:T(1,128)} %copy-done.22) | copy-start | bytes 12292
  817.7 11.2 slice-start
  817.7 11.2 slice-start.2
  820.4 8.4 copy-start.10
  820.4 8.5 slice-start.1
  820.4 8.5 slice-start.3
  820.4 8.5 copy-start.13
  857.1 403.4 %all-reduce.9.cloned.1.call-start = ((), (), s32[]{:S(2)}) async-start(), calls=%async_computation.15 | async-start | bytes 17301504 | tf_op jit(solution)/shard_map/psum | solution.py:116
  857.2 10.4 copy-start.11
  857.2 10.4 copy-start.33
  872.9 506.4 %all-gather.20.cloned.1.call-start = ((), (), s32[]{:S(2)}) async-start(), calls=%async_computation.12 | async-start | bytes 7864320 | tf_op jit(solution)/shard_map/all_gather | solution.py:234
  1219.0 237.9 %reduce-scatter.10.cloned.1.call-start = ((), (), s32[]{:S(2)}) async-start(), calls=%async_computation.14 | async-start | bytes 557056
  1260.5 5.3 copy-start.9
  1260.5 5.3 copy-start.25
  1265.8 7.1 copy-start.27
  1265.9 7.1 copy-start.28
  1274.0 205.7 %all-gather.22.cloned.1.call-start = ((), (), s32[]{:S(2)}) async-start(), calls=%async_computation.13 | async-start | bytes 18874368 | tf_op jit(solution)/shard_map/all_gather | solution.py:235
  1379.4 78.3 %copy-start.31 = (f32[4,64]{1,0:T(4,128)S(1)}, f32[4,64]{1,0:T(4,128)}, u32[]{:S(2)}) copy-start(f32[4,64]{1,0:T(4,128)} %param.33) | copy-start | bytes 3076
  1457.7 32.1 %copy-start.29 = (f32[4,64]{1,0:T(4,128)}, f32[4,64]{1,0:T(4,128)S(1)}, u32[]{:S(2)}) copy-start(f32[4,64]{1,0:T(4,128)S(1)} %copy.185) | copy-start | bytes 3076
  1517.8 3.1 copy-start.5
  1517.8 3.1 copy-start.14
  1520.9 17.4 %copy-start.15 = (f32[3,1,128,1024]{3,2,1,0:T(8,128)S(1)}, f32[3,1,128,1024]{3,2,1,0:T(8,128)}, u32[]{:S(2)}) copy-start(f32[3,1,128,1024]{3,2,1,0:T(8,128)} %param.29) | copy-start | bytes 4718596
  (5 other events, 8.5 us)
Sparse Core Ops, SparseCore 0:
  9.6 66.1 all-gather.9
  86.0 88.4 all-gather.11
  176.1 30.1 all-gather.13
  266.9 28.6 all-reduce.4
  297.0 81.9 all-gather.15
  380.5 79.0 all-gather.17
  478.7 26.7 all-reduce.6
  658.4 159.2 reduce-scatter.5
  857.3 361.6 reduce-scatter.7
  1222.1 38.3 all-reduce.8
  1262.7 116.5 all-gather.19
  1382.1 74.7 reduce-scatter.9
  1458.4 21.2 all-gather.21
where the time goes:
time: 1570 us; the launch traced here: 1560 us
  waiting for transfers between devices  1030 us (66%)
  matrix products  280 us (18%)
  local copies, waits for them, and re-layouts  112 us (7%)
  other arithmetic  92.7 us (6%)
  blocking collectives  25.4 us (2%)
    reduce_scatter x1, waiting for transfers between devices, per_device(): lax.psum_scatter(placed, ('fsdp', 'context'), scatter_dimension=0, tiled=...  346 us
    reduce_scatter x1, waiting for transfers between devices, per_device(): lax.psum_scatter(key_terms, 'context', scatter_dimension=1, tiled=True)  109 us
    all_gather x1, waiting for transfers between devices, per_device(): grad_half = lax.all_gather(grad_mine, 'fsdp', axis=1, tiled=True)  105 us
    all_gather x1, waiting for transfers between devices, per_device(): lax.all_gather(kv_local, 'context', axis=1, tiled=True)  76.8 us
    all_gather x1, waiting for transfers between devices, per_device(): lax.all_gather(w_up, 'fsdp', axis=0, tiled=True)  75.3 us
    unnamed x14, waiting for transfers between devices  72.9 us
    all_gather x1, waiting for transfers between devices, per_device(): lax.all_gather(w_down, 'fsdp', axis=1, tiled=True)  70.2 us
    all_gather x1, waiting for transfers between devices, per_device(): lax.all_gather(w_qkv, 'fsdp', axis=0, tiled=True)  62.4 us
  transfers between devices with their start and end apart: 13, of which 12 were waited for; matrix products, arithmetic and copies ran while one was open for 13% of the time, Pallas kernels for 0%

commit v1 on v0

v1 whole, which is shorter than its diff:
```python
import functools

import jax
import jax.numpy as jnp
from jax import lax
from jax.experimental import pallas as pl
from jax.experimental.pallas import tpu as pltpu
from jax.sharding import PartitionSpec as P

D = 1024
HD = 64
SEQ = 1408
NBLK = 12
LATE = 3
EARLY = NBLK - LATE
BF = jnp.bfloat16
F32 = jnp.float32
SCALE = HD ** (-0.5)


def norm_fwd(field_in, gain_vec):
    centred = field_in - jnp.mean(field_in, axis=-1, keepdims=True)
    inv_std = lax.rsqrt(jnp.mean(centred * centred, axis=-1, keepdims=True) + 1e-06)
    normed = centred * inv_std
    return (normed, inv_std, normed * gain_vec)


def norm_back(grad_out, gain_vec, normed, inv_std):
    scaled = grad_out * gain_vec
    inner_sum = (
        scaled
        - jnp.mean(scaled, axis=-1, keepdims=True)
        - normed * jnp.mean(scaled * normed, axis=-1, keepdims=True)
    )
    return (inner_sum * inv_std, jnp.sum(grad_out * normed, axis=(0, 1)))


def gelu_parts(field_in):
    normal_cdf = 0.5 * (1.0 + lax.erf(field_in * 0.7071067811865476))
    normal_pdf = jnp.exp(-0.5 * field_in * field_in) * 0.3989422804014327
    return (field_in * normal_cdf, normal_cdf + field_in * normal_pdf)


def dot_nt(a, b):
    return lax.dot_general(a, b, (((1,), (1,)), ((), ())), preferred_element_type=F32)


def dot_tn(a, b):
    return lax.dot_general(a, b, (((0,), (0,)), ((), ())), preferred_element_type=F32)


def dot_nn(a, b):
    return lax.dot_general(a, b, (((1,), (0,)), ((), ())), preferred_element_type=F32)


def attn_fwd_kernel(q_ref, k_ref, v_ref, bias_ref, o_ref, lse_ref):
    q = q_ref[...] * SCALE
    k = k_ref[...]
    v = v_ref[...]
    bias = bias_ref[...]
    first = lax.broadcasted_iota(jnp.int32, q.shape, 1) < HD
    outs, sums = [], []
    for head in range(2):
        mask = first if head == 0 else jnp.logical_not(first)
        scores = dot_nt(jnp.where(mask, q, jnp.zeros_like(q)), k) + bias
        peak = jnp.max(scores, axis=-1, keepdims=True)
        expo = jnp.exp(scores - peak)
        total = jnp.sum(expo, axis=-1, keepdims=True)
        outs.append(dot_nn(expo.astype(BF), v) / total)
        sums.append(peak + jnp.log(total))
    o_ref[...] = jnp.where(first, outs[0], outs[1]).astype(BF)
    lse_ref[...] = jnp.where(first, sums[0], sums[1])


def attn_fwd(qkv, bias_row):
    rows = qkv.shape[0]
    bq = rows // 4
    return pl.pallas_call(
        attn_fwd_kernel,
        grid=(rows // bq,),
        out_shape=(
            jax.ShapeDtypeStruct((rows, 128), BF),
            jax.ShapeDtypeStruct((rows, 128), F32),
        ),
        in_specs=[
            pl.BlockSpec((bq, 128), lambda i: (i, 0)),
            pl.BlockSpec((rows, 128), lambda i: (0, 1)),
            pl.BlockSpec((rows, 128), lambda i: (0, 2)),
            pl.BlockSpec((1, rows), lambda i: (0, 0)),
        ],
        out_specs=(
            pl.BlockSpec((bq, 128), lambda i: (i, 0)),
            pl.BlockSpec((bq, 128), lambda i: (i, 0)),
        ),
        compiler_params=pltpu.CompilerParams(vmem_limit_bytes=40 << 20),
        cost_estimate=pl.CostEstimate(
            flops=4 * rows * rows * 512, bytes_accessed=rows * 2048, transcendentals=2 * rows * rows
        ),
        name="attn_fwd",
    )(qkv, qkv, qkv, bias_row)


def attn_bwd_kernel(q_ref, k_ref, v_ref, do_ref, o_ref, lse_ref, live_ref, out_ref, dq_ref, row_ref):
    step = pl.program_id(0)
    chunk = k_ref.shape[0]

    @pl.when(step == 0)
    def _():
        row_ref[0:128, :] = lse_ref[...].T
        prod = do_ref[...].astype(F32) * o_ref[...].astype(F32)
        prod_t = prod.T
        row_ref[128:136, :] = jnp.broadcast_to(
            jnp.sum(prod_t[0:HD], axis=0, keepdims=True), (8, prod_t.shape[1])
        )
        row_ref[136:144, :] = jnp.broadcast_to(
            jnp.sum(prod_t[HD:128], axis=0, keepdims=True), (8, prod_t.shape[1])
        )
        dq_ref[...] = jnp.zeros_like(dq_ref)

    q = q_ref[...]
    k = k_ref[...] * SCALE
    v = v_ref[...]
    do = do_ref[...]
    live = live_ref[:, 0:1] > 0
    first = lax.broadcasted_iota(jnp.int32, k.shape, 1) < HD
    dks, dvs = [], []
    for head in range(2):
        mask = first if head == 0 else jnp.logical_not(first)
        kh = jnp.where(mask, k, jnp.zeros_like(k))
        vh = jnp.where(mask, v, jnp.zeros_like(v))
        lse = row_ref[64 * head : 64 * head + 1, :]
        delta = row_ref[128 + 8 * head : 129 + 8 * head, :]
        prob = jnp.where(live, jnp.exp(dot_nt(kh, q) - lse), 0.0)
        ds = (prob * (dot_nt(vh, do) - delta)).astype(BF)
        dvs.append(dot_nn(prob.astype(BF), do))
        dks.append(dot_nn(ds, q) * SCALE)
        dq_ref[...] += dot_tn(ds, kh)
    at = pl.ds(pl.multiple_of(step * chunk, chunk), chunk)
    out_ref[at, 128:256] = jnp.where(first, dks[0], dks[1]).astype(BF)
    out_ref[at, 256:384] = jnp.where(first, dvs[0], dvs[1]).astype(BF)

    @pl.when(step == pl.num_programs(0) - 1)
    def _():
        out_ref[:, 0:128] = dq_ref[...].astype(BF)


def attn_bwd(qkv, grad, out, lse, live_col):
    rows = qkv.shape[0]
    chunk = rows // 4
    return pl.pallas_call(
        attn_bwd_kernel,
        grid=(rows // chunk,),
        out_shape=jax.ShapeDtypeStruct((rows, 384), BF),
        in_specs=[
            pl.BlockSpec((rows, 128), lambda i: (0, 0)),
            pl.BlockSpec((chunk, 128), lambda i: (i, 1)),
            pl.BlockSpec((chunk, 128), lambda i: (i, 2)),
            pl.BlockSpec((rows, 128), lambda i: (0, 0)),
            pl.BlockSpec((rows, 128), lambda i: (0, 0)),
            pl.BlockSpec((rows, 128), lambda i: (0, 0)),
            pl.BlockSpec((chunk, 128), lambda i: (i, 0)),
        ],
        out_specs=pl.BlockSpec((rows, 384), lambda i: (0, 0)),
        scratch_shapes=[pltpu.VMEM((rows, 128), F32), pltpu.VMEM((144, rows), F32)],
        compiler_params=pltpu.CompilerParams(vmem_limit_bytes=50 << 20),
        cost_estimate=pl.CostEstimate(
            flops=10 * rows * rows * 512, bytes_accessed=rows * 4096, transcendentals=2 * rows * rows
        ),
        name="attn_bwd",
    )(qkv, qkv, qkv, grad, out, lse, live_col)


def xor_permute(value, axis, step):
    size = lax.axis_size(axis)
    return lax.ppermute(value, axis, [(j, j ^ step) for j in range(size)])


def xor_order(pieces, index):
    bit = 1
    while bit < len(pieces):
        odd = (index & bit) > 0
        pieces = [jnp.where(odd, pieces[j ^ bit], pieces[j]) for j in range(len(pieces))]
        bit *= 2
    return pieces


def sum_tensor(value):
    low = lax.optimization_barrier(value.astype(BF))
    return low.astype(F32) + xor_permute(low, "tensor", 1).astype(F32)


def gather_fsdp(value):
    size = lax.axis_size("fsdp")
    if size > 4:
        return lax.all_gather(value, "fsdp", axis=0, tiled=False)
    pieces = [value] + [
        lax.ppermute(value, "fsdp", [(j, (j - k) % size) for j in range(size)])
        for k in range(1, size)
    ]
    doubled = jnp.stack(pieces + pieces[:-1])
    start = lax.rem(size - lax.axis_index("fsdp"), size)
    return lax.dynamic_slice_in_dim(doubled, start, size, 0)


def sum_fsdp(value):
    size = lax.axis_size("fsdp")
    if size > 4:
        return lax.psum(value, "fsdp")
    total = value
    for k in range(1, size):
        total = total + lax.ppermute(value, "fsdp", [(j, (j - k) % size) for j in range(size)])
    return total


def per_device(
    tokens,
    cotangent,
    gains,
    w_qkv,
    w_out,
    w_up,
    w_down,
    key_mask,
    owner,
    stat_left,
    stat_right,
    root_left,
    root_right,
    master,
    gain_state,
):
    images, local_len = tokens.shape[:2]
    tok_rows = images * local_len
    nz, nc, nt = (lax.axis_size(a) for a in ("fsdp", "context", "tensor"))
    me_z, me_c, me_t = (lax.axis_index(a) for a in ("fsdp", "context", "tensor"))
    half_width = w_qkv.shape[2]
    hidden = w_up.shape[1]
    up_blocks = hidden // half_width
    cols = half_width // nc
    half_len = local_len // nt

    wq_part = lax.dynamic_slice_in_dim(w_qkv, me_c * cols, cols, 2)
    wq = gather_fsdp(wq_part).reshape(D, 3 * cols)

    def two_stage(weight, member_axis, fsdp_axis):
        width = weight.shape[member_axis] // nc
        part = lax.dynamic_slice_in_dim(weight, me_c * width, width, member_axis)
        part = lax.all_gather(part, "fsdp", axis=fsdp_axis, tiled=True)
        return lax.all_gather(part, "context", axis=member_axis, tiled=True)

    out_full = two_stage(w_out, 0, 1)
    up_full = two_stage(w_up, 1, 0)
    down_full = two_stage(w_down, 0, 1)

    counts = jnp.sum(key_mask, axis=1)
    real = counts
    for k in range(1, nc):
        real = real + xor_permute(counts, "context", k)
    position = (
        (me_c ^ jnp.arange(nc))[:, None, None] * local_len
        + (me_t ^ jnp.arange(nt))[None, :, None] * half_len
        + jnp.arange(half_len)[None, None, :]
    ).reshape(-1)
    live = position[None, :] < real[:, None]
    bias = jnp.where(live, 0.0, -1e30).astype(F32)
    live_col = jnp.broadcast_to(live[:, :, None].astype(F32), (images, SEQ, 128))

    normed1, inv_std1, pre_norm1 = norm_fwd(tokens, gains[0])
    normed1_low = pre_norm1.astype(BF)

    def to_natural(value):
        parts = value.reshape((nt, half_len) + value.shape[1:])
        return jnp.where(me_t > 0, parts[::-1], parts).reshape(value.shape)

    x_all, qkv, out_heads, log_sums, attended = [], [], [], [], []
    for i in range(images):
        mine = lax.dynamic_slice_in_dim(normed1_low[i], me_t * half_len, half_len, 0)
        held = jnp.stack([mine] + [xor_permute(mine, "context", k) for k in range(1, nc)])
        other = xor_permute(held, "tensor", 1)
        x_i = jnp.stack([held, other], axis=1).reshape(SEQ, D)
        qkv_i = dot_nn(x_i, wq).astype(BF)
        o_i, lse_i = attn_fwd(qkv_i, bias[i][None])
        chunks = o_i.reshape(nc, local_len, 2 * HD)
        moved = [to_natural(chunks[0])] + [
            to_natural(xor_permute(chunks[k], "context", k)) for k in range(1, nc)
        ]
        attended.append(jnp.concatenate(xor_order(moved, me_c), axis=-1))
        x_all.append(x_i)
        qkv.append(qkv_i)
        out_heads.append(o_i)
        log_sums.append(lse_i)
    attended = jnp.stack(attended)

    branch_attn = sum_tensor(
        jnp.einsum("ish,hd->isd", attended, out_full, preferred_element_type=F32)
    )
    middle = tokens + gains[2] * branch_attn
    normed2, inv_std2, pre_norm2 = norm_fwd(middle, gains[1])
    normed2_low = pre_norm2.astype(BF)
    pre_act = jnp.einsum("isd,df->isf", normed2_low, up_full, preferred_element_type=F32)
    act_val, act_slope = gelu_parts(pre_act)
    act_low = act_val.astype(BF)
    branch_mlp = sum_tensor(
        jnp.einsum("isf,fd->isd", act_low, down_full, preferred_element_type=F32)
    )
    output = middle + gains[3] * branch_mlp

    grad_mlp = (gains[3] * cotangent).astype(BF)
    grad_hidden = jnp.einsum("isd,fd->isf", grad_mlp, down_full, preferred_element_type=F32)
    grad_pre = (grad_hidden * act_slope).astype(BF)
    grad_n2 = sum_tensor(
        jnp.einsum("isf,df->isd", grad_pre, up_full, preferred_element_type=F32)
    )
    middle_part, grad_gain2 = norm_back(grad_n2, gains[1], normed2, inv_std2)
    grad_middle = cotangent + middle_part
    grad_branch = (gains[2] * grad_middle).astype(BF)
    grad_att = jnp.einsum(
        "isd,hd->ish", grad_branch, out_full, preferred_element_type=F32
    ).astype(BF)

    term_qkv = None
    grad_tok = []
    for i in range(images):
        pieces = [grad_att[i, :, j * cols : (j + 1) * cols] for j in range(nc)]
        pieces = [to_natural(p) for p in xor_order(pieces, me_c)]
        grad_i = jnp.concatenate(
            [pieces[0]] + [xor_permute(pieces[k], "context", k) for k in range(1, nc)]
        )
        g_i = attn_bwd(qkv[i], grad_i, out_heads[i], log_sums[i], live_col[i])
        chunks = g_i.reshape(nc, local_len, 3 * cols)
        moved = [to_natural(chunks[0])] + [
            to_natural(xor_permute(chunks[k], "context", k)) for k in range(1, nc)
        ]
        grad_tok.append(jnp.stack(xor_order(moved, me_c), axis=1))
        term = dot_tn(g_i, x_all[i])
        term_qkv = term if term_qkv is None else term_qkv + term
    grad_tok = jnp.stack(grad_tok)
    wq_all = lax.all_gather(wq, "context", axis=0, tiled=False)
    grad_n1 = sum_tensor(
        jnp.einsum("isjc,jdc->isd", grad_tok, wq_all, preferred_element_type=F32)
    )
    input_part, grad_gain1 = norm_back(grad_n1, gains[0], normed1, inv_std1)
    grad_tokens = grad_middle + input_part
    grad_gain3 = jnp.sum(grad_middle * branch_attn, axis=(0, 1))
    grad_gain4 = jnp.sum(cotangent * branch_mlp, axis=(0, 1))
    gain_terms = jnp.stack([grad_gain1, grad_gain2, grad_gain3, grad_gain4], axis=0)

    def early_terms(left, right):
        term = dot_tn(left.reshape(tok_rows, -1), right.reshape(tok_rows, D)).astype(BF)
        term = jnp.swapaxes(term.reshape(-1, nc, half_width // nc, D), 0, 1)
        return lax.psum_scatter(
            term.reshape(-1, D), "context", scatter_dimension=0, tiled=True
        ).reshape(-1, half_width // nc, D)

    early = jnp.concatenate(
        [
            early_terms(attended, grad_branch),
            early_terms(grad_pre, normed2_low),
            early_terms(act_low, grad_mlp),
        ],
        axis=0,
    )
    sub = half_width // nc // nz
    early = lax.psum_scatter(
        jnp.swapaxes(early.reshape(EARLY, nz, sub, D), 0, 1).reshape(-1, D),
        "fsdp",
        scatter_dimension=0,
        tiled=True,
    ).reshape(EARLY, sub, D)
    onehot = (owner[:, None] == jnp.arange(NBLK, dtype=jnp.int32)[None, :]).astype(jnp.int32)
    block_of = jnp.sum(onehot * jnp.arange(NBLK, dtype=jnp.int32)[:, None], axis=0)
    slot_count = NBLK // nc
    slots_of = block_of.reshape(nc, slot_count)

    def slots_for(k):
        blocks = lax.dynamic_index_in_dim(slots_of, me_c ^ k, 0, keepdims=False)
        return early[jnp.clip(blocks - LATE, 0, EARLY - 1)]

    placed = [slots_for(0)] + [xor_permute(slots_for(k), "context", k) for k in range(1, nc)]
    placed = jnp.stack(xor_order(placed, me_c), axis=1)
    placed = lax.all_gather(placed, "fsdp", axis=2, tiled=False)
    placed = placed.reshape(slot_count, half_width, D)
    placed_other = xor_permute(placed, "tensor", 1)
    both = jnp.stack([placed, placed_other], axis=1)
    early_full = jnp.where(me_t > 0, both[:, ::-1], both).reshape(slot_count, D, D)

    late = jnp.swapaxes(term_qkv.astype(BF).reshape(LATE, nz, sub, D), 0, 1).reshape(-1, D)
    late = lax.psum_scatter(late, "fsdp", scatter_dimension=0, tiled=True)
    late = lax.all_gather(late, ("context", "fsdp"), axis=0, tiled=True)
    late = jnp.swapaxes(late.reshape(nc * nz, LATE, sub, D), 0, 1).reshape(LATE, half_width, D)
    late_other = xor_permute(late, "tensor", 1)
    both = jnp.stack([late, late_other], axis=1)
    late_full = jnp.where(me_t > 0, both[:, ::-1], both).reshape(LATE, D, D)

    mine = lax.dynamic_index_in_dim(slots_of, me_c, 0, keepdims=False)
    grad_full = jnp.where(
        (mine < LATE)[:, None, None], late_full[jnp.clip(mine, 0, LATE - 1)], early_full
    )

    row_count = half_width // nz
    row_offset = me_t * half_width + me_z * row_count
    tokens_all = images * nz * SEQ
    grad_mine = lax.dynamic_slice_in_dim(grad_full, row_offset, row_count, 1)
    left_new = 0.5 * stat_left[:, 0] + 0.5 / tokens_all * jnp.einsum(
        "sra,sba->srb", grad_mine, grad_full, preferred_element_type=F32
    )
    grad_cols = lax.dynamic_slice_in_dim(grad_full, row_offset, row_count, 2)
    right_new = 0.5 * stat_right[:, 0] + 0.5 / tokens_all * jnp.einsum(
        "sar,sab->srb", grad_cols, grad_full, preferred_element_type=F32
    )
    inner_prod = jnp.einsum(
        "sra,sab->srb", root_left[:, 0].astype(BF), grad_full, preferred_element_type=F32
    ).astype(BF)
    update = jnp.einsum(
        "srb,sbc->src", inner_prod, root_right.astype(BF), preferred_element_type=F32
    )
    square_sum = jnp.sum(update * update, axis=(1, 2))
    square_sum = sum_fsdp(square_sum + xor_permute(square_sum, "tensor", 1))
    factor = lax.rsqrt(square_sum / (D * D) + 1e-06)
    weight_new = master[:, 0] - factor[:, None, None] * update

    gain_sum = gain_terms
    step = 1
    while step < nc:
        gain_sum = gain_sum + xor_permute(gain_sum, "context", step)
        step *= 2
    gain_sum = sum_fsdp(gain_sum)
    share_width = gain_state.shape[1]
    gain_index = lax.axis_index(("fsdp", "context"))
    gain_grad = lax.dynamic_slice_in_dim(gain_sum, gain_index * share_width, share_width, 1)
    gain_mine = lax.dynamic_slice_in_dim(gains, gain_index * share_width, share_width, 1)
    state_new = 0.5 * gain_state + 0.5 * gain_grad * gain_grad / tokens_all
    gain_new = gain_mine - 0.1 * gain_grad * lax.rsqrt(tokens_all * state_new)
    return (
        output,
        grad_tokens,
        grad_mine.astype(F32)[:, None],
        left_new[:, None],
        right_new[:, None],
        weight_new[:, None],
        gain_grad,
        state_new,
        gain_new,
    )


def solution(mesh):
    return jax.shard_map(
        per_device,
        mesh=mesh,
        in_specs=(
            P("fsdp", "context", None),
            P("fsdp", "context", None),
            P(),
            P("fsdp", None, "tensor"),
            P("tensor", "fsdp"),
            P("fsdp", "tensor"),
            P("tensor", "fsdp"),
            P("fsdp", "context"),
            P(),
            P("context", "tensor", "fsdp", None),
            P("context", "tensor", "fsdp", None),
            P("context", "tensor", "fsdp", None),
            P("context", None, None),
            P("context", "tensor", "fsdp", None),
            P(None, ("fsdp", "context")),
        ),
        out_specs=(
            P("fsdp", "context", None),
            P("fsdp", "context", None),
            P("context", "tensor", "fsdp", None),
            P("context", "tensor", "fsdp", None),
            P("context", "tensor", "fsdp", None),
            P("context", "tensor", "fsdp", None),
            P(None, ("fsdp", "context")),
            P(None, ("fsdp", "context")),
            P(None, ("fsdp", "context")),
        ),
        check_vma=False,
    )
```

time: 1570 us -> 785 us (0.50)
  waiting for transfers between devices: 1030 us -> 361 us
  matrix products: 280 us -> 96.3 us
  Pallas kernels: 0 us -> 70.7 us
  starting transfers between devices: 1.31 us -> 71.4 us
  local copies, waits for them, and re-layouts: 112 us -> 54.5 us
    reduce_scatter x2 -> x5, waiting for transfers between devices: 455 us -> 105 us  [the longest x3 47.8 us: early_terms(): lax.psum_scatter(term.reshape(-1, D), 'context', scatter_dimension=0, til...]
    all_gather x7 -> x8, waiting for transfers between devices: 411 us -> 164 us  [the longest x1 63.3 us: per_device(): late = lax.all_gather(late, ('context', 'fsdp'), axis=0, tiled=True)]
    dot_general x72 -> x19, matrix products: 280 us -> 96.3 us  [the longest x6 27.1 us: dot_tn(): lax.dot_general(a, b, (((0,), (0,)), ((), ())), preferred_element_type=F32)]
    psum x3 -> x0, waiting for transfers between devices: 91.3 us -> none  [the longest x1 41.5 us: per_device(): lax.psum(jnp.einsum('isf,fd->isd', act_low, down_full, preferred_element_...]
    ppermute x0 -> x63, waiting for transfers between devices: none -> 91 us  [the longest x54 86.9 us: xor_permute(): return lax.ppermute(value, axis, [(j, j ^ step) for j in range(size)])]
    unnamed x14 -> x13, waiting for transfers between devices: 72.9 us -> 0.21 us
    ppermute x0 -> x63, starting transfers between devices: none -> 70.8 us  [the longest x54 59.6 us: xor_permute(): return lax.ppermute(value, axis, [(j, j ^ step) for j in range(size)])]
    pallas_call x0 -> x6, Pallas kernels: none -> 70.7 us  [the longest x3 42.7 us: attn_bwd(): pl.pallas_call(attn_bwd_kernel, grid=(rows // chunk,), out_shape=jax.Shap...]
  transfers between devices with their start and end apart: 13 -> 76, of which waited for: 12 -> 34; matrix products, arithmetic and copies ran while one was open for 13% -> 23% of each run, Pallas kernels for 0% -> 9%
where the time goes in v1:
time: 785 us; the launch traced here: 778 us
  waiting for transfers between devices  361 us (46%)
  matrix products  96.3 us (12%)
  other arithmetic  90.4 us (12%)
  starting transfers between devices  71.4 us (9%)
  Pallas kernels  70.7 us (9%)
  local copies, waits for them, and re-layouts  54.5 us (7%)
  blocking collectives  17.7 us (2%)
  between operations  15.9 us (2%)
    ppermute x54, waiting for transfers between devices, xor_permute(): return lax.ppermute(value, axis, [(j, j ^ step) for j in range(size)])  86.9 us
    all_gather x1, waiting for transfers between devices, per_device(): late = lax.all_gather(late, ('context', 'fsdp'), axis=0, tiled=True)  63.3 us
    ppermute x54, starting transfers between devices, xor_permute(): return lax.ppermute(value, axis, [(j, j ^ step) for j in range(size)])  59.6 us
    all_gather x1, waiting for transfers between devices, per_device(): placed = lax.all_gather(placed, 'fsdp', axis=2, tiled=False)  54.7 us
    reduce_scatter x3, waiting for transfers between devices, early_terms(): lax.psum_scatter(term.reshape(-1, D), 'context', scatter_dimension=0, til...  47.8 us
    pallas_call x3, Pallas kernels, attn_bwd(): pl.pallas_call(attn_bwd_kernel, grid=(rows // chunk,), out_shape=jax.Shap...  42.7 us
    reduce_scatter x1, waiting for transfers between devices, per_device(): lax.psum_scatter(jnp.swapaxes(early.reshape(EARLY, nz, sub, D), 0, 1).res...  40.7 us
    pallas_call x3, Pallas kernels, attn_fwd(): pl.pallas_call(attn_fwd_kernel, grid=(rows // bq,), out_shape=(jax.ShapeD...  28 us
  transfers between devices with their start and end apart: 76, of which 34 were waited for; matrix products, arithmetic and copies ran while one was open for 23% of the time, Pallas kernels for 9%

profile of v1, /device:TPU:0, one launch (start us, length us, event | category | flops | bytes accessed | tf_op | source)
XLA Modules:
  0.0 777.5 jit_solution(4884369760868344310)
XLA Ops:
  11.8 17.7 %all_gather.30 = bf16[128,1024]{1,0:T(8,128)(2,1)} all-gather(bf16[128,256]{1,0:T(8,128)(2,1)S(1)} %constant_dynamic-slice_fusion.11), channel_id=1, replica_groups=mesh['fsdp'=4,'context'=4,'tensor'=2] {'fsdp'}, dimensions={1}, use_global_device_ids=true | all-gather | bytes 327680 | tf_op jit(solution)/shard_map/all_gather | solution.py:248
  29.6 12.9 %all-gather.12.cloned.1.call-done = bf16[1024,512]{1,0:T(8,128)(2,1)} async-done(((bf16[256,512]{1,0:T(8,128)(2,1)}), bf16[1024,512]{1,0:T(8,128)(2,1)}) %all-gather.12.cloned.1.call-update) | async-done | bytes 1048592 | tf_op jit(solution)/shard_map/all_gather | solution.py:248
  60.9 5.0 collective-permute-done.7
  78.9 7.3 collective-permute-done.2
  97.0 6.7 collective-permute-done.15
  108.9 4.2 collective-permute-done.20
  113.7 8.0 %collective-permute-done.22 = bf16[176,1024]{1,0:T(8,128)(2,1)} collective-permute-done((bf16[176,1024]{1,0:T(8,128)(2,1)}, bf16[176,1024]{1,0:T(8,128)(2,1)}, u32[]{:S(2)}, u32[]{:S(2)}) %collective-permute-start.22) | collective-permute-done | bytes 360480 | tf_op jit(solution)/shard_map/ppermute | solution.py:175
  129.2 9.3 %attn_fwd.3 = (bf16[1408,128]{1,0:T(8,128)(2,1)S(1)}, f32[1408,128]{1,0:T(8,128)S(1)}) custom-call(bf16[1408,384]{1,0:T(8,128)(2,1)S(1)} %convolution_convert_fusion.2.q_ref.k_ref.v_ref, bf16[1408,384]{1,0:T(8,128)(2,1)S(1)} %convolution_convert_fusion.2.q_ref.k_ref.v_ref, bf16[1408,384]{1,0:T(8,128)(2,1)S(1)} %convolution_convert_fusion.2.q_ref.k_ref.v_ref, ...), custom_call_target="tpu_custom_call" | custom-call | flops 4060086272 | bytes 2883584 | tf_op jit(solution)/shard_map/attn_fwd/pallas_call | solution.py:78
  145.8 9.1 %attn_fwd.4 = (bf16[1408,128]{1,0:T(8,128)(2,1)S(1)}, f32[1408,128]{1,0:T(8,128)S(1)}) custom-call(bf16[1408,384]{1,0:T(8,128)(2,1)S(1)} %convolution_convert_fusion.1.q_ref.k_ref.v_ref, bf16[1408,384]{1,0:T(8,128)(2,1)S(1)} %convolution_convert_fusion.1.q_ref.k_ref.v_ref, bf16[1408,384]{1,0:T(8,128)(2,1)S(1)} %convolution_convert_fusion.1.q_ref.k_ref.v_ref, ...), custom_call_target="tpu_custom_call" | custom-call | flops 4060086272 | bytes 2883584 | tf_op jit(solution)/shard_map/attn_fwd/pallas_call | solution.py:78
  161.7 9.6 %attn_fwd.5 = (bf16[1408,128]{1,0:T(8,128)(2,1)S(1)}, f32[1408,128]{1,0:T(8,128)S(1)}) custom-call(bf16[1408,384]{1,0:T(8,128)(2,1)S(1)} %convolution_convert_fusion.q_ref.k_ref.v_ref, bf16[1408,384]{1,0:T(8,128)(2,1)S(1)} %convolution_convert_fusion.q_ref.k_ref.v_ref, bf16[1408,384]{1,0:T(8,128)(2,1)S(1)} %convolution_convert_fusion.q_ref.k_ref.v_ref, ...), custom_call_target="tpu_custom_call" | custom-call | flops 4060086272 | bytes 2883584 | tf_op jit(solution)/shard_map/attn_fwd/pallas_call | solution.py:78
  180.3 4.8 collective-permute-done.24
  191.7 4.2 collective-permute-done.27
  195.9 6.3 fusion.75
  205.1 11.2 %multiply_convert_fusion = (bf16[3,352,2048]{2,1,0:T(8,128)(2,1)}, f32[3,352,2048]{2,1,0:T(8,128)}) fusion(bf16[1024,2048]{1,0:T(8,128)(2,1)} %all-gather.14.cloned.1.call-done, f32[3,352,1024]{2,1,0:T(8,128)} %get-tuple-element.90, f32[1024]{0:T(1024)S(1)} %bitcast.424, f32[3,352]{1,0:T(4,128)S(1)} %add_rsqrt_fusion, f32[3,352]{1,0:T(4,128)S(1)} %broadcast_multiply_fusion.4), kind=kOutput, calls=%fused_computation.15 | convolution fusion | flops 4444323840 | bytes 21508352 | tf_op jit(solution)/shard_map/isd,df->isf/dot_general | solution.py:300
  216.3 25.0 %all-gather.18.cloned.1.call-done = bf16[2048,1024]{1,0:T(8,128)(2,1)} async-done(((bf16[512,1024]{1,0:T(8,128)(2,1)}), bf16[2048,1024]{1,0:T(8,128)(2,1)}) %all-gather.18.cloned.1.call-update) | async-done | bytes 4194320 | tf_op jit(solution)/shard_map/all_gather | solution.py:249
  241.3 10.8 %fusion.5 = bf16[3,352,2048]{2,1,0:T(8,128)(2,1)S(1)} fusion(f32[3,352,2048]{2,1,0:T(8,128)} %get-tuple-element.185, bf16[2048,1024]{1,0:T(8,128)(2,1)} %all-gather.18.cloned.1.call-done, f32[3,352,1024]{2,1,0:T(8,128)} %param.16, f32[1024]{0:T(1024)S(1)} %bitcast.431), kind=kOutput, calls=%fused_computation.14 | convolution fusion | flops 4452974592 | bytes 21499904 | tf_op jit(solution)/shard_map/isd,fd->isf/dot_general | solution.py:309
  252.2 4.9 fusion.30
  257.2 5.1 fusion.33
  262.9 4.4 multiply_reduce_fusion.2
  267.4 7.7 multiply_reduce_fusion
  275.0 4.7 bitcast_convert_fusion.3
  279.9 9.3 %bitcast_convert_fusion.1 = bf16[2048,1024]{1,0:T(8,128)(2,1)S(1)} fusion(bf16[3,352,2048]{2,1,0:T(8,128)(2,1)} %copy-done.51, f32[3,352,1024]{2,1,0:T(8,128)} %get-tuple-element.90, f32[1024]{0:T(1024)S(1)} %bitcast.427, f32[3,352]{1,0:T(4,128)S(1)} %add_rsqrt_fusion, f32[3,352]{1,0:T(4,128)S(1)} %broadcast_multiply_fusion.4), kind=kOutput, calls=%fused_computation.18 | convolution fusion | flops 4435607552 | bytes 12857600 | tf_op jit(solution)/shard_map/dot_general | solution.py:49
  291.8 8.9 %bitcast_convert_fusion = bf16[2048,1024]{1,0:T(8,128)(2,1)S(1)} fusion(bf16[3,352,2048]{2,1,0:T(8,128)(2,1)} %get-tuple-element.184, f32[3,352,1024]{2,1,0:T(8,128)} %param.16, f32[1024]{0:T(1024)S(1)} %bitcast.433), kind=kOutput, calls=%fused_computation.17 | convolution fusion | flops 4433444864 | bytes 12849152 | tf_op jit(solution)/shard_map/dot_general | solution.py:49
  304.4 3.6 convolution_convert_fusion.4
  321.6 3.1 collective-permute-done.42
  327.2 14.7 %attn_bwd.4 = bf16[1408,384]{1,0:T(8,128)(2,1)S(1)} custom-call(bf16[1408,384]{1,0:T(8,128)(2,1)} %copy-done.5, bf16[1408,384]{1,0:T(8,128)(2,1)} %copy-done.5, bf16[1408,384]{1,0:T(8,128)(2,1)} %copy-done.5, bf16[1408,128]{1,0:T(8,128)(2,1)S(1)} %pad_maximum_fusion.14.do_ref, bf16[1408,128]{1,0:T(8,128)(2,1)S(1)} %get-tuple-element.16.o_ref, ...), custom_call_target="tpu_custom_call" | custom-call | flops 10150215680 | bytes 5767168 | tf_op jit(solution)/shard_map/attn_bwd/pallas_call | solution.py:150
  343.6 14.0 %attn_bwd.3 = bf16[1408,384]{1,0:T(8,128)(2,1)S(1)} custom-call(bf16[1408,384]{1,0:T(8,128)(2,1)} %copy-done.4, bf16[1408,384]{1,0:T(8,128)(2,1)} %copy-done.4, bf16[1408,384]{1,0:T(8,128)(2,1)} %copy-done.4, bf16[1408,128]{1,0:T(8,128)(2,1)S(1)} %pad_maximum_fusion.13.do_ref, bf16[1408,128]{1,0:T(8,128)(2,1)S(1)} %get-tuple-element.15.o_ref, ...), custom_call_target="tpu_custom_call" | custom-call | flops 10150215680 | bytes 5767168 | tf_op jit(solution)/shard_map/attn_bwd/pallas_call | solution.py:150
  359.3 14.1 %attn_bwd.5 = bf16[1408,384]{1,0:T(8,128)(2,1)S(1)} custom-call(bf16[1408,384]{1,0:T(8,128)(2,1)} %copy-done.6, bf16[1408,384]{1,0:T(8,128)(2,1)} %copy-done.6, bf16[1408,384]{1,0:T(8,128)(2,1)} %copy-done.6, bf16[1408,128]{1,0:T(8,128)(2,1)S(1)} %pad_maximum_fusion.15.do_ref, bf16[1408,128]{1,0:T(8,128)(2,1)S(1)} %copy-done.3, f32[1408,128]{1,0:T(8,128)S(1)} %copy-done.12, ...), custom_call_target="tpu_custom_call" | custom-call | flops 10150215680 | bytes 5767168 | tf_op jit(solution)/shard_map/attn_bwd/pallas_call | solution.py:150
  375.9 47.8 %reduce-scatter.12.cloned.1.call-done = bf16[512,1024]{1,0:T(8,128)(2,1)} async-done(((bf16[2048,1024]{1,0:T(8,128)(2,1)}), bf16[512,1024]{1,0:T(8,128)(2,1)}) %reduce-scatter.12.cloned.1.call-update) | async-done | bytes 1048592 | tf_op jit(solution)/shard_map/reduce_scatter | solution.py:351
  423.6 3.4 pad_maximum_fusion.5
  429.9 3.2 reshape.1212
  433.2 16.8 %reduce-scatter.6.cloned.1.call-done = bf16[96,1024]{1,0:T(8,128)(2,1)} async-done(((bf16[384,1024]{1,0:T(8,128)(2,1)}), bf16[96,1024]{1,0:T(8,128)(2,1)}) %reduce-scatter.6.cloned.1.call-update) | async-done | bytes 196624 | tf_op jit(solution)/shard_map/reduce_scatter | solution.py:388
  459.4 40.7 %reduce-scatter.14.cloned.1.call-done = bf16[288,1024]{1,0:T(8,128)(2,1)} async-done(((bf16[1152,1024]{1,0:T(8,128)(2,1)}), bf16[288,1024]{1,0:T(8,128)(2,1)}) %reduce-scatter.14.cloned.1.call-update) | async-done | bytes 589840 | tf_op jit(solution)/shard_map/reduce_scatter | solution.py:364
  517.7 7.1 collective-permute-done.50
  535.6 4.7 collective-permute-done.45
  540.3 9.9 %collective-permute-done.47 = bf16[352,384]{1,0:T(8,128)(2,1)S(1)} collective-permute-done((bf16[352,384]{1,0:T(8,128)(2,1)}, bf16[352,384]{1,0:T(8,128)(2,1)S(1)}, u32[]{:S(2)}, u32[]{:S(2)}) %collective-permute-start.47) | collective-permute-done | bytes 270368 | tf_op jit(solution)/shard_map/ppermute | solution.py:175
  551.8 8.2 %all-gather.20.cloned.1.call-done = bf16[4,1024,384]{2,1,0:T(8,128)(2,1)} async-done(((bf16[1,1024,384]{2,1,0:T(8,128)(2,1)}), bf16[4,1024,384]{2,1,0:T(8,128)(2,1)}) %all-gather.20.cloned.1.call-update) | async-done | bytes 3145744 | tf_op jit(solution)/shard_map/all_gather | solution.py:338
  560.0 6.6 bitcast_convert_fusion.2
  566.7 63.3 %all-gather.22.cloned.1.call-done = bf16[1536,1024]{1,0:T(8,128)(2,1)} async-done(((bf16[96,1024]{1,0:T(8,128)(2,1)}), bf16[1536,1024]{1,0:T(8,128)(2,1)}) %all-gather.22.cloned.1.call-update) | async-done | bytes 3145744 | tf_op jit(solution)/shard_map/all_gather | solution.py:389
  632.4 5.5 multiply_reduce_fusion.3
  639.5 54.7 %all-gather.24.cloned.1.call-done = bf16[3,4,128,1024]{3,2,1,0:T(8,128)(2,1)} async-done(((bf16[3,4,32,1024]{3,2,1,0:T(8,128)(2,1)}), bf16[3,4,128,1024]{3,2,1,0:T(8,128)(2,1)}) %all-gather.24.cloned.1.call-update) | async-done | bytes 3145744 | tf_op jit(solution)/shard_map/all_gather | solution.py:381
  701.2 7.3 multiply_add_fusion
  718.3 4.4 gather_fusion.4
  725.2 3.4 pad_maximum_fusion.1
  733.5 5.7 maximum_select_fusion
  739.3 10.1 %multiply_reduce_fusion.8 = (f32[3]{0:T(128)S(1)}, f32[3,128,1024]{2,1,0:T(8,128)S(1)}) fusion(f32[3,1024,1024]{2,1,0:T(8,128)} %param.27, bf16[3,1024,1024]{2,1,0:T(8,128)(2,1)} %maximum_select_fusion, f32[3,1,128,1024]{3,2,1,0:T(8,128)} %param.26), kind=kOutput, calls=%fused_computation.84 | convolution fusion | flops 1615331328 | bytes 22020108 | tf_op jit(solution)/shard_map/srb,sbc->src/dot_general | solution.py:414
  752.0 5.6 fusion.37
  757.7 3.4 fusion.38
  (393 shorter events, 203.3 us)
Async XLA Ops:
  7.2 35.3 %all-gather.12.cloned.1.call-start = ((), (), s32[]{:S(2)}) async-start(), calls=%async_computation.6 | async-start | bytes 1310720 | tf_op jit(solution)/shard_map/all_gather | solution.py:248
  9.2 115.5 %all-gather.16.cloned.1.call-start = ((), (), s32[]{:S(2)}) async-start(), calls=%async_computation.8 | async-start | bytes 1310720 | tf_op jit(solution)/shard_map/all_gather | solution.py:248
  10.9 177.9 %all-gather.10.cloned.1.call-start = ((), (), s32[]{:S(2)}) async-start(), calls=%async_computation.5 | async-start | bytes 1310720 | tf_op jit(solution)/shard_map/all_gather | solution.py:249
  29.6 175.5 %all-gather.14.cloned.1.call-start = ((), (), s32[]{:S(2)}) async-start(), calls=%async_computation.7 | async-start | bytes 5242880 | tf_op jit(solution)/shard_map/all_gather | solution.py:249
  42.6 198.8 %all-gather.18.cloned.1.call-start = ((), (), s32[]{:S(2)}) async-start(), calls=%async_computation.9 | async-start | bytes 5242880 | tf_op jit(solution)/shard_map/all_gather | solution.py:249
  44.3 32.1 %collective-permute-start.4 = (bf16[256,3,128]{2,0,1:T(8,128)(2,1)}, bf16[256,3,128]{2,0,1:T(8,128)(2,1)S(1)}, u32[]{:S(2)}, u32[]{:S(2)}) collective-permute-start(bf16[256,3,128]{2,0,1:T(8,128)(2,1)} %get-tuple-element.92), channel_id=1, source_target_pairs={{0,24},{8,0},{16,8},{24,16},{1,25},{9,1},{17,9},{25,17},{2,26},{10... | collective-permute-start | bytes 589832 | tf_op jit(solution)/shard_map/ppermute | solution.py:197
  46.3 44.7 %collective-permute-start.5 = (bf16[256,3,128]{2,0,1:T(8,128)(2,1)}, bf16[256,3,128]{2,0,1:T(8,128)(2,1)S(1)}, u32[]{:S(2)}, u32[]{:S(2)}) collective-permute-start(bf16[256,3,128]{2,0,1:T(8,128)(2,1)} %get-tuple-element.92), channel_id=1, source_target_pairs={{0,16},{8,24},{16,0},{24,8},{1,17},{9,25},{17,1},{25,9},{2,18},{10... | collective-permute-start | bytes 589832 | tf_op jit(solution)/shard_map/ppermute | solution.py:197
  55.9 21.9 %collective-permute-start = (bf16[176,1024]{1,0:T(8,128)(2,1)S(1)}, bf16[176,1024]{1,0:T(8,128)(2,1)}, u32[]{:S(2)}, u32[]{:S(2)}) collective-permute-start(bf16[176,1024]{1,0:T(8,128)(2,1)S(1)} %fusion.110), channel_id=1, source_target_pairs={{0,2},{2,0},{4,6},{6,4},{1,3},{3,1},{5,7},{7,5},{8,10},{10,8},{12,... | collective-permute-start | bytes 1081352 | tf_op jit(solution)/shard_map/ppermute | solution.py:175
  57.5 20.9 %collective-permute-start.1 = (bf16[176,1024]{1,0:T(8,128)(2,1)S(1)}, bf16[176,1024]{1,0:T(8,128)(2,1)}, u32[]{:S(2)}, u32[]{:S(2)}) collective-permute-start(bf16[176,1024]{1,0:T(8,128)(2,1)S(1)} %fusion.110), channel_id=1, source_target_pairs={{0,4},{2,6},{4,0},{6,2},{1,5},{3,7},{5,1},{7,3},{8,12},{10,14},{12... | collective-permute-start | bytes 1081352 | tf_op jit(solution)/shard_map/ppermute | solution.py:175
  73.9 12.3 %collective-permute-start.2 = (bf16[176,1024]{1,0:T(8,128)(2,1)S(1)}, bf16[176,1024]{1,0:T(8,128)(2,1)S(1)}, u32[]{:S(2)}, u32[]{:S(2)}) collective-permute-start(bf16[176,1024]{1,0:T(8,128)(2,1)S(1)} %fusion.110), channel_id=1, source_target_pairs={{0,6},{2,4},{4,2},{6,0},{1,7},{3,5},{5,3},{7,1},{8,14},{10,12},{12... | collective-permute-start | bytes 1081352 | tf_op jit(solution)/shard_map/ppermute | solution.py:175
  76.5 14.7 %collective-permute-start.6 = (bf16[256,3,128]{2,0,1:T(8,128)(2,1)}, bf16[256,3,128]{2,0,1:T(8,128)(2,1)S(1)}, u32[]{:S(2)}, u32[]{:S(2)}) collective-permute-start(bf16[256,3,128]{2,0,1:T(8,128)(2,1)} %get-tuple-element.92), channel_id=1, source_target_pairs={{0,8},{8,16},{16,24},{24,0},{1,9},{9,17},{17,25},{25,1},{2,10},{10... | collective-permute-start | bytes 589832 | tf_op jit(solution)/shard_map/ppermute | solution.py:197
  77.8 16.0 %collective-permute-start.13 = (bf16[176,1024]{1,0:T(8,128)(2,1)S(1)}, bf16[176,1024]{1,0:T(8,128)(2,1)S(1)}, u32[]{:S(2)}, u32[]{:S(2)}) collective-permute-start(bf16[176,1024]{1,0:T(8,128)(2,1)S(1)} %fusion.111), channel_id=1, source_target_pairs={{0,2},{2,0},{4,6},{6,4},{1,3},{3,1},{5,7},{7,5},{8,10},{10,8},{12,... | collective-permute-start | bytes 1081352 | tf_op jit(solution)/shard_map/ppermute | solution.py:175
  78.4 16.0 %collective-permute-start.14 = (bf16[176,1024]{1,0:T(8,128)(2,1)S(1)}, bf16[176,1024]{1,0:T(8,128)(2,1)S(1)}, u32[]{:S(2)}, u32[]{:S(2)}) collective-permute-start(bf16[176,1024]{1,0:T(8,128)(2,1)S(1)} %fusion.111), channel_id=1, source_target_pairs={{0,4},{2,6},{4,0},{6,2},{1,5},{3,7},{5,1},{7,3},{8,12},{10,14},{12... | collective-permute-start | bytes 1081352 | tf_op jit(solution)/shard_map/ppermute | solution.py:175
  86.2 17.4 %collective-permute-start.15 = (bf16[176,1024]{1,0:T(8,128)(2,1)S(1)}, bf16[176,1024]{1,0:T(8,128)(2,1)S(1)}, u32[]{:S(2)}, u32[]{:S(2)}) collective-permute-start(bf16[176,1024]{1,0:T(8,128)(2,1)S(1)} %fusion.111), channel_id=1, source_target_pairs={{0,6},{2,4},{4,2},{6,0},{1,7},{3,5},{5,3},{7,1},{8,14},{10,12},{12... | collective-permute-start | bytes 1081352 | tf_op jit(solution)/shard_map/ppermute | solution.py:175
  91.1 33.7 %collective-permute-start.3 = (bf16[4,176,1024]{2,1,0:T(8,128)(2,1)}, bf16[4,176,1024]{2,1,0:T(8,128)(2,1)}, u32[]{:S(2)}, u32[]{:S(2)}) collective-permute-start(bf16[4,176,1024]{2,1,0:T(8,128)(2,1)} %get-tuple-element.103), channel_id=1, source_target_pairs={{0,1},{1,0},{2,3},{3,2},{4,5},{5,4},{6,7},{7,6},{8,9},{9,8},{10,11... | collective-permute-start | bytes 4325384 | tf_op jit(solution)/shard_map/ppermute | solution.py:175
  91.1 22.0 %collective-permute-start.20 = (bf16[176,1024]{1,0:T(8,128)(2,1)}, bf16[176,1024]{1,0:T(8,128)(2,1)S(1)}, u32[]{:S(2)}, u32[]{:S(2)}) collective-permute-start(bf16[176,1024]{1,0:T(8,128)(2,1)} %fusion.112), channel_id=1, source_target_pairs={{0,2},{2,0},{4,6},{6,4},{1,3},{3,1},{5,7},{7,5},{8,10},{10,8},{12,... | collective-permute-start | bytes 1081352 | tf_op jit(solution)/shard_map/ppermute | solution.py:175
  93.8 19.9 %collective-permute-start.21 = (bf16[176,1024]{1,0:T(8,128)(2,1)}, bf16[176,1024]{1,0:T(8,128)(2,1)}, u32[]{:S(2)}, u32[]{:S(2)}) collective-permute-start(bf16[176,1024]{1,0:T(8,128)(2,1)} %fusion.112), channel_id=1, source_target_pairs={{0,4},{2,6},{4,0},{6,2},{1,5},{3,7},{5,1},{7,3},{8,12},{10,14},{12... | collective-permute-start | bytes 1081352 | tf_op jit(solution)/shard_map/ppermute | solution.py:175
  94.4 27.4 %collective-permute-start.22 = (bf16[176,1024]{1,0:T(8,128)(2,1)}, bf16[176,1024]{1,0:T(8,128)(2,1)}, u32[]{:S(2)}, u32[]{:S(2)}) collective-permute-start(bf16[176,1024]{1,0:T(8,128)(2,1)} %fusion.112), channel_id=1, source_target_pairs={{0,6},{2,4},{4,2},{6,0},{1,7},{3,5},{5,3},{7,1},{8,14},{10,12},{12... | collective-permute-start | bytes 1081352 | tf_op jit(solution)/shard_map/ppermute | solution.py:175
  105.4 36.7 %collective-permute-start.16 = (bf16[4,176,1024]{2,1,0:T(8,128)(2,1)}, bf16[4,176,1024]{2,1,0:T(8,128)(2,1)}, u32[]{:S(2)}, u32[]{:S(2)}) collective-permute-start(bf16[4,176,1024]{2,1,0:T(8,128)(2,1)} %get-tuple-element.105), channel_id=1, source_target_pairs={{0,1},{1,0},{2,3},{3,2},{4,5},{5,4},{6,7},{7,6},{8,9},{9,8},{10,11... | collective-permute-start | bytes 4325384 | tf_op jit(solution)/shard_map/ppermute | solution.py:175
  124.6 32.8 %collective-permute-start.23 = (bf16[4,176,1024]{2,1,0:T(8,128)(2,1)}, bf16[4,176,1024]{2,1,0:T(8,128)(2,1)}, u32[]{:S(2)}, u32[]{:S(2)}) collective-permute-start(bf16[4,176,1024]{2,1,0:T(8,128)(2,1)} %get-tuple-element.107), channel_id=1, source_target_pairs={{0,1},{1,0},{2,3},{3,2},{4,5},{5,4},{6,7},{7,6},{8,9},{9,8},{10,11... | collective-permute-start | bytes 4325384 | tf_op jit(solution)/shard_map/ppermute | solution.py:175
  124.7 251.1 %reduce-scatter.8.cloned.1.call-start = ((), (), s32[]{:S(2)}) async-start(), calls=%async_computation.13 | async-start | bytes 1310720 | tf_op jit(solution)/shard_map/reduce_scatter | solution.py:351
  138.6 34.3 %collective-permute-start.10 = (bf16[352,128]{1,0:T(8,128)(2,1)S(1)}, bf16[352,128]{1,0:T(8,128)(2,1)S(1)}, u32[]{:S(2)}, u32[]{:S(2)}) collective-permute-start(bf16[352,128]{1,0:T(8,128)(2,1)S(1)} %get-tuple-element.155), channel_id=1, source_target_pairs={{0,6},{2,4},{4,2},{6,0},{1,7},{3,5},{5,3},{7,1},{8,14},{10,12},{12... | collective-permute-start | bytes 270344 | tf_op jit(solution)/shard_map/ppermute | solution.py:175
  141.1 32.4 %collective-permute-start.11 = (bf16[352,128]{1,0:T(8,128)(2,1)S(1)}, bf16[352,128]{1,0:T(8,128)(2,1)S(1)}, u32[]{:S(2)}, u32[]{:S(2)}) collective-permute-start(bf16[352,128]{1,0:T(8,128)(2,1)S(1)} %get-tuple-element.154), channel_id=1, source_target_pairs={{0,4},{2,6},{4,0},{6,2},{1,5},{3,7},{5,1},{7,3},{8,12},{10,14},{12... | collective-permute-start | bytes 270344 | tf_op jit(solution)/shard_map/ppermute | solution.py:175
  141.6 34.3 %collective-permute-start.12 = (bf16[352,128]{1,0:T(8,128)(2,1)S(1)}, bf16[352,128]{1,0:T(8,128)(2,1)S(1)}, u32[]{:S(2)}, u32[]{:S(2)}) collective-permute-start(bf16[352,128]{1,0:T(8,128)(2,1)S(1)} %get-tuple-element.153), channel_id=1, source_target_pairs={{0,2},{2,0},{4,6},{6,4},{1,3},{3,1},{5,7},{7,5},{8,10},{10,8},{12,... | collective-permute-start | bytes 270344 | tf_op jit(solution)/shard_map/ppermute | solution.py:175
  155.0 21.5 %collective-permute-start.17 = (bf16[352,128]{1,0:T(8,128)(2,1)S(1)}, bf16[352,128]{1,0:T(8,128)(2,1)S(1)}, u32[]{:S(2)}, u32[]{:S(2)}) collective-permute-start(bf16[352,128]{1,0:T(8,128)(2,1)S(1)} %get-tuple-element.163), channel_id=1, source_target_pairs={{0,6},{2,4},{4,2},{6,0},{1,7},{3,5},{5,3},{7,1},{8,14},{10,12},{12... | collective-permute-start | bytes 270344 | tf_op jit(solution)/shard_map/ppermute | solution.py:175
  157.5 19.7 %collective-permute-start.18 = (bf16[352,128]{1,0:T(8,128)(2,1)S(1)}, bf16[352,128]{1,0:T(8,128)(2,1)S(1)}, u32[]{:S(2)}, u32[]{:S(2)}) collective-permute-start(bf16[352,128]{1,0:T(8,128)(2,1)S(1)} %get-tuple-element.162), channel_id=1, source_target_pairs={{0,4},{2,6},{4,0},{6,2},{1,5},{3,7},{5,1},{7,3},{8,12},{10,14},{12... | collective-permute-start | bytes 270344 | tf_op jit(solution)/shard_map/ppermute | solution.py:175
  279.8 96.0 %reduce-scatter.10.cloned.1.call-start = ((), (), s32[]{:S(2)}) async-start(), calls=%async_computation.14 | async-start | bytes 5242880 | tf_op jit(solution)/shard_map/reduce_scatter | solution.py:351
  291.6 132.0 %reduce-scatter.12.cloned.1.call-start = ((), (), s32[]{:S(2)}) async-start(), calls=%async_computation.15 | async-start | bytes 5242880 | tf_op jit(solution)/shard_map/reduce_scatter | solution.py:351
  303.2 146.8 %reduce-scatter.6.cloned.1.call-start = ((), (), s32[]{:S(2)}) async-start(), calls=%async_computation.11 | async-start | bytes 983040 | tf_op jit(solution)/shard_map/reduce_scatter | solution.py:388
  375.8 124.3 %reduce-scatter.14.cloned.1.call-start = ((), (), s32[]{:S(2)}) async-start(), calls=%async_computation.16 | async-start | bytes 2949120 | tf_op jit(solution)/shard_map/reduce_scatter | solution.py:364
  427.0 132.9 %all-gather.20.cloned.1.call-start = ((), (), s32[]{:S(2)}) async-start(), calls=%async_computation.10 | async-start | bytes 3932160 | tf_op jit(solution)/shard_map/all_gather | solution.py:338
  433.1 196.8 %all-gather.22.cloned.1.call-start = ((), (), s32[]{:S(2)}) async-start(), calls=%async_computation.12 | async-start | bytes 3342336 | tf_op jit(solution)/shard_map/all_gather | solution.py:389
  450.0 244.2 %all-gather.24.cloned.1.call-start = ((), (), s32[]{:S(2)}) async-start(), calls=%async_computation.17 | async-start | bytes 3932160 | tf_op jit(solution)/shard_map/all_gather | solution.py:381
  451.2 53.8 %collective-permute-start.33 = (bf16[352,384]{1,0:T(8,128)(2,1)}, bf16[352,384]{1,0:T(8,128)(2,1)}, u32[]{:S(2)}, u32[]{:S(2)}) collective-permute-start(bf16[352,384]{1,0:T(8,128)(2,1)} %get-tuple-element.115), channel_id=1, source_target_pairs={{0,6},{2,4},{4,2},{6,0},{1,7},{3,5},{5,3},{7,1},{8,14},{10,12},{12... | collective-permute-start | bytes 811016 | tf_op jit(solution)/shard_map/ppermute | solution.py:175
  453.6 52.9 %collective-permute-start.34 = (bf16[352,384]{1,0:T(8,128)(2,1)}, bf16[352,384]{1,0:T(8,128)(2,1)}, u32[]{:S(2)}, u32[]{:S(2)}) collective-permute-start(bf16[352,384]{1,0:T(8,128)(2,1)} %get-tuple-element.114), channel_id=1, source_target_pairs={{0,4},{2,6},{4,0},{6,2},{1,5},{3,7},{5,1},{7,3},{8,12},{10,14},{12... | collective-permute-start | bytes 811016 | tf_op jit(solution)/shard_map/ppermute | solution.py:175
  454.1 53.9 %collective-permute-start.35 = (bf16[352,384]{1,0:T(8,128)(2,1)}, bf16[352,384]{1,0:T(8,128)(2,1)}, u32[]{:S(2)}, u32[]{:S(2)}) collective-permute-start(bf16[352,384]{1,0:T(8,128)(2,1)} %get-tuple-element.113), channel_id=1, source_target_pairs={{0,2},{2,0},{4,6},{6,4},{1,3},{3,1},{5,7},{7,5},{8,10},{10,8},{12,... | collective-permute-start | bytes 811016 | tf_op jit(solution)/shard_map/ppermute | solution.py:175
  455.6 72.7 %collective-permute-start.39 = (bf16[352,384]{1,0:T(8,128)(2,1)}, bf16[352,384]{1,0:T(8,128)(2,1)S(1)}, u32[]{:S(2)}, u32[]{:S(2)}) collective-permute-start(bf16[352,384]{1,0:T(8,128)(2,1)} %get-tuple-element.127), channel_id=1, source_target_pairs={{0,6},{2,4},{4,2},{6,0},{1,7},{3,5},{5,3},{7,1},{8,14},{10,12},{12... | collective-permute-start | bytes 811016 | tf_op jit(solution)/shard_map/ppermute | solution.py:175
  458.0 73.1 %collective-permute-start.40 = (bf16[352,384]{1,0:T(8,128)(2,1)}, bf16[352,384]{1,0:T(8,128)(2,1)S(1)}, u32[]{:S(2)}, u32[]{:S(2)}) collective-permute-start(bf16[352,384]{1,0:T(8,128)(2,1)} %get-tuple-element.126), channel_id=1, source_target_pairs={{0,4},{2,6},{4,0},{6,2},{1,5},{3,7},{5,1},{7,3},{8,12},{10,14},{12... | collective-permute-start | bytes 811016 | tf_op jit(solution)/shard_map/ppermute | solution.py:175
  508.0 16.8 %collective-permute-start.50 = (bf16[3,32,1024]{2,1,0:T(8,128)(2,1)S(1)}, bf16[3,32,1024]{2,1,0:T(8,128)(2,1)}, u32[]{:S(2)}, u32[]{:S(2)}) collective-permute-start(bf16[3,32,1024]{2,1,0:T(8,128)(2,1)S(1)} %gather_fusion), channel_id=1, source_target_pairs={{0,6},{2,4},{4,2},{6,0},{1,7},{3,5},{5,3},{7,1},{8,14},{10,12},{12... | collective-permute-start | bytes 589832 | tf_op jit(solution)/shard_map/ppermute | solution.py:175
  512.3 20.6 %collective-permute-start.41 = (bf16[352,384]{1,0:T(8,128)(2,1)}, bf16[352,384]{1,0:T(8,128)(2,1)}, u32[]{:S(2)}, u32[]{:S(2)}) collective-permute-start(bf16[352,384]{1,0:T(8,128)(2,1)} %get-tuple-element.125), channel_id=1, source_target_pairs={{0,2},{2,0},{4,6},{6,4},{1,3},{3,1},{5,7},{7,5},{8,10},{10,8},{12,... | collective-permute-start | bytes 811016 | tf_op jit(solution)/shard_map/ppermute | solution.py:175
  516.4 23.9 %collective-permute-start.45 = (bf16[352,384]{1,0:T(8,128)(2,1)}, bf16[352,384]{1,0:T(8,128)(2,1)S(1)}, u32[]{:S(2)}, u32[]{:S(2)}) collective-permute-start(bf16[352,384]{1,0:T(8,128)(2,1)} %get-tuple-element.139), channel_id=1, source_target_pairs={{0,6},{2,4},{4,2},{6,0},{1,7},{3,5},{5,3},{7,1},{8,14},{10,12},{12... | collective-permute-start | bytes 811016 | tf_op jit(solution)/shard_map/ppermute | solution.py:175
  524.8 15.5 %collective-permute-start.46 = (bf16[352,384]{1,0:T(8,128)(2,1)}, bf16[352,384]{1,0:T(8,128)(2,1)}, u32[]{:S(2)}, u32[]{:S(2)}) collective-permute-start(bf16[352,384]{1,0:T(8,128)(2,1)} %get-tuple-element.138), channel_id=1, source_target_pairs={{0,4},{2,6},{4,0},{6,2},{1,5},{3,7},{5,1},{7,3},{8,12},{10,14},{12... | collective-permute-start | bytes 811016 | tf_op jit(solution)/shard_map/ppermute | solution.py:175
  528.3 21.9 %collective-permute-start.47 = (bf16[352,384]{1,0:T(8,128)(2,1)}, bf16[352,384]{1,0:T(8,128)(2,1)S(1)}, u32[]{:S(2)}, u32[]{:S(2)}) collective-permute-start(bf16[352,384]{1,0:T(8,128)(2,1)} %get-tuple-element.137), channel_id=1, source_target_pairs={{0,2},{2,0},{4,6},{6,4},{1,3},{3,1},{5,7},{7,5},{8,10},{10,8},{12,... | collective-permute-start | bytes 811016 | tf_op jit(solution)/shard_map/ppermute | solution.py:175
  566.6 65.8 %collective-permute-start.48 = (bf16[3,352,1024]{2,1,0:T(8,128)(2,1)}, bf16[3,352,1024]{2,1,0:T(8,128)(2,1)}, u32[]{:S(2)}, u32[]{:S(2)}) collective-permute-start(bf16[3,352,1024]{2,1,0:T(8,128)(2,1)} %bitcast_convert_fusion.2), channel_id=1, source_target_pairs={{0,1},{1,0},{2,3},{3,2},{4,5},{5,4},{6,7},{7,6},{8,9},{9,8},{10,11... | collective-permute-start | bytes 6488072 | tf_op jit(solution)/shard_map/ppermute | solution.py:175
  632.2 77.6 %collective-permute-start.49 = (bf16[3,512,1024]{2,1,0:T(8,128)(2,1)S(1)}, bf16[3,512,1024]{2,1,0:T(8,128)(2,1)}, u32[]{:S(2)}, u32[]{:S(2)}) collective-permute-start(bf16[3,512,1024]{2,1,0:T(8,128)(2,1)S(1)} %bitcast.308), channel_id=1, source_target_pairs={{0,1},{1,0},{2,3},{3,2},{4,5},{5,4},{6,7},{7,6},{8,9},{9,8},{10,11... | collective-permute-start | bytes 9437192 | tf_op jit(solution)/shard_map/ppermute | solution.py:175
  638.0 56.2 %collective-permute-start.58 = (f32[4,1024]{1,0:T(4,128)S(1)}, f32[4,1024]{1,0:T(4,128)S(1)}, u32[]{:S(2)}, u32[]{:S(2)}) collective-permute-start(f32[4,1024]{1,0:T(4,128)S(1)} %pad_maximum_fusion.16), channel_id=1, source_target_pairs={{0,2},{2,0},{4,6},{6,4},{1,3},{3,1},{5,7},{7,5},{8,10},{10,8},{12,... | collective-permute-start | bytes 49160 | tf_op jit(solution)/shard_map/ppermute | solution.py:175
  694.2 31.0 %collective-permute-start.53 = (bf16[3,512,1024]{2,1,0:T(8,128)(2,1)}, bf16[3,512,1024]{2,1,0:T(8,128)(2,1)}, u32[]{:S(2)}, u32[]{:S(2)}) collective-permute-start(bf16[3,512,1024]{2,1,0:T(8,128)(2,1)} %bitcast.320), channel_id=1, source_target_pairs={{0,1},{1,0},{2,3},{3,2},{4,5},{5,4},{6,7},{7,6},{8,9},{9,8},{10,11... | collective-permute-start | bytes 9437192 | tf_op jit(solution)/shard_map/ppermute | solution.py:175
  749.4 11.7 %collective-permute-start.54 = (f32[3]{0:T(128)S(1)}, f32[3]{0:T(128)S(1)}, u32[]{:S(2)}, u32[]{:S(2)}) collective-permute-start(f32[3]{0:T(128)S(1)} %get-tuple-element.186), channel_id=1, source_target_pairs={{0,1},{1,0},{2,3},{3,2},{4,5},{5,4},{6,7},{7,6},{8,9},{9,8},{10,11... | collective-permute-start | bytes 44 | tf_op jit(solution)/shard_map/ppermute | solution.py:175
  (84 other events, 611.9 us)
Sparse Core Ops, SparseCore 0:
  10.2 32.3 all-gather.11
  44.1 38.1 all-gather.15
  84.2 37.9 all-gather.9
  123.8 63.4 all-gather.13
  189.0 52.3 all-gather.17
  279.9 27.7 reduce-scatter.7
  311.5 56.3 reduce-scatter.9
  370.9 52.6 reduce-scatter.11
  426.6 23.2 reduce-scatter.5
  452.8 47.2 reduce-scatter.13
  502.7 57.2 all-gather.19
  563.1 66.8 all-gather.21
  632.2 61.9 all-gather.23

commit v2 on v1

--- a/solution.py
+++ b/solution.py
@@ -170,6 +170,223 @@
     )(qkv, qkv, qkv, grad, out, lse, live_col)
 
 
+class Moves:
+    def __init__(self, send_sems, recv_sems):
+        self.send_sems, self.recv_sems, self.count = send_sems, recv_sems, 0
+
+    def make(self, src, dst, device, cond=None, recv_cond=None):
+        index = self.count
+        self.count += 1
+        return Move(self, index, src, dst, device, cond, recv_cond)
+
+
+class Move:
+    def __init__(self, moves, index, src, dst, device, cond, recv_cond):
+        self.args = (src, dst, moves.send_sems.at[index], moves.recv_sems.at[index])
+        self.device, self.cond, self.recv_cond = device, cond, recv_cond
+
+    def copy(self):
+        return pltpu.make_async_remote_copy(
+            *self.args, device_id=self.device, device_id_type=pl.DeviceIdType.MESH
+        )
+
+    def when(self, cond, act):
+        if cond is None:
+            act()
+        else:
+            pl.when(cond)(act)
+
+    def start(self):
+        self.when(self.cond, lambda: self.copy().start())
+
+    def wait_recv(self):
+        self.when(self.recv_cond, lambda: self.copy().wait_recv())
+
+    def wait_send(self):
+        self.when(self.cond, lambda: self.copy().wait_send())
+
+
+def greet(devices):
+    barrier = pltpu.get_barrier_semaphore()
+    for device in devices:
+        pl.semaphore_signal(
+            barrier, inc=1, device_id=device, device_id_type=pl.DeviceIdType.MESH
+        )
+    pl.semaphore_wait(barrier, len(devices))
+
+
+def grad_gather_kernel(
+    nz, nc, slot_blocks, early_ref, late_ref, out_ref, g_ref, l_ref, place_ref, part_ref, send, recv
+):
+    me_z, me_c, me_t = (lax.axis_index(a) for a in ("fsdp", "context", "tensor"))
+    slots = out_ref.shape[0]
+    core = {"tensor": 1 - me_t}
+    x_near, y_near = {"context": me_c ^ 1}, {"context": me_c ^ 2}
+    above, below = {"fsdp": me_z + 1}, {"fsdp": me_z - 1}
+    z_peers = [{"fsdp": lax.rem(me_z + k, nz)} for k in range(1, nz)]
+    c_peers = [{"context": me_c ^ k} for k in range(1, nc)]
+    greet(z_peers + c_peers + [core])
+    moves = Moves(send, recv)
+    sent = []
+
+    def go(*args, **kw):
+        move = moves.make(*args, **kw)
+        move.start()
+        sent.append(move)
+        return move
+
+    late_in = [
+        go(late_ref.at[lax.rem(me_z + k, nz)], part_ref.at[k - 1], z_peers[k - 1])
+        for k in range(1, nz)
+    ]
+    for slot in range(NBLK):
+        block = jnp.clip(slot_blocks[slot] - LATE, 0, EARLY - 1)
+        place_ref[slot] = early_ref[block]
+    placed = []
+    for k in range(1, nc):
+        theirs = place_ref.at[pl.ds((me_c ^ k) * slots, slots)]
+        placed.append(go(theirs, g_ref.at[:, me_t, me_c, me_z], c_peers[k - 1]))
+    for slot in range(slots):
+        g_ref[slot, me_t, me_c, me_z] = place_ref[me_c * slots + slot]
+
+    def along_fsdp(ref, member, ready):
+        ready()
+        own = ref.at[:, me_t, member, me_z]
+        up = go(own, own, above, cond=me_z < nz - 1, recv_cond=me_z > 0)
+        down = go(own, own, below, cond=me_z > 0, recv_cond=me_z < nz - 1)
+        return [up, down]
+
+    def onward(ref, member, last, hop):
+        up_in, down_in = last
+        up_z, down_z = me_z - hop, me_z + hop
+        up_in.wait_recv()
+        up = down = None
+        if hop < nz - 1:
+            piece = ref.at[:, me_t, member, up_z]
+            up = go(
+                piece,
+                piece,
+                above,
+                cond=jnp.logical_and(me_z < nz - 1, up_z >= 0),
+                recv_cond=up_z - 1 >= 0,
+            )
+        down_in.wait_recv()
+        if hop < nz - 1:
+            piece = ref.at[:, me_t, member, down_z]
+            down = go(
+                piece,
+                piece,
+                below,
+                cond=jnp.logical_and(me_z > 0, down_z <= nz - 1),
+                recv_cond=down_z + 1 <= nz - 1,
+            )
+        return [up, down], [(up_z, up_z >= 0), (down_z, down_z <= nz - 1)]
+
+    swapped = []
+
+    def swap(ref, member, z, cond=None, columns=None):
+        piece = ref.at[:, me_t, member, z]
+        if columns is not None:
+            piece = ref.at[:, me_t, member, z, :, columns]
+        swapped.append(go(piece, piece, core, cond=cond, recv_cond=cond))
+
+    lines = {}
+    for k in range(nc):
+        member = me_c ^ k
+        lines[k] = along_fsdp(
+            g_ref, member, (lambda: None) if k == 0 else placed[k - 1].wait_recv
+        )
+        swap(g_ref, member, me_z)
+
+    total = late_ref[me_z].astype(F32)
+    for k in range(1, nz):
+        late_in[k - 1].wait_recv()
+        total = total + part_ref[k - 1].astype(F32)
+    l_ref[:, me_t, me_c, me_z] = total.astype(BF)
+    late_line = along_fsdp(l_ref, me_c, lambda: None)
+    left, right = pl.ds(0, D // 2), pl.ds(D // 2, D // 2)
+    near = []
+
+    def spread(z, cond=None):
+        piece = l_ref.at[:, me_t, me_c, z]
+        near.append(
+            (
+                z,
+                cond,
+                go(piece, piece, x_near, cond=cond, recv_cond=cond),
+                go(piece, piece, y_near, cond=cond, recv_cond=cond),
+            )
+        )
+        swap(l_ref, me_c, z, cond)
+
+    spread(me_z)
+    far = []
+    done = 0
+
+    def spread_on():
+        nonlocal done
+        for z, cond, x_in, y_in in near[done:]:
+            x_in.wait_recv()
+            piece = l_ref.at[:, me_t, me_c ^ 1, z, :, left]
+            far.append((z, cond, left, go(piece, piece, y_near, cond=cond, recv_cond=cond)))
+            swap(l_ref, me_c ^ 1, z, cond)
+            y_in.wait_recv()
+            piece = l_ref.at[:, me_t, me_c ^ 2, z, :, right]
+            far.append((z, cond, right, go(piece, piece, x_near, cond=cond, recv_cond=cond)))
+            swap(l_ref, me_c ^ 2, z, cond)
+        done = len(near)
+
+    for hop in range(1, nz):
+        before = late_line
+        late_line, here = onward(l_ref, me_c, before, hop)
+        for z, cond in here:
+            spread(z, cond)
+        for k in range(nc):
+            member = me_c ^ k
+            lines[k], here = onward(g_ref, member, lines[k], hop)
+            for z, cond in here:
+                swap(g_ref, member, z, cond)
+        spread_on()
+    for z, cond, columns, move in far:
+        move.wait_recv()
+        swap(l_ref, me_c ^ 3, z, cond, columns)
+    for move in swapped:
+        move.wait_recv()
+    for slot in range(slots):
+        block = slot_blocks[me_c * slots + slot]
+        late = l_ref[jnp.clip(block, 0, LATE - 1)]
+        out_ref[slot] = jnp.where(block < LATE, late, g_ref[slot])
+    for move in sent:
+        move.wait_send()
+
+
+def grad_gather(block_of, early, late, nz, nc, nt):
+    sub = early.shape[1]
+    slots = NBLK // nc
+    shape = (slots, nt, nc, nz, sub, D)
+    count = 192
+    vmem = pl.BlockSpec(memory_space=pltpu.VMEM)
+    out = pl.pallas_call(
+        functools.partial(grad_gather_kernel, nz, nc),
+        out_shape=jax.ShapeDtypeStruct(shape, BF),
+        in_specs=[pl.BlockSpec(memory_space=pltpu.SMEM), vmem, vmem],
+        out_specs=vmem,
+        scratch_shapes=[
+            pltpu.VMEM(shape, BF),
+            pltpu.VMEM((LATE, nt, nc, nz, sub, D), BF),
+            pltpu.VMEM((NBLK, sub, D), BF),
+            pltpu.VMEM((nz - 1, LATE, sub, D), BF),
+            pltpu.SemaphoreType.DMA((count,)),
+            pltpu.SemaphoreType.DMA((count,)),
+        ],
+        compiler_params=pltpu.CompilerParams(
+            collective_id=0, has_side_effects=True, vmem_limit_bytes=40 << 20
+        ),
+        name="grad_gather",
+    )(block_of, early, late)
+    return out.reshape(slots, D, D)
+
+
 def xor_permute(value, axis, step):
     size = lax.axis_size(axis)
     return lax.ppermute(value, axis, [(j, j ^ step) for j in range(size)])
@@ -210,6 +427,39 @@
     for k in range(1, size):
         total = total + lax.ppermute(value, "fsdp", [(j, (j - k) % size) for j in range(size)])
     return total
+
+
+def grad_gather_plain(block_of, early, late, nz, nc):
+    me_c, me_t = (lax.axis_index(a) for a in ("context", "tensor"))
+    sub = early.shape[1]
+    half_width = nc * nz * sub
+    slot_count = NBLK // nc
+    slots_of = block_of.reshape(nc, slot_count)
+
+    def slots_for(k):
+        blocks = lax.dynamic_index_in_dim(slots_of, me_c ^ k, 0, keepdims=False)
+        return early[jnp.clip(blocks - LATE, 0, EARLY - 1)]
+
+    placed = [slots_for(0)] + [xor_permute(slots_for(k), "context", k) for k in range(1, nc)]
+    placed = jnp.stack(xor_order(placed, me_c), axis=1)
+    placed = lax.all_gather(placed, "fsdp", axis=2, tiled=False)
+    placed = placed.reshape(slot_count, half_width, D)
+    placed_other = xor_permute(placed, "tensor", 1)
+    both = jnp.stack([placed, placed_other], axis=1)
+    early_full = jnp.where(me_t > 0, both[:, ::-1], both).reshape(slot_count, D, D)
+
+    late = late.reshape(-1, D)
+    late = lax.psum_scatter(late, "fsdp", scatter_dimension=0, tiled=True)
+    late = lax.all_gather(late, ("context", "fsdp"), axis=0, tiled=True)
+    late = jnp.swapaxes(late.reshape(nc * nz, LATE, sub, D), 0, 1).reshape(LATE, half_width, D)
+    late_other = xor_permute(late, "tensor", 1)
+    both = jnp.stack([late, late_other], axis=1)
+    late_full = jnp.where(me_t > 0, both[:, ::-1], both).reshape(LATE, D, D)
+
+    mine = lax.dynamic_index_in_dim(slots_of, me_c, 0, keepdims=False)
+    return jnp.where(
+        (mine < LATE)[:, None, None], late_full[jnp.clip(mine, 0, LATE - 1)], early_full
+    )
 
 
 def per_device(
@@ -369,33 +619,12 @@
     ).reshape(EARLY, sub, D)
     onehot = (owner[:, None] == jnp.arange(NBLK, dtype=jnp.int32)[None, :]).astype(jnp.int32)
     block_of = jnp.sum(onehot * jnp.arange(NBLK, dtype=jnp.int32)[:, None], axis=0)
-    slot_count = NBLK // nc
-    slots_of = block_of.reshape(nc, slot_count)
-
-    def slots_for(k):
-        blocks = lax.dynamic_index_in_dim(slots_of, me_c ^ k, 0, keepdims=False)
-        return early[jnp.clip(blocks - LATE, 0, EARLY - 1)]
-
-    placed = [slots_for(0)] + [xor_permute(slots_for(k), "context", k) for k in range(1, nc)]
-    placed = jnp.stack(xor_order(placed, me_c), axis=1)
-    placed = lax.all_gather(placed, "fsdp", axis=2, tiled=False)
-    placed = placed.reshape(slot_count, half_width, D)
-    placed_other = xor_permute(placed, "tensor", 1)
-    both = jnp.stack([placed, placed_other], axis=1)
-    early_full = jnp.where(me_t > 0, both[:, ::-1], both).reshape(slot_count, D, D)
-
-    late = jnp.swapaxes(term_qkv.astype(BF).reshape(LATE, nz, sub, D), 0, 1).reshape(-1, D)
-    late = lax.psum_scatter(late, "fsdp", scatter_dimension=0, tiled=True)
-    late = lax.all_gather(late, ("context", "fsdp"), axis=0, tiled=True)
-    late = jnp.swapaxes(late.reshape(nc * nz, LATE, sub, D), 0, 1).reshape(LATE, half_width, D)
-    late_other = xor_permute(late, "tensor", 1)
-    both = jnp.stack([late, late_other], axis=1)
-    late_full = jnp.where(me_t > 0, both[:, ::-1], both).reshape(LATE, D, D)
-
-    mine = lax.dynamic_index_in_dim(slots_of, me_c, 0, keepdims=False)
-    grad_full = jnp.where(
-        (mine < LATE)[:, None, None], late_full[jnp.clip(mine, 0, LATE - 1)], early_full
-    )
+
+    late = jnp.swapaxes(term_qkv.astype(BF).reshape(LATE, nz, sub, D), 0, 1)
+    if nz == 4 and nc == 4:
+        grad_full = grad_gather(block_of, early, late, nz, nc, nt)
+    else:
+        grad_full = grad_gather_plain(block_of, early, late, nz, nc)
 
     row_count = half_width // nz
     row_offset = me_t * half_width + me_z * row_count

time: 785 us -> 667 us (0.85)
  waiting for transfers between devices: 361 us -> 205 us
  Pallas kernels: 70.7 us -> 164 us
  other arithmetic: 90.4 us -> 59.3 us
  local copies, waits for them, and re-layouts: 54.5 us -> 35.5 us
    all_gather x2 -> x0, waiting for transfers between devices: 118 us -> none  [the longest x1 63.3 us: per_device(): late = lax.all_gather(late, ('context', 'fsdp'), axis=0, tiled=True)]
    pallas_call x0 -> x1, Pallas kernels: none -> 94.5 us  [grad_gather(): pl.pallas_call(functools.partial(grad_gather_kernel, nz, nc), out_shape=j...]
    reduce_scatter x1, waiting for transfers between devices: 40.7 us -> 18.5 us  [per_device(): lax.psum_scatter(jnp.swapaxes(early.reshape(EARLY, nz, sub, D), 0, 1).res...]
    reduce_scatter x3, waiting for transfers between devices: 47.8 us -> 68.5 us  [early_terms(): lax.psum_scatter(term.reshape(-1, D), 'context', scatter_dimension=0, til...]
    reduce_scatter x1 -> x0, waiting for transfers between devices: 16.8 us -> none  [per_device(): late = lax.psum_scatter(late, 'fsdp', scatter_dimension=0, tiled=True)]
    gather x7 -> x0, local copies, waits for them, and re-layouts: 15.9 us -> none  [the longest x3 9.31 us: per_device(): late_full[jnp.clip(mine, 0, LATE - 1)]]
    ppermute x54 -> x49, waiting for transfers between devices: 86.9 us -> 74.7 us  [xor_permute(): return lax.ppermute(value, axis, [(j, j ^ step) for j in range(size)])]
    select_n x4 -> x0, other arithmetic: 9.92 us -> none  [the longest x1 5.7 us: per_device(): jnp.where((mine < LATE)[:, None, None], late_full[jnp.clip(mine, 0, LATE...]
  transfers between devices with their start and end apart: 76 -> 68, of which waited for: 34 -> 29; matrix products, arithmetic and copies ran while one was open for 23% -> 25% of each run, Pallas kernels for 9% -> 11%
where the time goes in v2:
time: 667 us; the launch traced here: 660 us
  waiting for transfers between devices  205 us (31%)
  Pallas kernels  164 us (25%)
  matrix products  98.9 us (15%)
  starting transfers between devices  64.1 us (10%)
  other arithmetic  59.3 us (9%)
  local copies, waits for them, and re-layouts  35.5 us (5%)
  blocking collectives  17.7 us (3%)
  between operations  15.7 us (2%)
    pallas_call x1, Pallas kernels, grad_gather(): pl.pallas_call(functools.partial(grad_gather_kernel, nz, nc), out_shape=j...  94.5 us
    ppermute x49, waiting for transfers between devices, xor_permute(): return lax.ppermute(value, axis, [(j, j ^ step) for j in range(size)])  74.7 us
    reduce_scatter x3, waiting for transfers between devices, early_terms(): lax.psum_scatter(term.reshape(-1, D), 'context', scatter_dimension=0, til...  68.5 us
    ppermute x49, starting transfers between devices, xor_permute(): return lax.ppermute(value, axis, [(j, j ^ step) for j in range(size)])  53.1 us
    pallas_call x3, Pallas kernels, attn_bwd(): pl.pallas_call(attn_bwd_kernel, grid=(rows // chunk,), out_shape=jax.Shap...  42 us
    pallas_call x3, Pallas kernels, attn_fwd(): pl.pallas_call(attn_fwd_kernel, grid=(rows // bq,), out_shape=(jax.ShapeD...  27.5 us
    dot_general x6, matrix products, dot_tn(): lax.dot_general(a, b, (((0,), (0,)), ((), ())), preferred_element_type=F32)  27.1 us
    all_gather x3, waiting for transfers between devices, two_stage(): return lax.all_gather(part, 'context', axis=member_axis, tiled=True)  25.8 us
  transfers between devices with their start and end apart: 68, of which 29 were waited for; matrix products, arithmetic and copies ran while one was open for 25% of the time, Pallas kernels for 11%

profile of v2, /device:TPU:0, one launch (start us, length us, event | category | flops | bytes accessed | tf_op | source)
XLA Modules:
  0.0 659.9 jit_solution(11558673860358909033)
XLA Ops:
  11.8 17.7 %all_gather.21 = bf16[128,1024]{1,0:T(8,128)(2,1)} all-gather(bf16[128,256]{1,0:T(8,128)(2,1)S(1)} %constant_dynamic-slice_fusion.7), channel_id=1, replica_groups=mesh['fsdp'=4,'context'=4,'tensor'=2] {'fsdp'}, dimensions={1}, use_global_device_ids=true | all-gather | bytes 327680 | tf_op jit(solution)/shard_map/all_gather | solution.py:498
  29.6 12.9 %all-gather.9.cloned.1.call-done = bf16[1024,512]{1,0:T(8,128)(2,1)} async-done(((bf16[256,512]{1,0:T(8,128)(2,1)}), bf16[1024,512]{1,0:T(8,128)(2,1)}) %all-gather.9.cloned.1.call-update) | async-done | bytes 1048592 | tf_op jit(solution)/shard_map/all_gather | solution.py:498
  49.8 2.9 multiply_reduce_fusion.7
  52.8 2.8 multiply_convert_fusion.4
  60.2 5.7 collective-permute-done.7
  78.9 7.3 %collective-permute-done.2 = bf16[176,1024]{1,0:T(8,128)(2,1)S(1)} collective-permute-done((bf16[176,1024]{1,0:T(8,128)(2,1)S(1)}, bf16[176,1024]{1,0:T(8,128)(2,1)S(1)}, u32[]{:S(2)}, u32[]{:S(2)}) %collective-permute-start.2) | collective-permute-done | bytes 360480 | tf_op jit(solution)/shard_map/ppermute | solution.py:392
  88.6 2.9 fusion.61
  94.3 2.9 collective-permute-start.22
  97.3 6.2 collective-permute-done.15
  107.1 6.2 collective-permute-done.20
  113.3 8.3 %collective-permute-done.22 = bf16[176,1024]{1,0:T(8,128)(2,1)} collective-permute-done((bf16[176,1024]{1,0:T(8,128)(2,1)S(1)}, bf16[176,1024]{1,0:T(8,128)(2,1)}, u32[]{:S(2)}, u32[]{:S(2)}) %collective-permute-start.22) | collective-permute-done | bytes 360480 | tf_op jit(solution)/shard_map/ppermute | solution.py:392
  121.7 2.9 fusion.59
  129.6 9.3 %attn_fwd.3 = (bf16[1408,128]{1,0:T(8,128)(2,1)S(1)}, f32[1408,128]{1,0:T(8,128)S(1)}) custom-call(bf16[1408,384]{1,0:T(8,128)(2,1)S(1)} %convolution_convert_fusion.2.q_ref.k_ref.v_ref, bf16[1408,384]{1,0:T(8,128)(2,1)S(1)} %convolution_convert_fusion.2.q_ref.k_ref.v_ref, bf16[1408,384]{1,0:T(8,128)(2,1)S(1)} %convolution_convert_fusion.2.q_ref.k_ref.v_ref, ...), custom_call_target="tpu_custom_call" | custom-call | flops 4060086272 | bytes 2883584 | tf_op jit(solution)/shard_map/attn_fwd/pallas_call | solution.py:78
  146.1 9.1 %attn_fwd.4 = (bf16[1408,128]{1,0:T(8,128)(2,1)S(1)}, f32[1408,128]{1,0:T(8,128)S(1)}) custom-call(bf16[1408,384]{1,0:T(8,128)(2,1)S(1)} %convolution_convert_fusion.1.q_ref.k_ref.v_ref, bf16[1408,384]{1,0:T(8,128)(2,1)S(1)} %convolution_convert_fusion.1.q_ref.k_ref.v_ref, bf16[1408,384]{1,0:T(8,128)(2,1)S(1)} %convolution_convert_fusion.1.q_ref.k_ref.v_ref, ...), custom_call_target="tpu_custom_call" | custom-call | flops 4060086272 | bytes 2883584 | tf_op jit(solution)/shard_map/attn_fwd/pallas_call | solution.py:78
  162.1 9.1 %attn_fwd.5 = (bf16[1408,128]{1,0:T(8,128)(2,1)S(1)}, f32[1408,128]{1,0:T(8,128)S(1)}) custom-call(bf16[1408,384]{1,0:T(8,128)(2,1)S(1)} %convolution_convert_fusion.q_ref.k_ref.v_ref, bf16[1408,384]{1,0:T(8,128)(2,1)S(1)} %convolution_convert_fusion.q_ref.k_ref.v_ref, bf16[1408,384]{1,0:T(8,128)(2,1)S(1)} %convolution_convert_fusion.q_ref.k_ref.v_ref, ...), custom_call_target="tpu_custom_call" | custom-call | flops 4060086272 | bytes 2883584 | tf_op jit(solution)/shard_map/attn_fwd/pallas_call | solution.py:78
  176.3 3.1 collective-permute-done.19
  179.4 4.8 collective-permute-done.24
  187.6 4.0 convolution_convert_fusion.3
  193.2 3.3 reshape.1000
  196.5 4.8 fusion.64
  204.0 11.6 %multiply_convert_fusion = (bf16[3,352,2048]{2,1,0:T(8,128)(2,1)}, f32[3,352,2048]{2,1,0:T(8,128)}) fusion(bf16[1024,2048]{1,0:T(8,128)(2,1)} %all-gather.11.cloned.1.call-done, f32[3,352,1024]{2,1,0:T(8,128)} %copy-done.16, f32[1024]{0:T(1024)S(1)} %bitcast.381, f32[3,352]{1,0:T(4,128)S(1)} %add_rsqrt_fusion, f32[3,352]{1,0:T(4,128)S(1)} %broadcast_multiply_fusion.4), kind=kOutput, calls=%fused_computation.7 | convolution fusion | flops 4444323840 | bytes 21508352 | tf_op jit(solution)/shard_map/isd,df->isf/dot_general | solution.py:550
  215.7 25.7 %all-gather.15.cloned.1.call-done = bf16[2048,1024]{1,0:T(8,128)(2,1)} async-done(((bf16[512,1024]{1,0:T(8,128)(2,1)}), bf16[2048,1024]{1,0:T(8,128)(2,1)}) %all-gather.15.cloned.1.call-update) | async-done | bytes 4194320 | tf_op jit(solution)/shard_map/all_gather | solution.py:499
  241.4 10.8 %fusion.5 = bf16[3,352,2048]{2,1,0:T(8,128)(2,1)S(1)} fusion(f32[3,352,2048]{2,1,0:T(8,128)} %get-tuple-element.165, bf16[2048,1024]{1,0:T(8,128)(2,1)} %all-gather.15.cloned.1.call-done, f32[3,352,1024]{2,1,0:T(8,128)} %param.16, f32[1024]{0:T(1024)S(1)} %bitcast.388), kind=kOutput, calls=%fused_computation.6 | convolution fusion | flops 4452974592 | bytes 21499904 | tf_op jit(solution)/shard_map/isd,fd->isf/dot_general | solution.py:559
  254.3 5.0 fusion.30
  259.4 4.9 fusion.33
  268.7 6.9 %multiply_reduce_fusion = (f32[1024]{0:T(1024)S(1)}, f32[3,352,1024]{2,1,0:T(8,128)}, f32[1024]{0:T(1024)S(1)}, f32[3,352,1024]{2,1,0:T(8,128)S(1)}) fusion(f32[3,352,1024]{2,1,0:T(8,128)S(1)} %bitcast.274, bf16[3,352,1024]{2,1,0:T(8,128)(2,1)S(1)} %collective-permute-done.28, bf16[3,352,1024]{2,1,0:T(8,128)(2,1)S(1)} %fusion.33, ...), kind=kLoop, calls=%fused_computation.14 | loop fusion | flops 24868864 | bytes 30310912 | tf_op jit(solution)/shard_map/reduce_sum | solution.py:595
  280.3 9.2 %bitcast_convert_fusion.1 = bf16[2048,1024]{1,0:T(8,128)(2,1)S(1)} fusion(bf16[3,352,2048]{2,1,0:T(8,128)(2,1)} %copy-done.45, f32[3,352,1024]{2,1,0:T(8,128)} %copy-done.16, f32[1024]{0:T(1024)S(1)} %bitcast.384, f32[3,352]{1,0:T(4,128)S(1)} %add_rsqrt_fusion, f32[3,352]{1,0:T(4,128)S(1)} %broadcast_multiply_fusion.4), kind=kOutput, calls=%fused_computation.10 | convolution fusion | flops 4435607552 | bytes 12857600 | tf_op jit(solution)/shard_map/dot_general | solution.py:49
  292.2 8.8 %bitcast_convert_fusion = bf16[2048,1024]{1,0:T(8,128)(2,1)S(1)} fusion(bf16[3,352,2048]{2,1,0:T(8,128)(2,1)} %get-tuple-element.164, f32[3,352,1024]{2,1,0:T(8,128)} %param.16, f32[1024]{0:T(1024)S(1)} %bitcast.390), kind=kOutput, calls=%fused_computation.9 | convolution fusion | flops 4433444864 | bytes 12849152 | tf_op jit(solution)/shard_map/dot_general | solution.py:49
  304.7 3.6 convolution_convert_fusion.4
  320.5 14.0 %attn_bwd.3 = bf16[1408,384]{1,0:T(8,128)(2,1)S(1)} custom-call(bf16[1408,384]{1,0:T(8,128)(2,1)} %copy-done.9, bf16[1408,384]{1,0:T(8,128)(2,1)} %copy-done.9, bf16[1408,384]{1,0:T(8,128)(2,1)} %copy-done.9, bf16[1408,128]{1,0:T(8,128)(2,1)S(1)} %pad_maximum_fusion.9.do_ref, bf16[1408,128]{1,0:T(8,128)(2,1)S(1)} %get-tuple-element.15.o_ref, ...), custom_call_target="tpu_custom_call" | custom-call | flops 10150215680 | bytes 5767168 | tf_op jit(solution)/shard_map/attn_bwd/pallas_call | solution.py:150
  338.6 13.8 %attn_bwd.4 = bf16[1408,384]{1,0:T(8,128)(2,1)S(1)} custom-call(bf16[1408,384]{1,0:T(8,128)(2,1)} %copy-done.8, bf16[1408,384]{1,0:T(8,128)(2,1)} %copy-done.8, bf16[1408,384]{1,0:T(8,128)(2,1)} %copy-done.8, bf16[1408,128]{1,0:T(8,128)(2,1)S(1)} %pad_maximum_fusion.10.do_ref, bf16[1408,128]{1,0:T(8,128)(2,1)S(1)} %get-tuple-element.16.o_ref, ...), custom_call_target="tpu_custom_call" | custom-call | flops 10150215680 | bytes 5767168 | tf_op jit(solution)/shard_map/attn_bwd/pallas_call | solution.py:150
  356.5 14.2 %attn_bwd.5 = bf16[1408,384]{1,0:T(8,128)(2,1)S(1)} custom-call(bf16[1408,384]{1,0:T(8,128)(2,1)} %copy-done.7, bf16[1408,384]{1,0:T(8,128)(2,1)} %copy-done.7, bf16[1408,384]{1,0:T(8,128)(2,1)} %copy-done.7, bf16[1408,128]{1,0:T(8,128)(2,1)S(1)} %pad_maximum_fusion.11.do_ref, bf16[1408,128]{1,0:T(8,128)(2,1)S(1)} %copy-done.6, f32[1408,128]{1,0:T(8,128)S(1)} %copy-done.11, ...), custom_call_target="tpu_custom_call" | custom-call | flops 10150215680 | bytes 5767168 | tf_op jit(solution)/shard_map/attn_bwd/pallas_call | solution.py:150
  374.7 3.8 collective-permute-done.39
  379.3 4.2 collective-permute-done.41
  386.1 4.0 collective-permute-done.45
  390.1 3.7 collective-permute-done.46
  395.4 7.8 %bitcast_convert_fusion.2 = bf16[3,352,1024]{2,1,0:T(8,128)(2,1)} fusion(bf16[4,1024,384]{2,1,0:T(8,128)(2,1)} %all-gather.17.cloned.1.call-done, bf16[1,352,4,384]{3,1,2,0:T(8,128)(2,1)} %maximum_bitcast_fusion.3, bf16[1,352,4,384]{3,1,2,0:T(8,128)(2,1)} %maximum_bitcast_fusion.2, bf16[1,352,4,384]{3,1,2,0:T(8,128)(2,1)} %maximum_bitcast_fusion.1), kind=kOutput, calls=%fused_computation.13 | convolution fusion | flops 3326214144 | bytes 8552448 | tf_op jit(solution)/shard_map/isjc,jdc->isd/dot_general | solution.py:590
  403.2 12.3 %reduce-scatter.7.cloned.1.call-done = bf16[512,1024]{1,0:T(8,128)(2,1)} async-done(((bf16[2048,1024]{1,0:T(8,128)(2,1)}), bf16[512,1024]{1,0:T(8,128)(2,1)}) %reduce-scatter.7.cloned.1.call-update) | async-done | bytes 1048592 | tf_op jit(solution)/shard_map/reduce_scatter | solution.py:601
  415.4 56.3 %reduce-scatter.9.cloned.1.call-done = bf16[512,1024]{1,0:T(8,128)(2,1)} async-done(((bf16[2048,1024]{1,0:T(8,128)(2,1)}), bf16[512,1024]{1,0:T(8,128)(2,1)}) %reduce-scatter.9.cloned.1.call-update) | async-done | bytes 1048592 | tf_op jit(solution)/shard_map/reduce_scatter | solution.py:601
  475.4 3.7 fusion.77
  482.6 4.6 multiply_reduce_fusion.3
  494.8 3.3 collective-permute-start.55
  499.3 5.1 multiply_add_fusion
  505.9 18.5 %reduce-scatter.11.cloned.1.call-done = bf16[288,1024]{1,0:T(8,128)(2,1)} async-done(((bf16[1152,1024]{1,0:T(8,128)(2,1)}), bf16[288,1024]{1,0:T(8,128)(2,1)}) %reduce-scatter.11.cloned.1.call-update) | async-done | bytes 589840 | tf_op jit(solution)/shard_map/reduce_scatter | solution.py:614
  525.5 94.5 %grad_gather.1 = bf16[3,2,4,4,32,1024]{5,4,3,2,1,0:T(8,128)(2,1)S(1)} custom-call(s32[12]{0:T(128)S(1)} %select_reduce_fusion.slot_blocks, bf16[9,32,1024]{2,1,0:T(8,128)(2,1)S(1)} %bitcast.261, bf16[4,3,32,1024]{3,2,1,0:T(8,128)(2,1)S(1)} %bitcast.260), custom_call_target="tpu_custom_call" | custom-call | tf_op jit(solution)/shard_map/grad_gather/pallas_call | solution.py:369
  622.6 10.1 %multiply_reduce_fusion.8 = (f32[3]{0:T(128)S(1)}, f32[3,128,1024]{2,1,0:T(8,128)S(1)}) fusion(f32[3,1024,1024]{2,1,0:T(8,128)} %param.27, bf16[3,1024,1024]{2,1,0:T(8,128)(2,1)} %bitcast.254, f32[3,1,128,1024]{3,2,1,0:T(8,128)} %param.26), kind=kOutput, calls=%fused_computation.73 | convolution fusion | flops 1615331328 | bytes 22020108 | tf_op jit(solution)/shard_map/srb,sbc->src/dot_general | solution.py:643
  636.4 5.6 fusion.37
  642.1 3.4 fusion.38
  (354 shorter events, 148.6 us)
Async XLA Ops:
  7.2 35.3 %all-gather.9.cloned.1.call-start = ((), (), s32[]{:S(2)}) async-start(), calls=%async_computation.5 | async-start | bytes 1310720 | tf_op jit(solution)/shard_map/all_gather | solution.py:498
  9.2 115.4 %all-gather.13.cloned.1.call-start = ((), (), s32[]{:S(2)}) async-start(), calls=%async_computation.7 | async-start | bytes 1310720 | tf_op jit(solution)/shard_map/all_gather | solution.py:498
  10.9 176.6 %all-gather.7.cloned.1.call-start = ((), (), s32[]{:S(2)}) async-start(), calls=%async_computation.4 | async-start | bytes 1310720 | tf_op jit(solution)/shard_map/all_gather | solution.py:499
  29.6 174.5 %all-gather.11.cloned.1.call-start = ((), (), s32[]{:S(2)}) async-start(), calls=%async_computation.6 | async-start | bytes 5242880 | tf_op jit(solution)/shard_map/all_gather | solution.py:499
  42.6 198.8 %all-gather.15.cloned.1.call-start = ((), (), s32[]{:S(2)}) async-start(), calls=%async_computation.8 | async-start | bytes 5242880 | tf_op jit(solution)/shard_map/all_gather | solution.py:499
  44.3 32.2 %collective-permute-start.4 = (bf16[256,3,128]{2,0,1:T(8,128)(2,1)S(1)}, bf16[256,3,128]{2,0,1:T(8,128)(2,1)S(1)}, u32[]{:S(2)}, u32[]{:S(2)}) collective-permute-start(bf16[256,3,128]{2,0,1:T(8,128)(2,1)S(1)} %get-tuple-element.83), channel_id=1, source_target_pairs={{0,24},{8,0},{16,8},{24,16},{1,25},{9,1},{17,9},{25,17},{2,26},{10... | collective-permute-start | bytes 589832 | tf_op jit(solution)/shard_map/ppermute | solution.py:414
  46.3 45.2 %collective-permute-start.5 = (bf16[256,3,128]{2,0,1:T(8,128)(2,1)S(1)}, bf16[256,3,128]{2,0,1:T(8,128)(2,1)S(1)}, u32[]{:S(2)}, u32[]{:S(2)}) collective-permute-start(bf16[256,3,128]{2,0,1:T(8,128)(2,1)S(1)} %get-tuple-element.83), channel_id=1, source_target_pairs={{0,16},{8,24},{16,0},{24,8},{1,17},{9,25},{17,1},{25,9},{2,18},{10... | collective-permute-start | bytes 589832 | tf_op jit(solution)/shard_map/ppermute | solution.py:414
  55.9 21.9 %collective-permute-start = (bf16[176,1024]{1,0:T(8,128)(2,1)S(1)}, bf16[176,1024]{1,0:T(8,128)(2,1)}, u32[]{:S(2)}, u32[]{:S(2)}) collective-permute-start(bf16[176,1024]{1,0:T(8,128)(2,1)S(1)} %fusion.98), channel_id=1, source_target_pairs={{0,2},{2,0},{4,6},{6,4},{1,3},{3,1},{5,7},{7,5},{8,10},{10,8},{12,... | collective-permute-start | bytes 1081352 | tf_op jit(solution)/shard_map/ppermute | solution.py:392
  57.5 20.9 %collective-permute-start.1 = (bf16[176,1024]{1,0:T(8,128)(2,1)S(1)}, bf16[176,1024]{1,0:T(8,128)(2,1)}, u32[]{:S(2)}, u32[]{:S(2)}) collective-permute-start(bf16[176,1024]{1,0:T(8,128)(2,1)S(1)} %fusion.98), channel_id=1, source_target_pairs={{0,4},{2,6},{4,0},{6,2},{1,5},{3,7},{5,1},{7,3},{8,12},{10,14},{12... | collective-permute-start | bytes 1081352 | tf_op jit(solution)/shard_map/ppermute | solution.py:392
  73.9 12.3 %collective-permute-start.2 = (bf16[176,1024]{1,0:T(8,128)(2,1)S(1)}, bf16[176,1024]{1,0:T(8,128)(2,1)S(1)}, u32[]{:S(2)}, u32[]{:S(2)}) collective-permute-start(bf16[176,1024]{1,0:T(8,128)(2,1)S(1)} %fusion.98), channel_id=1, source_target_pairs={{0,6},{2,4},{4,2},{6,0},{1,7},{3,5},{5,3},{7,1},{8,14},{10,12},{12... | collective-permute-start | bytes 1081352 | tf_op jit(solution)/shard_map/ppermute | solution.py:392
  76.5 15.1 %collective-permute-start.6 = (bf16[256,3,128]{2,0,1:T(8,128)(2,1)S(1)}, bf16[256,3,128]{2,0,1:T(8,128)(2,1)S(1)}, u32[]{:S(2)}, u32[]{:S(2)}) collective-permute-start(bf16[256,3,128]{2,0,1:T(8,128)(2,1)S(1)} %get-tuple-element.83), channel_id=1, source_target_pairs={{0,8},{8,16},{16,24},{24,0},{1,9},{9,17},{17,25},{25,1},{2,10},{10... | collective-permute-start | bytes 589832 | tf_op jit(solution)/shard_map/ppermute | solution.py:414
  77.8 16.0 %collective-permute-start.13 = (bf16[176,1024]{1,0:T(8,128)(2,1)S(1)}, bf16[176,1024]{1,0:T(8,128)(2,1)S(1)}, u32[]{:S(2)}, u32[]{:S(2)}) collective-permute-start(bf16[176,1024]{1,0:T(8,128)(2,1)S(1)} %fusion.99), channel_id=1, source_target_pairs={{0,2},{2,0},{4,6},{6,4},{1,3},{3,1},{5,7},{7,5},{8,10},{10,8},{12,... | collective-permute-start | bytes 1081352 | tf_op jit(solution)/shard_map/ppermute | solution.py:392
  78.4 16.0 %collective-permute-start.14 = (bf16[176,1024]{1,0:T(8,128)(2,1)S(1)}, bf16[176,1024]{1,0:T(8,128)(2,1)S(1)}, u32[]{:S(2)}, u32[]{:S(2)}) collective-permute-start(bf16[176,1024]{1,0:T(8,128)(2,1)S(1)} %fusion.99), channel_id=1, source_target_pairs={{0,4},{2,6},{4,0},{6,2},{1,5},{3,7},{5,1},{7,3},{8,12},{10,14},{12... | collective-permute-start | bytes 1081352 | tf_op jit(solution)/shard_map/ppermute | solution.py:392
  86.2 17.3 %collective-permute-start.15 = (bf16[176,1024]{1,0:T(8,128)(2,1)S(1)}, bf16[176,1024]{1,0:T(8,128)(2,1)S(1)}, u32[]{:S(2)}, u32[]{:S(2)}) collective-permute-start(bf16[176,1024]{1,0:T(8,128)(2,1)S(1)} %fusion.99), channel_id=1, source_target_pairs={{0,6},{2,4},{4,2},{6,0},{1,7},{3,5},{5,3},{7,1},{8,14},{10,12},{12... | collective-permute-start | bytes 1081352 | tf_op jit(solution)/shard_map/ppermute | solution.py:392
  91.5 33.1 %collective-permute-start.3 = (bf16[4,176,1024]{2,1,0:T(8,128)(2,1)}, bf16[4,176,1024]{2,1,0:T(8,128)(2,1)}, u32[]{:S(2)}, u32[]{:S(2)}) collective-permute-start(bf16[4,176,1024]{2,1,0:T(8,128)(2,1)} %get-tuple-element.92), channel_id=1, source_target_pairs={{0,1},{1,0},{2,3},{3,2},{4,5},{5,4},{6,7},{7,6},{8,9},{9,8},{10,11... | collective-permute-start | bytes 4325384 | tf_op jit(solution)/shard_map/ppermute | solution.py:392
  91.6 21.8 %collective-permute-start.20 = (bf16[176,1024]{1,0:T(8,128)(2,1)S(1)}, bf16[176,1024]{1,0:T(8,128)(2,1)S(1)}, u32[]{:S(2)}, u32[]{:S(2)}) collective-permute-start(bf16[176,1024]{1,0:T(8,128)(2,1)S(1)} %fusion.100), channel_id=1, source_target_pairs={{0,2},{2,0},{4,6},{6,4},{1,3},{3,1},{5,7},{7,5},{8,10},{10,8},{12,... | collective-permute-start | bytes 1081352 | tf_op jit(solution)/shard_map/ppermute | solution.py:392
  93.8 19.5 %collective-permute-start.21 = (bf16[176,1024]{1,0:T(8,128)(2,1)S(1)}, bf16[176,1024]{1,0:T(8,128)(2,1)}, u32[]{:S(2)}, u32[]{:S(2)}) collective-permute-start(bf16[176,1024]{1,0:T(8,128)(2,1)S(1)} %fusion.100), channel_id=1, source_target_pairs={{0,4},{2,6},{4,0},{6,2},{1,5},{3,7},{5,1},{7,3},{8,12},{10,14},{12... | collective-permute-start | bytes 1081352 | tf_op jit(solution)/shard_map/ppermute | solution.py:392
  94.3 27.3 %collective-permute-start.22 = (bf16[176,1024]{1,0:T(8,128)(2,1)S(1)}, bf16[176,1024]{1,0:T(8,128)(2,1)}, u32[]{:S(2)}, u32[]{:S(2)}) collective-permute-start(bf16[176,1024]{1,0:T(8,128)(2,1)S(1)} %fusion.100), channel_id=1, source_target_pairs={{0,6},{2,4},{4,2},{6,0},{1,7},{3,5},{5,3},{7,1},{8,14},{10,12},{12... | collective-permute-start | bytes 1081352 | tf_op jit(solution)/shard_map/ppermute | solution.py:392
  105.3 37.2 %collective-permute-start.16 = (bf16[4,176,1024]{2,1,0:T(8,128)(2,1)}, bf16[4,176,1024]{2,1,0:T(8,128)(2,1)}, u32[]{:S(2)}, u32[]{:S(2)}) collective-permute-start(bf16[4,176,1024]{2,1,0:T(8,128)(2,1)} %get-tuple-element.94), channel_id=1, source_target_pairs={{0,1},{1,0},{2,3},{3,2},{4,5},{5,4},{6,7},{7,6},{8,9},{9,8},{10,11... | collective-permute-start | bytes 4325384 | tf_op jit(solution)/shard_map/ppermute | solution.py:392
  124.6 33.3 %collective-permute-start.23 = (bf16[4,176,1024]{2,1,0:T(8,128)(2,1)}, bf16[4,176,1024]{2,1,0:T(8,128)(2,1)}, u32[]{:S(2)}, u32[]{:S(2)}) collective-permute-start(bf16[4,176,1024]{2,1,0:T(8,128)(2,1)} %get-tuple-element.96), channel_id=1, source_target_pairs={{0,1},{1,0},{2,3},{3,2},{4,5},{5,4},{6,7},{7,6},{8,9},{9,8},{10,11... | collective-permute-start | bytes 4325384 | tf_op jit(solution)/shard_map/ppermute | solution.py:392
  124.6 270.8 %all-gather.17.cloned.1.call-start = ((), (), s32[]{:S(2)}) async-start(), calls=%async_computation.9 | async-start | bytes 3932160 | tf_op jit(solution)/shard_map/all_gather | solution.py:588
  138.9 33.1 %collective-permute-start.10 = (bf16[352,128]{1,0:T(8,128)(2,1)S(1)}, bf16[352,128]{1,0:T(8,128)(2,1)S(1)}, u32[]{:S(2)}, u32[]{:S(2)}) collective-permute-start(bf16[352,128]{1,0:T(8,128)(2,1)S(1)} %get-tuple-element.140), channel_id=1, source_target_pairs={{0,6},{2,4},{4,2},{6,0},{1,7},{3,5},{5,3},{7,1},{8,14},{10,12},{12... | collective-permute-start | bytes 270344 | tf_op jit(solution)/shard_map/ppermute | solution.py:392
  141.4 31.1 %collective-permute-start.11 = (bf16[352,128]{1,0:T(8,128)(2,1)S(1)}, bf16[352,128]{1,0:T(8,128)(2,1)S(1)}, u32[]{:S(2)}, u32[]{:S(2)}) collective-permute-start(bf16[352,128]{1,0:T(8,128)(2,1)S(1)} %get-tuple-element.139), channel_id=1, source_target_pairs={{0,4},{2,6},{4,0},{6,2},{1,5},{3,7},{5,1},{7,3},{8,12},{10,14},{12... | collective-permute-start | bytes 270344 | tf_op jit(solution)/shard_map/ppermute | solution.py:392
  141.9 33.1 %collective-permute-start.12 = (bf16[352,128]{1,0:T(8,128)(2,1)S(1)}, bf16[352,128]{1,0:T(8,128)(2,1)S(1)}, u32[]{:S(2)}, u32[]{:S(2)}) collective-permute-start(bf16[352,128]{1,0:T(8,128)(2,1)S(1)} %get-tuple-element.138), channel_id=1, source_target_pairs={{0,2},{2,0},{4,6},{6,4},{1,3},{3,1},{5,7},{7,5},{8,10},{10,8},{12,... | collective-permute-start | bytes 270344 | tf_op jit(solution)/shard_map/ppermute | solution.py:392
  155.3 20.3 %collective-permute-start.17 = (bf16[352,128]{1,0:T(8,128)(2,1)S(1)}, bf16[352,128]{1,0:T(8,128)(2,1)S(1)}, u32[]{:S(2)}, u32[]{:S(2)}) collective-permute-start(bf16[352,128]{1,0:T(8,128)(2,1)S(1)} %get-tuple-element.148), channel_id=1, source_target_pairs={{0,6},{2,4},{4,2},{6,0},{1,7},{3,5},{5,3},{7,1},{8,14},{10,12},{12... | collective-permute-start | bytes 270344 | tf_op jit(solution)/shard_map/ppermute | solution.py:392
  157.8 18.5 %collective-permute-start.18 = (bf16[352,128]{1,0:T(8,128)(2,1)S(1)}, bf16[352,128]{1,0:T(8,128)(2,1)S(1)}, u32[]{:S(2)}, u32[]{:S(2)}) collective-permute-start(bf16[352,128]{1,0:T(8,128)(2,1)S(1)} %get-tuple-element.147), channel_id=1, source_target_pairs={{0,4},{2,6},{4,0},{6,2},{1,5},{3,7},{5,1},{7,3},{8,12},{10,14},{12... | collective-permute-start | bytes 270344 | tf_op jit(solution)/shard_map/ppermute | solution.py:392
  172.5 11.7 %collective-permute-start.24 = (bf16[352,128]{1,0:T(8,128)(2,1)S(1)}, bf16[352,128]{1,0:T(8,128)(2,1)S(1)}, u32[]{:S(2)}, u32[]{:S(2)}) collective-permute-start(bf16[352,128]{1,0:T(8,128)(2,1)S(1)} %get-tuple-element.156), channel_id=1, source_target_pairs={{0,6},{2,4},{4,2},{6,0},{1,7},{3,5},{5,3},{7,1},{8,14},{10,12},{12... | collective-permute-start | bytes 270344 | tf_op jit(solution)/shard_map/ppermute | solution.py:392
  196.5 206.7 %reduce-scatter.5.cloned.1.call-start = ((), (), s32[]{:S(2)}) async-start(), calls=%async_computation.10 | async-start | bytes 1310720 | tf_op jit(solution)/shard_map/reduce_scatter | solution.py:601
  280.2 135.2 %reduce-scatter.7.cloned.1.call-start = ((), (), s32[]{:S(2)}) async-start(), calls=%async_computation.11 | async-start | bytes 5242880 | tf_op jit(solution)/shard_map/reduce_scatter | solution.py:601
  292.0 179.7 %reduce-scatter.9.cloned.1.call-start = ((), (), s32[]{:S(2)}) async-start(), calls=%async_computation.12 | async-start | bytes 5242880 | tf_op jit(solution)/shard_map/reduce_scatter | solution.py:601
  303.5 220.9 %reduce-scatter.11.cloned.1.call-start = ((), (), s32[]{:S(2)}) async-start(), calls=%async_computation.13 | async-start | bytes 2949120 | tf_op jit(solution)/shard_map/reduce_scatter | solution.py:614
  312.2 22.4 %collective-permute-start.36 = (bf16[352,128]{1,0:T(8,128)(2,1)S(1)}, bf16[352,128]{1,0:T(8,128)(2,1)S(1)}, u32[]{:S(2)}, u32[]{:S(2)}) collective-permute-start(bf16[352,128]{1,0:T(8,128)(2,1)S(1)} %bitcast.356), channel_id=1, source_target_pairs={{0,2},{2,0},{4,6},{6,4},{1,3},{3,1},{5,7},{7,5},{8,10},{10,8},{12,... | collective-permute-start | bytes 270344 | tf_op jit(solution)/shard_map/ppermute | solution.py:392
  313.8 22.9 %collective-permute-start.37 = (bf16[352,128]{1,0:T(8,128)(2,1)S(1)}, bf16[352,128]{1,0:T(8,128)(2,1)S(1)}, u32[]{:S(2)}, u32[]{:S(2)}) collective-permute-start(bf16[352,128]{1,0:T(8,128)(2,1)S(1)} %bitcast.354), channel_id=1, source_target_pairs={{0,4},{2,6},{4,0},{6,2},{1,5},{3,7},{5,1},{7,3},{8,12},{10,14},{12... | collective-permute-start | bytes 270344 | tf_op jit(solution)/shard_map/ppermute | solution.py:392
  315.0 22.6 %collective-permute-start.38 = (bf16[352,128]{1,0:T(8,128)(2,1)S(1)}, bf16[352,128]{1,0:T(8,128)(2,1)S(1)}, u32[]{:S(2)}, u32[]{:S(2)}) collective-permute-start(bf16[352,128]{1,0:T(8,128)(2,1)S(1)} %bitcast.355), channel_id=1, source_target_pairs={{0,6},{2,4},{4,2},{6,0},{1,7},{3,5},{5,3},{7,1},{8,14},{10,12},{12... | collective-permute-start | bytes 270344 | tf_op jit(solution)/shard_map/ppermute | solution.py:392
  318.7 33.9 %collective-permute-start.42 = (bf16[352,128]{1,0:T(8,128)(2,1)S(1)}, bf16[352,128]{1,0:T(8,128)(2,1)S(1)}, u32[]{:S(2)}, u32[]{:S(2)}) collective-permute-start(bf16[352,128]{1,0:T(8,128)(2,1)S(1)} %bitcast.353), channel_id=1, source_target_pairs={{0,2},{2,0},{4,6},{6,4},{1,3},{3,1},{5,7},{7,5},{8,10},{10,8},{12,... | collective-permute-start | bytes 270344 | tf_op jit(solution)/shard_map/ppermute | solution.py:392
  318.9 35.7 %collective-permute-start.43 = (bf16[352,128]{1,0:T(8,128)(2,1)S(1)}, bf16[352,128]{1,0:T(8,128)(2,1)S(1)}, u32[]{:S(2)}, u32[]{:S(2)}) collective-permute-start(bf16[352,128]{1,0:T(8,128)(2,1)S(1)} %bitcast.352), channel_id=1, source_target_pairs={{0,4},{2,6},{4,0},{6,2},{1,5},{3,7},{5,1},{7,3},{8,12},{10,14},{12... | collective-permute-start | bytes 270344 | tf_op jit(solution)/shard_map/ppermute | solution.py:392
  334.7 20.8 %collective-permute-start.44 = (bf16[352,128]{1,0:T(8,128)(2,1)S(1)}, bf16[352,128]{1,0:T(8,128)(2,1)S(1)}, u32[]{:S(2)}, u32[]{:S(2)}) collective-permute-start(bf16[352,128]{1,0:T(8,128)(2,1)S(1)} %bitcast.351), channel_id=1, source_target_pairs={{0,6},{2,4},{4,2},{6,0},{1,7},{3,5},{5,3},{7,1},{8,14},{10,12},{12... | collective-permute-start | bytes 270344 | tf_op jit(solution)/shard_map/ppermute | solution.py:392
  336.7 34.1 %collective-permute-start.33 = (bf16[352,384]{1,0:T(8,128)(2,1)S(1)}, bf16[352,384]{1,0:T(8,128)(2,1)S(1)}, u32[]{:S(2)}, u32[]{:S(2)}) collective-permute-start(bf16[352,384]{1,0:T(8,128)(2,1)S(1)} %get-tuple-element.104), channel_id=1, source_target_pairs={{0,6},{2,4},{4,2},{6,0},{1,7},{3,5},{5,3},{7,1},{8,14},{10,12},{12... | collective-permute-start | bytes 811016 | tf_op jit(solution)/shard_map/ppermute | solution.py:392
  337.7 35.1 %collective-permute-start.34 = (bf16[352,384]{1,0:T(8,128)(2,1)S(1)}, bf16[352,384]{1,0:T(8,128)(2,1)S(1)}, u32[]{:S(2)}, u32[]{:S(2)}) collective-permute-start(bf16[352,384]{1,0:T(8,128)(2,1)S(1)} %get-tuple-element.103), channel_id=1, source_target_pairs={{0,4},{2,6},{4,0},{6,2},{1,5},{3,7},{5,1},{7,3},{8,12},{10,14},{12... | collective-permute-start | bytes 811016 | tf_op jit(solution)/shard_map/ppermute | solution.py:392
  352.6 21.1 %collective-permute-start.35 = (bf16[352,384]{1,0:T(8,128)(2,1)S(1)}, bf16[352,384]{1,0:T(8,128)(2,1)S(1)}, u32[]{:S(2)}, u32[]{:S(2)}) collective-permute-start(bf16[352,384]{1,0:T(8,128)(2,1)S(1)} %get-tuple-element.102), channel_id=1, source_target_pairs={{0,2},{2,0},{4,6},{6,4},{1,3},{3,1},{5,7},{7,5},{8,10},{10,8},{12,... | collective-permute-start | bytes 811016 | tf_op jit(solution)/shard_map/ppermute | solution.py:392
  354.5 24.0 %collective-permute-start.39 = (bf16[352,384]{1,0:T(8,128)(2,1)S(1)}, bf16[352,384]{1,0:T(8,128)(2,1)S(1)}, u32[]{:S(2)}, u32[]{:S(2)}) collective-permute-start(bf16[352,384]{1,0:T(8,128)(2,1)S(1)} %get-tuple-element.116), channel_id=1, source_target_pairs={{0,6},{2,4},{4,2},{6,0},{1,7},{3,5},{5,3},{7,1},{8,14},{10,12},{12... | collective-permute-start | bytes 811016 | tf_op jit(solution)/shard_map/ppermute | solution.py:392
  355.5 23.8 %collective-permute-start.40 = (bf16[352,384]{1,0:T(8,128)(2,1)S(1)}, bf16[352,384]{1,0:T(8,128)(2,1)S(1)}, u32[]{:S(2)}, u32[]{:S(2)}) collective-permute-start(bf16[352,384]{1,0:T(8,128)(2,1)S(1)} %get-tuple-element.115), channel_id=1, source_target_pairs={{0,4},{2,6},{4,0},{6,2},{1,5},{3,7},{5,1},{7,3},{8,12},{10,14},{12... | collective-permute-start | bytes 811016 | tf_op jit(solution)/shard_map/ppermute | solution.py:392
  370.8 12.7 %collective-permute-start.41 = (bf16[352,384]{1,0:T(8,128)(2,1)S(1)}, bf16[352,384]{1,0:T(8,128)(2,1)S(1)}, u32[]{:S(2)}, u32[]{:S(2)}) collective-permute-start(bf16[352,384]{1,0:T(8,128)(2,1)S(1)} %get-tuple-element.114), channel_id=1, source_target_pairs={{0,2},{2,0},{4,6},{6,4},{1,3},{3,1},{5,7},{7,5},{8,10},{10,8},{12,... | collective-permute-start | bytes 811016 | tf_op jit(solution)/shard_map/ppermute | solution.py:392
  372.7 17.4 %collective-permute-start.45 = (bf16[352,384]{1,0:T(8,128)(2,1)S(1)}, bf16[352,384]{1,0:T(8,128)(2,1)S(1)}, u32[]{:S(2)}, u32[]{:S(2)}) collective-permute-start(bf16[352,384]{1,0:T(8,128)(2,1)S(1)} %get-tuple-element.128), channel_id=1, source_target_pairs={{0,6},{2,4},{4,2},{6,0},{1,7},{3,5},{5,3},{7,1},{8,14},{10,12},{12... | collective-permute-start | bytes 811016 | tf_op jit(solution)/shard_map/ppermute | solution.py:392
  373.7 20.1 %collective-permute-start.46 = (bf16[352,384]{1,0:T(8,128)(2,1)S(1)}, bf16[352,384]{1,0:T(8,128)(2,1)S(1)}, u32[]{:S(2)}, u32[]{:S(2)}) collective-permute-start(bf16[352,384]{1,0:T(8,128)(2,1)S(1)} %get-tuple-element.127), channel_id=1, source_target_pairs={{0,4},{2,6},{4,0},{6,2},{1,5},{3,7},{5,1},{7,3},{8,12},{10,14},{12... | collective-permute-start | bytes 811016 | tf_op jit(solution)/shard_map/ppermute | solution.py:392
  378.5 15.4 %collective-permute-start.47 = (bf16[352,384]{1,0:T(8,128)(2,1)S(1)}, bf16[352,384]{1,0:T(8,128)(2,1)S(1)}, u32[]{:S(2)}, u32[]{:S(2)}) collective-permute-start(bf16[352,384]{1,0:T(8,128)(2,1)S(1)} %get-tuple-element.126), channel_id=1, source_target_pairs={{0,2},{2,0},{4,6},{6,4},{1,3},{3,1},{5,7},{7,5},{8,10},{10,8},{12,... | collective-permute-start | bytes 811016 | tf_op jit(solution)/shard_map/ppermute | solution.py:392
  403.2 79.3 %collective-permute-start.48 = (bf16[3,352,1024]{2,1,0:T(8,128)(2,1)}, bf16[3,352,1024]{2,1,0:T(8,128)(2,1)}, u32[]{:S(2)}, u32[]{:S(2)}) collective-permute-start(bf16[3,352,1024]{2,1,0:T(8,128)(2,1)} %bitcast_convert_fusion.2), channel_id=1, source_target_pairs={{0,1},{1,0},{2,3},{3,2},{4,5},{5,4},{6,7},{7,6},{8,9},{9,8},{10,11... | collective-permute-start | bytes 6488072 | tf_op jit(solution)/shard_map/ppermute | solution.py:392
  632.7 12.8 %collective-permute-start.49 = (f32[3]{0:T(128)S(1)}, f32[3]{0:T(128)S(1)}, u32[]{:S(2)}, u32[]{:S(2)}) collective-permute-start(f32[3]{0:T(128)S(1)} %get-tuple-element.166), channel_id=1, source_target_pairs={{0,1},{1,0},{2,3},{3,2},{4,5},{5,4},{6,7},{7,6},{8,9},{9,8},{10,11... | collective-permute-start | bytes 44 | tf_op jit(solution)/shard_map/ppermute | solution.py:392
  (76 other events, 458.3 us)
Sparse Core Ops, SparseCore 0:
  10.2 32.3 all-gather.8
  44.1 37.8 all-gather.12
  83.9 37.3 all-gather.6
  123.0 63.9 all-gather.10
  188.7 52.6 all-gather.14
  243.1 43.9 all-gather.16
  290.0 33.7 reduce-scatter.4
  327.0 88.3 reduce-scatter.6
  419.0 52.6 reduce-scatter.8
  475.4 48.9 reduce-scatter.10

commit v3 on v2

--- a/solution.py
+++ b/solution.py
@@ -215,16 +215,90 @@
     pl.semaphore_wait(barrier, len(devices))
 
 
-def grad_gather_kernel(
-    nz, nc, slot_blocks, early_ref, late_ref, out_ref, g_ref, l_ref, place_ref, part_ref, send, recv
+def span(start, size):
+    return pl.ds(pl.multiple_of(start, size & -size), size)
+
+
+class Local:
+    def __init__(self, sems):
+        self.sems, self.count, self.open = sems, 0, []
+
+    def start(self, src, dst):
+        copy = pltpu.make_async_copy(src, dst, self.sems.at[self.count])
+        self.count += 1
+        copy.start()
+        self.open.append(copy)
+        return copy
+
+    def wait(self, copy):
+        copy.wait()
+        self.open = [c for c in self.open if c is not copy]
+
+    def finish(self):
+        for copy in self.open:
+            copy.wait()
+        self.open = []
+
+
+def spread_plane(go, ref_of, me_c, cond=None):
+    own = ref_of(me_c, None)
+    return [go(own, own, {"context": me_c ^ 1}), go(own, own, {"context": me_c ^ 2})]
+
+
+def spread_plane_on(go, ref_of, me_c, near):
+    near[0].wait_recv()
+    piece = ref_of(me_c ^ 1, 0)
+    first = go(piece, piece, {"context": me_c ^ 2})
+    near[1].wait_recv()
+    piece = ref_of(me_c ^ 2, 1)
+    second = go(piece, piece, {"context": me_c ^ 1})
+    return [first, second]
+
+
+def forward_kernel(
+    nz,
+    nc,
+    tokens_ref,
+    gain_ref,
+    count_ref,
+    wq_ref,
+    wout_ref,
+    wup_ref,
+    wdown_ref,
+    x_out,
+    qkv_out,
+    o_out,
+    lse_out,
+    att_out,
+    cnt_out,
+    wq_out,
+    out_full,
+    up_full,
+    down_part,
+    tok,
+    x_all,
+    qkv,
+    o_all,
+    lse_all,
+    wq,
+    counts,
+    send,
+    recv,
+    local_sems,
 ):
     me_z, me_c, me_t = (lax.axis_index(a) for a in ("fsdp", "context", "tensor"))
-    slots = out_ref.shape[0]
+    images, local_len = att_out.shape[:2]
+    half = local_len // 2
+    seq = x_all.shape[1]
     core = {"tensor": 1 - me_t}
-    x_near, y_near = {"context": me_c ^ 1}, {"context": me_c ^ 2}
-    above, below = {"fsdp": me_z + 1}, {"fsdp": me_z - 1}
     z_peers = [{"fsdp": lax.rem(me_z + k, nz)} for k in range(1, nz)]
     c_peers = [{"context": me_c ^ k} for k in range(1, nc)]
+    local = Local(local_sems)
+    token_in = [
+        local.start(tokens_ref.at[i, span(me_t * half, half)], tok.at[i]) for i in range(images)
+    ]
+    depth = wq_ref.shape[0]
+    wq_own = local.start(wq_ref, wq.at[span(me_z * depth, depth)])
     greet(z_peers + c_peers + [core])
     moves = Moves(send, recv)
     sent = []
@@ -235,52 +309,388 @@
         sent.append(move)
         return move
 
-    late_in = [
-        go(late_ref.at[lax.rem(me_z + k, nz)], part_ref.at[k - 1], z_peers[k - 1])
+    wq_in = [go(wq_ref, wq.at[span(me_z * depth, depth)], peer) for peer in z_peers]
+    counts[me_c] = count_ref[...]
+    count_in = [go(count_ref, counts.at[me_c], peer) for peer in c_peers]
+
+    def to_line(src, dst):
+        local_copy = local.start(src, dst)
+        return [local_copy] + [go(src, dst, peer) for peer in z_peers]
+
+    cols, hid, depth_o = wout_ref.shape[0] // nc, wup_ref.shape[1] // nc, wout_ref.shape[1]
+    out_in = to_line(
+        wout_ref.at[span(me_c * cols, cols)],
+        out_full.at[span(me_c * cols, cols), span(me_z * depth_o, depth_o)],
+    )
+    up_in = to_line(
+        wup_ref.at[:, span(me_c * hid, hid)],
+        up_full.at[span(me_z * depth, depth), span(me_c * hid, hid)],
+    )
+    down_in = to_line(
+        wdown_ref.at[span(me_c * hid, hid)], down_part.at[:, span(me_z * depth_o, depth_o)]
+    )
+
+    def x_piece(i):
+        def at(member, part):
+            rows = span(member * local_len + me_t * half, half)
+            if part is None:
+                return x_all.at[i, rows]
+            return x_all.at[i, rows, pl.ds(part * (D // 2), D // 2)]
+
+        return at
+
+    swaps = [[] for _ in range(images)]
+
+    def swap(i, member, part=None):
+        piece = x_piece(i)(member, part)
+        swaps[i].append(go(piece, piece, core))
+
+    near = []
+    for i in range(images):
+        local.wait(token_in[i])
+        value = tok[i]
+        centred = value - jnp.mean(value, axis=-1, keepdims=True)
+        inv_std = lax.rsqrt(jnp.mean(centred * centred, axis=-1, keepdims=True) + 1e-06)
+        x_all[i, span(me_c * local_len + me_t * half, half)] = (
+            centred * inv_std * gain_ref[...]
+        ).astype(BF)
+        near.append(spread_plane(go, x_piece(i), me_c))
+        swap(i, me_c)
+    far = []
+    for i in range(images):
+        far.append(spread_plane_on(go, x_piece(i), me_c, near[i]))
+        swap(i, me_c ^ 1)
+        swap(i, me_c ^ 2)
+
+    local.wait(wq_own)
+    for move in wq_in:
+        move.wait_recv()
+    local.start(wq, wq_out)
+    for move in count_in:
+        move.wait_recv()
+    total = counts[0]
+    for k in range(1, nc):
+        total = total + counts[k]
+    cnt_out[...] = total
+
+    first = lax.broadcasted_iota(jnp.int32, (local_len, 128), 1) < HD
+    place = lax.broadcasted_iota(jnp.int32, (1, seq), 1)
+
+    def weight_plane(move_in, ref_of):
+        local.wait(move_in[0])
+        for move in move_in[1:]:
+            move.wait_recv()
+        return spread_plane(go, ref_of, me_c)
+
+    def out_piece(member, part):
+        rows = span(member * cols, cols)
+        return out_full.at[rows] if part is None else out_full.at[rows, pl.ds(part * (D // 2), D // 2)]
+
+    def up_piece(member, part):
+        at = span(member * hid, hid)
+        return up_full.at[:, at] if part is None else up_full.at[pl.ds(part * (D // 2), D // 2), at]
+
+    att_in = []
+    for i in range(images):
+        for part in range(2):
+            far[i][part].wait_recv()
+            swap(i, me_c ^ 3, part)
+        for move in swaps[i]:
+            move.wait_recv()
+        local.start(x_all.at[i], x_out.at[i])
+
+        @pl.loop(0, nc)
+        def _(chunk):
+            rows = span(chunk * local_len, local_len)
+            qkv[i, rows] = dot_nn(x_all[i, rows], wq[...]).astype(BF)
+
+        local.start(qkv.at[i], qkv_out.at[i])
+        bias = jnp.where(place < cnt_out[i : i + 1, 0:1], 0.0, -1e30)
+
+        @pl.loop(0, nc)
+        def _(chunk):
+            rows = span(chunk * local_len, local_len)
+            q = qkv[i, rows, 0:128] * SCALE
+            k = qkv[i, :, 128:256]
+            v = qkv[i, :, 256:384]
+            outs, sums = [], []
+            for head in range(2):
+                mask = first if head == 0 else jnp.logical_not(first)
+                scores = dot_nt(jnp.where(mask, q, jnp.zeros_like(q)), k) + bias
+                peak = jnp.max(scores, axis=-1, keepdims=True)
+                expo = jnp.exp(scores - peak)
+                norm = jnp.sum(expo, axis=-1, keepdims=True)
+                outs.append(dot_nn(expo.astype(BF), v) / norm)
+                sums.append(peak + jnp.log(norm))
+            o_all[i, rows] = jnp.where(first, outs[0], outs[1]).astype(BF)
+            lse_all[rows] = jnp.where(first, sums[0], sums[1])
+
+        mine = att_out.at[i, :, span(me_c * 128, 128)]
+        for k in range(1, nc):
+            att_in.append(
+                go(o_all.at[i, span((me_c ^ k) * local_len, local_len)], mine, c_peers[k - 1])
+            )
+        local.start(o_all.at[i, span(me_c * local_len, local_len)], mine)
+        local.start(o_all.at[i], o_out.at[i])
+        sums_t = lse_all[...].T
+        for head in range(2):
+            lse_out[i, 8 * head : 8 * head + 8, :] = jnp.broadcast_to(
+                sums_t[HD * head : HD * head + 1], (8, seq)
+            )
+        if i == 0:
+            out_near = weight_plane(out_in, out_piece)
+        if i == images - 1:
+            up_near = weight_plane(up_in, up_piece)
+            out_far = spread_plane_on(go, out_piece, me_c, out_near)
+    up_far = spread_plane_on(go, up_piece, me_c, up_near)
+    for move in att_in + out_far + up_far + down_in[1:]:
+        move.wait_recv()
+    local.finish()
+    for move in sent:
+        move.wait_send()
+
+
+def forward_attention(tokens, gain, counts, wq_part, w_out, w_up, w_down, nz, nc):
+    images, local_len = tokens.shape[:2]
+    seq = nc * local_len
+    cols, hid = w_out.shape[0], w_up.shape[1]
+    any_ = pl.BlockSpec(memory_space=pl.ANY)
+    vmem = pl.BlockSpec(memory_space=pltpu.VMEM)
+    return pl.pallas_call(
+        functools.partial(forward_kernel, nz, nc),
+        out_shape=(
+            jax.ShapeDtypeStruct((images, seq, D), BF),
+            jax.ShapeDtypeStruct((images, seq, 384), BF),
+            jax.ShapeDtypeStruct((images, seq, 128), BF),
+            jax.ShapeDtypeStruct((images, 16, seq), F32),
+            jax.ShapeDtypeStruct((images, local_len, cols), BF),
+            jax.ShapeDtypeStruct((8, 128), jnp.int32),
+            jax.ShapeDtypeStruct((D, 384), BF),
+            jax.ShapeDtypeStruct((cols, D), BF),
+            jax.ShapeDtypeStruct((D, hid), BF),
+            jax.ShapeDtypeStruct((hid // nc, D), BF),
+        ),
+        in_specs=[any_, vmem, vmem, any_, any_, any_, any_],
+        out_specs=(any_, any_, any_, vmem, any_, vmem, any_, any_, any_, any_),
+        scratch_shapes=[
+            pltpu.VMEM((images, local_len // 2, D), F32),
+            pltpu.VMEM((images, seq, D), BF),
+            pltpu.VMEM((images, seq, 384), BF),
+            pltpu.VMEM((images, seq, 128), BF),
+            pltpu.VMEM((seq, 128), F32),
+            pltpu.VMEM((D, 384), BF),
+            pltpu.VMEM((nc, 8, 128), jnp.int32),
+            pltpu.SemaphoreType.DMA((96,)),
+            pltpu.SemaphoreType.DMA((96,)),
+            pltpu.SemaphoreType.DMA((32,)),
+        ],
+        compiler_params=pltpu.CompilerParams(
+            collective_id=1, has_side_effects=True, vmem_limit_bytes=56 << 20
+        ),
+        name="forward_attention",
+    )(tokens, gain, counts, wq_part, w_out, w_up, w_down)
+
+
+def backward_kernel(
+    nz,
+    nc,
+    slot_blocks,
+    qkv_ref,
+    o_ref,
+    lse_ref,
+    att_ref,
+    cnt_ref,
+    term_out_ref,
+    term_up_ref,
+    down_ref,
+    x_ref,
+    wq_ref,
+    out_ref,
+    tok_out,
+    wq_out,
+    grad,
+    heads,
+    qkv,
+    o_all,
+    x_all,
+    dq_ref,
+    row_ref,
+    weight_ref,
+    own_ref,
+    far_y,
+    far_x,
+    near_in,
+    far_in,
+    mine_ref,
+    zpart_ref,
+    early_ref,
+    late_ref,
+    lpart_ref,
+    place_ref,
+    g_ref,
+    l_ref,
+    send,
+    recv,
+    local_sems,
+):
+    me_z, me_c, me_t = (lax.axis_index(a) for a in ("fsdp", "context", "tensor"))
+    images, local_len = att_ref.shape[:2]
+    slots = out_ref.shape[0]
+    x_c, y_c, far_c = me_c ^ 1, me_c ^ 2, me_c ^ 3
+    core, x_near, y_near = {"tensor": 1 - me_t}, {"context": x_c}, {"context": y_c}
+    above, below = {"fsdp": me_z + 1}, {"fsdp": me_z - 1}
+    z_peers = [{"fsdp": lax.rem(me_z + k, nz)} for k in range(1, nz)]
+    c_peers = [{"context": me_c ^ k} for k in range(1, nc)]
+    left, right = pl.ds(0, D // 2), pl.ds(D // 2, D // 2)
+    ups, downs = term_up_ref.shape[0], down_ref.shape[0]
+    terms = [(term_out_ref, 0)] + [(term_up_ref, j) for j in range(ups)]
+    local = Local(local_sems)
+    held = [
+        [local.start(a.at[i], b.at[i]) for a, b in ((qkv_ref, qkv), (o_ref, o_all))]
+        for i in range(images)
+    ]
+    x_in = [local.start(x_ref.at[i], x_all.at[i % 2]) for i in range(2)]
+    own_in, far_own = [], []
+    for index, (ref, block) in enumerate(terms):
+        own_in.append(local.start(ref.at[block, me_c], own_ref.at[index]))
+        far_own.append(local.start(ref.at[block, y_c, :, :, left], far_y.at[index]))
+        far_own.append(local.start(ref.at[block, x_c, :, :, right], far_x.at[index]))
+    mine_in = local.start(down_ref.at[:, me_z], mine_ref)
+    greet(z_peers + c_peers + [core])
+    moves = Moves(send, recv)
+    sent = []
+
+    def go(*args, **kw):
+        move = moves.make(*args, **kw)
+        move.start()
+        sent.append(move)
+        return move
+
+    grad_in = []
+    for i in range(images):
+        here = grad.at[i, span(me_c * local_len, local_len)]
+        grad_in.append(
+            [local.start(att_ref.at[i, :, span(me_c * 128, 128)], here)]
+            + [
+                go(att_ref.at[i, :, span((me_c ^ k) * 128, 128)], here, c_peers[k - 1])
+                for k in range(1, nc)
+            ]
+        )
+    near = []
+    for index, (ref, block) in enumerate(terms):
+        near.append(
+            [
+                go(ref.at[block, x_c, :, :, left], near_in.at[index, 0], x_near),
+                go(ref.at[block, far_c, :, :, left], near_in.at[index, 1], x_near),
+                go(ref.at[block, y_c, :, :, right], near_in.at[index, 2], y_near),
+                go(ref.at[block, far_c, :, :, right], near_in.at[index, 3], y_near),
+            ]
+        )
+    down_in = [
+        go(
+            down_ref.at[:, lax.rem(me_z + k, nz)],
+            zpart_ref.at[k - 1, pl.ds(len(terms), downs)],
+            z_peers[k - 1],
+        )
         for k in range(1, nz)
     ]
-    for slot in range(NBLK):
-        block = jnp.clip(slot_blocks[slot] - LATE, 0, EARLY - 1)
-        place_ref[slot] = early_ref[block]
-    placed = []
-    for k in range(1, nc):
-        theirs = place_ref.at[pl.ds((me_c ^ k) * slots, slots)]
-        placed.append(go(theirs, g_ref.at[:, me_t, me_c, me_z], c_peers[k - 1]))
-    for slot in range(slots):
-        g_ref[slot, me_t, me_c, me_z] = place_ref[me_c * slots + slot]
-
-    def along_fsdp(ref, member, ready):
-        ready()
-        own = ref.at[:, me_t, member, me_z]
-        up = go(own, own, above, cond=me_z < nz - 1, recv_cond=me_z > 0)
-        down = go(own, own, below, cond=me_z > 0, recv_cond=me_z < nz - 1)
-        return [up, down]
-
-    def onward(ref, member, last, hop):
-        up_in, down_in = last
-        up_z, down_z = me_z - hop, me_z + hop
-        up_in.wait_recv()
-        up = down = None
-        if hop < nz - 1:
-            piece = ref.at[:, me_t, member, up_z]
-            up = go(
-                piece,
-                piece,
-                above,
-                cond=jnp.logical_and(me_z < nz - 1, up_z >= 0),
-                recv_cond=up_z - 1 >= 0,
+    width = wq_ref.shape[1]
+
+    def wq_piece(member, part):
+        at = span(member * width, width)
+        return wq_out.at[:, at] if part is None else wq_out.at[pl.ds(part * (D // 2), D // 2), at]
+
+    wq_own = local.start(wq_ref, wq_piece(me_c, None))
+    first = lax.broadcasted_iota(jnp.int32, (local_len, 128), 1) < HD
+    place = lax.broadcasted_iota(jnp.int32, (local_len, 128), 0)
+    weight_ref[...] = jnp.zeros_like(weight_ref)
+    far_moves = []
+
+    def sum_step(index):
+        for move in near[index]:
+            move.wait_recv()
+        local.wait(own_in[index])
+        local.wait(far_own[2 * index])
+        local.wait(far_own[2 * index + 1])
+        far_y[index] += near_in[index, 1]
+        first_far = go(far_y.at[index], far_in.at[index, 0], y_near)
+        far_x[index] += near_in[index, 3]
+        far_moves.append((first_far, go(far_x.at[index], far_in.at[index, 1], x_near)))
+
+    for i in range(images):
+        for copy in held[i]:
+            local.wait(copy)
+        local.wait(grad_in[i][0])
+        for move in grad_in[i][1:]:
+            move.wait_recv()
+        prod = (grad[i].astype(F32) * o_all[i].astype(F32)).T
+        for head in range(2):
+            row_ref[8 * head : 8 * head + 8, :] = jnp.broadcast_to(
+                jnp.sum(prod[HD * head : HD * (head + 1)], axis=0, keepdims=True),
+                (8, prod.shape[1]),
             )
-        down_in.wait_recv()
-        if hop < nz - 1:
-            piece = ref.at[:, me_t, member, down_z]
-            down = go(
-                piece,
-                piece,
-                below,
-                cond=jnp.logical_and(me_z > 0, down_z <= nz - 1),
-                recv_cond=down_z + 1 <= nz - 1,
-            )
-        return [up, down], [(up_z, up_z >= 0), (down_z, down_z <= nz - 1)]
+        dq_ref[...] = jnp.zeros_like(dq_ref)
+        real = cnt_ref[i : i + 1, :]
+
+        @pl.loop(0, nc)
+        def _(chunk):
+            rows = span(chunk * local_len, local_len)
+            q = qkv[i, :, 0:128]
+            k = qkv[i, rows, 128:256] * SCALE
+            v = qkv[i, rows, 256:384]
+            do = grad[i]
+            live = (place + chunk * local_len < real)[:, 0:1]
+            dks, dvs = [], []
+            for head in range(2):
+                mask = first if head == 0 else jnp.logical_not(first)
+                kh = jnp.where(mask, k, jnp.zeros_like(k))
+                vh = jnp.where(mask, v, jnp.zeros_like(v))
+                lse = lse_ref[i, 8 * head : 8 * head + 1, :]
+                delta = row_ref[8 * head : 8 * head + 1, :]
+                prob = jnp.where(live, jnp.exp(dot_nt(kh, q) - lse), 0.0)
+                ds = (prob * (dot_nt(vh, do) - delta)).astype(BF)
+                dvs.append(dot_nn(prob.astype(BF), do))
+                dks.append(dot_nn(ds, q) * SCALE)
+                dq_ref[...] += dot_tn(ds, kh)
+            heads[i, rows, 128:256] = jnp.where(first, dks[0], dks[1]).astype(BF)
+            heads[i, rows, 256:384] = jnp.where(first, dvs[0], dvs[1]).astype(BF)
+
+        heads[i, :, 0:128] = dq_ref[...].astype(BF)
+        local.wait(x_in[i])
+
+        @pl.loop(0, nc)
+        def _(chunk):
+            rows = span(chunk * local_len, local_len)
+            weight_ref[...] += dot_tn(heads[i, rows], x_all[i % 2, rows])
+
+        if i + 2 < images:
+            x_in.append(local.start(x_ref.at[i + 2], x_all.at[i % 2]))
+        if i == 1:
+            for index in range(3):
+                sum_step(index)
+    sub = late_ref.shape[2]
+    for z in range(nz):
+        for j in range(LATE):
+            late_ref[z, j] = weight_ref[pl.ds(j * 128 + z * sub, sub)].astype(BF)
+    late_in = [
+        go(late_ref.at[lax.rem(me_z + k, nz)], lpart_ref.at[k - 1], z_peers[k - 1])
+        for k in range(1, nz)
+    ]
+    for index in range(3, len(terms)):
+        sum_step(index)
+    for index in range(len(terms)):
+        for move in far_moves[index]:
+            move.wait_recv()
+        own_ref[index, :, :, left] += near_in[index, 0] + far_in[index, 0]
+        own_ref[index, :, :, right] += near_in[index, 2] + far_in[index, 1]
+    zterm_in = [
+        go(
+            own_ref.at[:, lax.rem(me_z + k, nz)],
+            zpart_ref.at[k - 1, pl.ds(0, len(terms))],
+            z_peers[k - 1],
+        )
+        for k in range(1, nz)
+    ]
 
     swapped = []
 
@@ -290,21 +700,34 @@
             piece = ref.at[:, me_t, member, z, :, columns]
         swapped.append(go(piece, piece, core, cond=cond, recv_cond=cond))
 
-    lines = {}
-    for k in range(nc):
-        member = me_c ^ k
-        lines[k] = along_fsdp(
-            g_ref, member, (lambda: None) if k == 0 else placed[k - 1].wait_recv
-        )
-        swap(g_ref, member, me_z)
+    def along_fsdp(ref, member):
+        own = ref.at[:, me_t, member, me_z]
+        return [
+            go(own, own, above, cond=me_z < nz - 1, recv_cond=me_z > 0),
+            go(own, own, below, cond=me_z > 0, recv_cond=me_z < nz - 1),
+        ]
+
+    def onward(ref, member, last, hop):
+        up_z, down_z = me_z - hop, me_z + hop
+        last[0].wait_recv()
+        up = down = None
+        if hop < nz - 1:
+            piece = ref.at[:, me_t, member, up_z]
+            cond = jnp.logical_and(me_z < nz - 1, up_z >= 0)
+            up = go(piece, piece, above, cond=cond, recv_cond=up_z - 1 >= 0)
+        last[1].wait_recv()
+        if hop < nz - 1:
+            piece = ref.at[:, me_t, member, down_z]
+            cond = jnp.logical_and(me_z > 0, down_z <= nz - 1)
+            down = go(piece, piece, below, cond=cond, recv_cond=down_z + 1 <= nz - 1)
+        return [up, down], [(up_z, up_z >= 0), (down_z, down_z <= nz - 1)]
 
     total = late_ref[me_z].astype(F32)
     for k in range(1, nz):
         late_in[k - 1].wait_recv()
-        total = total + part_ref[k - 1].astype(F32)
+        total = total + lpart_ref[k - 1].astype(F32)
     l_ref[:, me_t, me_c, me_z] = total.astype(BF)
-    late_line = along_fsdp(l_ref, me_c, lambda: None)
-    left, right = pl.ds(0, D // 2), pl.ds(D // 2, D // 2)
+    late_line = along_fsdp(l_ref, me_c)
     near = []
 
     def spread(z, cond=None):
@@ -319,26 +742,62 @@
         )
         swap(l_ref, me_c, z, cond)
 
+    for move in down_in + zterm_in:
+        move.wait_recv()
+    local.wait(mine_in)
+    for block in range(EARLY):
+        if block < len(terms):
+            total = own_ref[block, me_z].astype(F32)
+        else:
+            total = mine_ref[block - len(terms)].astype(F32)
+        for k in range(1, nz):
+            total = total + zpart_ref[k - 1, block].astype(F32)
+        early_ref[block] = total.astype(BF)
+    for slot in range(NBLK):
+        block = jnp.clip(slot_blocks[slot] - LATE, 0, EARLY - 1)
+        place_ref[slot] = early_ref[block]
+    placed = []
+    for k in range(1, nc):
+        theirs = place_ref.at[pl.ds((me_c ^ k) * slots, slots)]
+        placed.append(go(theirs, g_ref.at[:, me_t, me_c, me_z], c_peers[k - 1]))
+    for slot in range(slots):
+        g_ref[slot, me_t, me_c, me_z] = place_ref[me_c * slots + slot]
+    lines = {}
+    for k in range(nc):
+        member = me_c ^ k
+        if k > 0:
+            placed[k - 1].wait_recv()
+        lines[k] = along_fsdp(g_ref, member)
+        swap(g_ref, member, me_z)
+    tok_in = []
+    for i in range(images):
+        there = tok_out.at[i, :, span(me_c * 384, 384)]
+        for k in range(1, nc):
+            tok_in.append(
+                go(heads.at[i, span((me_c ^ k) * local_len, local_len)], there, c_peers[k - 1])
+            )
+        local.start(heads.at[i, span(me_c * local_len, local_len)], there)
     spread(me_z)
+    local.wait(wq_own)
+    wq_near = spread_plane(go, wq_piece, me_c)
     far = []
     done = 0
 
     def spread_on():
         nonlocal done
-        for z, cond, x_in, y_in in near[done:]:
-            x_in.wait_recv()
-            piece = l_ref.at[:, me_t, me_c ^ 1, z, :, left]
+        for z, cond, x_move, y_move in near[done:]:
+            x_move.wait_recv()
+            piece = l_ref.at[:, me_t, x_c, z, :, left]
             far.append((z, cond, left, go(piece, piece, y_near, cond=cond, recv_cond=cond)))
-            swap(l_ref, me_c ^ 1, z, cond)
-            y_in.wait_recv()
-            piece = l_ref.at[:, me_t, me_c ^ 2, z, :, right]
+            swap(l_ref, x_c, z, cond)
+            y_move.wait_recv()
+            piece = l_ref.at[:, me_t, y_c, z, :, right]
             far.append((z, cond, right, go(piece, piece, x_near, cond=cond, recv_cond=cond)))
-            swap(l_ref, me_c ^ 2, z, cond)
+            swap(l_ref, y_c, z, cond)
         done = len(near)
 
     for hop in range(1, nz):
-        before = late_line
-        late_line, here = onward(l_ref, me_c, before, hop)
+        late_line, here = onward(l_ref, me_c, late_line, hop)
         for z, cond in here:
             spread(z, cond)
         for k in range(nc):
@@ -347,44 +806,100 @@
             for z, cond in here:
                 swap(g_ref, member, z, cond)
         spread_on()
+    wq_far = spread_plane_on(go, wq_piece, me_c, wq_near)
     for z, cond, columns, move in far:
         move.wait_recv()
-        swap(l_ref, me_c ^ 3, z, cond, columns)
+        swap(l_ref, far_c, z, cond, columns)
     for move in swapped:
         move.wait_recv()
+    for move in tok_in + wq_far:
+        move.wait_recv()
+    for move in sent:
+        move.wait_send()
     for slot in range(slots):
         block = slot_blocks[me_c * slots + slot]
         late = l_ref[jnp.clip(block, 0, LATE - 1)]
-        out_ref[slot] = jnp.where(block < LATE, late, g_ref[slot])
-    for move in sent:
-        move.wait_send()
-
-
-def grad_gather(block_of, early, late, nz, nc, nt):
-    sub = early.shape[1]
+        g_ref[slot] = jnp.where(block < LATE, late, g_ref[slot])
+        local.start(g_ref.at[slot], out_ref.at[slot])
+    local.finish()
+
+
+def backward_attention(
+    block_of, qkv, o_heads, lse, grad_att, counts, term_out, term_up, down, x_all, wq, nz, nc, nt
+):
+    images, seq = qkv.shape[:2]
+    local_len = seq // nc
+    sub = term_up.shape[3]
     slots = NBLK // nc
+    terms = 1 + term_up.shape[0]
+    any_ = pl.BlockSpec(memory_space=pl.ANY)
+    vmem = pl.BlockSpec(memory_space=pltpu.VMEM)
     shape = (slots, nt, nc, nz, sub, D)
-    count = 192
-    vmem = pl.BlockSpec(memory_space=pltpu.VMEM)
-    out = pl.pallas_call(
-        functools.partial(grad_gather_kernel, nz, nc),
-        out_shape=jax.ShapeDtypeStruct(shape, BF),
-        in_specs=[pl.BlockSpec(memory_space=pltpu.SMEM), vmem, vmem],
-        out_specs=vmem,
+    out, tok, wq_all = pl.pallas_call(
+        functools.partial(backward_kernel, nz, nc),
+        out_shape=(
+            jax.ShapeDtypeStruct(shape, BF),
+            jax.ShapeDtypeStruct((images, local_len, nc * 384), BF),
+            jax.ShapeDtypeStruct((D, nc * 384), BF),
+        ),
+        in_specs=[
+            pl.BlockSpec(memory_space=pltpu.SMEM),
+            any_,
+            any_,
+            vmem,
+            any_,
+            vmem,
+            any_,
+            any_,
+            any_,
+            any_,
+            any_,
+        ],
+        out_specs=(any_, any_, any_),
         scratch_shapes=[
+            pltpu.VMEM((images, seq, 128), BF),
+            pltpu.VMEM((images, seq, 384), BF),
+            pltpu.VMEM((images, seq, 384), BF),
+            pltpu.VMEM((images, seq, 128), BF),
+            pltpu.VMEM((2, seq, D), BF),
+            pltpu.VMEM((seq, 128), F32),
+            pltpu.VMEM((16, seq), F32),
+            pltpu.VMEM((384, D), F32),
+            pltpu.VMEM((terms, nz, sub, D), BF),
+            pltpu.VMEM((terms, nz, sub, D // 2), BF),
+            pltpu.VMEM((terms, nz, sub, D // 2), BF),
+            pltpu.VMEM((terms, 4, nz, sub, D // 2), BF),
+            pltpu.VMEM((terms, 2, nz, sub, D // 2), BF),
+            pltpu.VMEM((EARLY - terms, sub, D), BF),
+            pltpu.VMEM((nz - 1, EARLY, sub, D), BF),
+            pltpu.VMEM((EARLY, sub, D), BF),
+            pltpu.VMEM((nz, LATE, sub, D), BF),
+            pltpu.VMEM((nz - 1, LATE, sub, D), BF),
+            pltpu.VMEM((NBLK, sub, D), BF),
             pltpu.VMEM(shape, BF),
             pltpu.VMEM((LATE, nt, nc, nz, sub, D), BF),
-            pltpu.VMEM((NBLK, sub, D), BF),
-            pltpu.VMEM((nz - 1, LATE, sub, D), BF),
-            pltpu.SemaphoreType.DMA((count,)),
-            pltpu.SemaphoreType.DMA((count,)),
+            pltpu.SemaphoreType.DMA((256,)),
+            pltpu.SemaphoreType.DMA((256,)),
+            pltpu.SemaphoreType.DMA((64,)),
         ],
         compiler_params=pltpu.CompilerParams(
-            collective_id=0, has_side_effects=True, vmem_limit_bytes=40 << 20
+            collective_id=2, has_side_effects=True, vmem_limit_bytes=61 << 20
         ),
-        name="grad_gather",
-    )(block_of, early, late)
-    return out.reshape(slots, D, D)
+        name="backward_attention",
+    )(
+        block_of,
+        qkv,
+        o_heads,
+        lse,
+        grad_att,
+        counts,
+        term_out,
+        term_up,
+        down,
+        x_all,
+        wq,
+    )
+    return out.reshape(slots, D, D), tok, wq_all
 
 
 def xor_permute(value, axis, step):
@@ -460,6 +975,116 @@
     return jnp.where(
         (mine < LATE)[:, None, None], late_full[jnp.clip(mine, 0, LATE - 1)], early_full
     )
+
+
+def to_natural(value, me_t, half_len):
+    parts = value.reshape((-1, half_len) + value.shape[1:])
+    return jnp.where(me_t > 0, parts[::-1], parts).reshape(value.shape)
+
+
+def forward_plain(tokens, gain, key_mask, w_qkv, w_out, w_up, w_down):
+    images, local_len = tokens.shape[:2]
+    nc, nt = (lax.axis_size(a) for a in ("context", "tensor"))
+    me_c, me_t = (lax.axis_index(a) for a in ("context", "tensor"))
+    cols = w_qkv.shape[2] // nc
+    half_len = local_len // nt
+    wq_part = lax.dynamic_slice_in_dim(w_qkv, me_c * cols, cols, 2)
+    wq = gather_fsdp(wq_part).reshape(D, 3 * cols)
+
+    def two_stage(weight, member_axis, fsdp_axis):
+        width = weight.shape[member_axis] // nc
+        part = lax.dynamic_slice_in_dim(weight, me_c * width, width, member_axis)
+        part = lax.all_gather(part, "fsdp", axis=fsdp_axis, tiled=True)
+        return lax.all_gather(part, "context", axis=member_axis, tiled=True)
+
+    out_full = two_stage(w_out, 0, 1)
+    up_full = two_stage(w_up, 1, 0)
+    down_full = two_stage(w_down, 0, 1)
+
+    counts = jnp.sum(key_mask, axis=1)
+    real = counts
+    for k in range(1, nc):
+        real = real + xor_permute(counts, "context", k)
+    position = (
+        (me_c ^ jnp.arange(nc))[:, None, None] * local_len
+        + (me_t ^ jnp.arange(nt))[None, :, None] * half_len
+        + jnp.arange(half_len)[None, None, :]
+    ).reshape(-1)
+    live = position[None, :] < real[:, None]
+    bias = jnp.where(live, 0.0, -1e30).astype(F32)
+    live_col = jnp.broadcast_to(live[:, :, None].astype(F32), (images, SEQ, 128))
+
+    normed1, inv_std1, pre_norm1 = norm_fwd(tokens, gain)
+    normed1_low = pre_norm1.astype(BF)
+
+    x_all, qkv, out_heads, log_sums, attended = [], [], [], [], []
+    for i in range(images):
+        mine = lax.dynamic_slice_in_dim(normed1_low[i], me_t * half_len, half_len, 0)
+        held = jnp.stack([mine] + [xor_permute(mine, "context", k) for k in range(1, nc)])
+        other = xor_permute(held, "tensor", 1)
+        x_i = jnp.stack([held, other], axis=1).reshape(SEQ, D)
+        qkv_i = dot_nn(x_i, wq).astype(BF)
+        o_i, lse_i = attn_fwd(qkv_i, bias[i][None])
+        chunks = o_i.reshape(nc, local_len, 2 * HD)
+        moved = [to_natural(chunks[0], me_t, half_len)] + [
+            to_natural(xor_permute(chunks[k], "context", k), me_t, half_len) for k in range(1, nc)
+        ]
+        attended.append(jnp.concatenate(xor_order(moved, me_c), axis=-1))
+        x_all.append(x_i)
+        qkv.append(qkv_i)
+        out_heads.append(o_i)
+        log_sums.append(lse_i)
+    attended = jnp.stack(attended)
+    return (
+        jnp.stack(x_all),
+        jnp.stack(qkv),
+        jnp.stack(out_heads),
+        jnp.stack(log_sums),
+        attended,
+        live_col,
+        wq,
+        out_full,
+        up_full,
+        down_full,
+        normed1,
+        inv_std1,
+    )
+
+
+def backward_plain(qkv, out_heads, log_sums, grad_att, live_col, early, wq):
+    images, local_len = grad_att.shape[:2]
+    nz, nc, nt = (lax.axis_size(a) for a in ("fsdp", "context", "tensor"))
+    me_c, me_t = (lax.axis_index(a) for a in ("context", "tensor"))
+    cols = grad_att.shape[2] // nc
+    half_len = local_len // nt
+    sub = early.shape[2]
+    grad_heads = []
+    grad_tok = []
+    for i in range(images):
+        pieces = [grad_att[i, :, j * cols : (j + 1) * cols] for j in range(nc)]
+        pieces = [to_natural(p, me_t, half_len) for p in xor_order(pieces, me_c)]
+        grad_i = jnp.concatenate(
+            [pieces[0]] + [xor_permute(pieces[k], "context", k) for k in range(1, nc)]
+        )
+        g_i = attn_bwd(qkv[i], grad_i, out_heads[i], log_sums[i], live_col[i])
+        chunks = g_i.reshape(nc, local_len, 3 * cols)
+        moved = [to_natural(chunks[0], me_t, half_len)] + [
+            to_natural(xor_permute(chunks[k], "context", k), me_t, half_len) for k in range(1, nc)
+        ]
+        grad_tok.append(jnp.stack(xor_order(moved, me_c), axis=1))
+        grad_heads.append(g_i)
+    grad_tok = jnp.stack(grad_tok)
+    wq_all = lax.all_gather(wq, "context", axis=0, tiled=False)
+    grad_n1 = sum_tensor(
+        jnp.einsum("isjc,jdc->isd", grad_tok, wq_all, preferred_element_type=F32)
+    )
+    early = lax.psum_scatter(
+        jnp.swapaxes(early, 0, 1).reshape(-1, D),
+        "fsdp",
+        scatter_dimension=0,
+        tiled=True,
+    ).reshape(EARLY, sub, D)
+    return jnp.stack(grad_heads), grad_n1, early
 
 
 def per_device(
@@ -487,59 +1112,42 @@
     hidden = w_up.shape[1]
     up_blocks = hidden // half_width
     cols = half_width // nc
-    half_len = local_len // nt
-
-    wq_part = lax.dynamic_slice_in_dim(w_qkv, me_c * cols, cols, 2)
-    wq = gather_fsdp(wq_part).reshape(D, 3 * cols)
-
-    def two_stage(weight, member_axis, fsdp_axis):
-        width = weight.shape[member_axis] // nc
-        part = lax.dynamic_slice_in_dim(weight, me_c * width, width, member_axis)
-        part = lax.all_gather(part, "fsdp", axis=fsdp_axis, tiled=True)
-        return lax.all_gather(part, "context", axis=member_axis, tiled=True)
-
-    out_full = two_stage(w_out, 0, 1)
-    up_full = two_stage(w_up, 1, 0)
-    down_full = two_stage(w_down, 0, 1)
-
-    counts = jnp.sum(key_mask, axis=1)
-    real = counts
-    for k in range(1, nc):
-        real = real + xor_permute(counts, "context", k)
-    position = (
-        (me_c ^ jnp.arange(nc))[:, None, None] * local_len
-        + (me_t ^ jnp.arange(nt))[None, :, None] * half_len
-        + jnp.arange(half_len)[None, None, :]
-    ).reshape(-1)
-    live = position[None, :] < real[:, None]
-    bias = jnp.where(live, 0.0, -1e30).astype(F32)
-    live_col = jnp.broadcast_to(live[:, :, None].astype(F32), (images, SEQ, 128))
-
-    normed1, inv_std1, pre_norm1 = norm_fwd(tokens, gains[0])
-    normed1_low = pre_norm1.astype(BF)
-
-    def to_natural(value):
-        parts = value.reshape((nt, half_len) + value.shape[1:])
-        return jnp.where(me_t > 0, parts[::-1], parts).reshape(value.shape)
-
-    x_all, qkv, out_heads, log_sums, attended = [], [], [], [], []
-    for i in range(images):
-        mine = lax.dynamic_slice_in_dim(normed1_low[i], me_t * half_len, half_len, 0)
-        held = jnp.stack([mine] + [xor_permute(mine, "context", k) for k in range(1, nc)])
-        other = xor_permute(held, "tensor", 1)
-        x_i = jnp.stack([held, other], axis=1).reshape(SEQ, D)
-        qkv_i = dot_nn(x_i, wq).astype(BF)
-        o_i, lse_i = attn_fwd(qkv_i, bias[i][None])
-        chunks = o_i.reshape(nc, local_len, 2 * HD)
-        moved = [to_natural(chunks[0])] + [
-            to_natural(xor_permute(chunks[k], "context", k)) for k in range(1, nc)
-        ]
-        attended.append(jnp.concatenate(xor_order(moved, me_c), axis=-1))
-        x_all.append(x_i)
-        qkv.append(qkv_i)
-        out_heads.append(o_i)
-        log_sums.append(lse_i)
-    attended = jnp.stack(attended)
+    fast = nz == 4 and nc == 4
+    if fast:
+        wq_part = lax.dynamic_slice_in_dim(w_qkv, me_c * cols, cols, 2).reshape(-1, 3 * cols)
+        counts = jnp.pad(jnp.sum(key_mask, axis=1), (0, 8 - images))
+        counts = jnp.broadcast_to(counts[:, None], (8, 128))
+        (
+            x_all,
+            qkv,
+            out_heads,
+            log_sums,
+            attended,
+            counts,
+            wq,
+            out_full,
+            up_full,
+            down_part,
+        ) = forward_attention(
+            tokens, gains[0:1], counts, wq_part, w_out, w_up, w_down, nz, nc
+        )
+        down_full = lax.all_gather(down_part, "context", axis=0, tiled=True)
+        normed1, inv_std1, _ = norm_fwd(tokens, gains[0])
+    else:
+        (
+            x_all,
+            qkv,
+            out_heads,
+            log_sums,
+            attended,
+            live_col,
+            wq,
+            out_full,
+            up_full,
+            down_full,
+            normed1,
+            inv_std1,
+        ) = forward_plain(tokens, gains[0], key_mask, w_qkv, w_out, w_up, w_down)
 
     branch_attn = sum_tensor(
         jnp.einsum("ish,hd->isd", attended, out_full, preferred_element_type=F32)
@@ -568,63 +1176,57 @@
         "isd,hd->ish", grad_branch, out_full, preferred_element_type=F32
     ).astype(BF)
 
-    term_qkv = None
-    grad_tok = []
-    for i in range(images):
-        pieces = [grad_att[i, :, j * cols : (j + 1) * cols] for j in range(nc)]
-        pieces = [to_natural(p) for p in xor_order(pieces, me_c)]
-        grad_i = jnp.concatenate(
-            [pieces[0]] + [xor_permute(pieces[k], "context", k) for k in range(1, nc)]
+    sub = half_width // nc // nz
+    onehot = (owner[:, None] == jnp.arange(NBLK, dtype=jnp.int32)[None, :]).astype(jnp.int32)
+    block_of = jnp.sum(onehot * jnp.arange(NBLK, dtype=jnp.int32)[:, None], axis=0)
+
+    def early_term(left, right):
+        term = dot_tn(left.reshape(tok_rows, -1), right.reshape(tok_rows, D)).astype(BF)
+        return term.reshape(-1, nc, nz, sub, D)
+
+    def early_sum(term):
+        return lax.psum_scatter(
+            jnp.swapaxes(term, 0, 1).reshape(-1, D), "context", scatter_dimension=0, tiled=True
+        ).reshape(-1, nz, sub, D)
+
+    term_out = early_term(attended, grad_branch)
+    term_up = early_term(grad_pre, normed2_low)
+    down = early_sum(early_term(act_low, grad_mlp))
+    if fast:
+        grad_full, grad_tok, wq_all = backward_attention(
+            block_of,
+            qkv,
+            out_heads,
+            log_sums,
+            grad_att,
+            counts,
+            term_out,
+            term_up,
+            down,
+            x_all,
+            wq,
+            nz,
+            nc,
+            nt,
         )
-        g_i = attn_bwd(qkv[i], grad_i, out_heads[i], log_sums[i], live_col[i])
-        chunks = g_i.reshape(nc, local_len, 3 * cols)
-        moved = [to_natural(chunks[0])] + [
-            to_natural(xor_permute(chunks[k], "context", k)) for k in range(1, nc)
-        ]
-        grad_tok.append(jnp.stack(xor_order(moved, me_c), axis=1))
-        term = dot_tn(g_i, x_all[i])
-        term_qkv = term if term_qkv is None else term_qkv + term
-    grad_tok = jnp.stack(grad_tok)
-    wq_all = lax.all_gather(wq, "context", axis=0, tiled=False)
-    grad_n1 = sum_tensor(
-        jnp.einsum("isjc,jdc->isd", grad_tok, wq_all, preferred_element_type=F32)
-    )
+        grad_n1 = sum_tensor(
+            lax.dot_general(
+                grad_tok, wq_all, (((2,), (1,)), ((), ())), preferred_element_type=F32
+            )
+        )
+    else:
+        early = jnp.concatenate([early_sum(term_out), early_sum(term_up), down], axis=0)
+        grad_heads, grad_n1, early = backward_plain(
+            qkv, out_heads, log_sums, grad_att, live_col, early, wq
+        )
+        term_qkv = jnp.einsum("isk,isd->kd", grad_heads, x_all, preferred_element_type=F32)
+        late = jnp.swapaxes(term_qkv.astype(BF).reshape(LATE, nz, sub, D), 0, 1)
+        grad_full = grad_gather_plain(block_of, early, late, nz, nc)
     input_part, grad_gain1 = norm_back(grad_n1, gains[0], normed1, inv_std1)
     grad_tokens = grad_middle + input_part
     grad_gain3 = jnp.sum(grad_middle * branch_attn, axis=(0, 1))
     grad_gain4 = jnp.sum(cotangent * branch_mlp, axis=(0, 1))
     gain_terms = jnp.stack([grad_gain1, grad_gain2, grad_gain3, grad_gain4], axis=0)
-
-    def early_terms(left, right):
-        term = dot_tn(left.reshape(tok_rows, -1), right.reshape(tok_rows, D)).astype(BF)
-        term = jnp.swapaxes(term.reshape(-1, nc, half_width // nc, D), 0, 1)
-        return lax.psum_scatter(
-            term.reshape(-1, D), "context", scatter_dimension=0, tiled=True
-        ).reshape(-1, half_width // nc, D)
-
-    early = jnp.concatenate(
-        [
-            early_terms(attended, grad_branch),
-            early_terms(grad_pre, normed2_low),
-            early_terms(act_low, grad_mlp),
-        ],
-        axis=0,
-    )
-    sub = half_width // nc // nz
-    early = lax.psum_scatter(
-        jnp.swapaxes(early.reshape(EARLY, nz, sub, D), 0, 1).reshape(-1, D),
-        "fsdp",
-        scatter_dimension=0,
-        tiled=True,
-    ).reshape(EARLY, sub, D)
-    onehot = (owner[:, None] == jnp.arange(NBLK, dtype=jnp.int32)[None, :]).astype(jnp.int32)
-    block_of = jnp.sum(onehot * jnp.arange(NBLK, dtype=jnp.int32)[:, None], axis=0)
-
-    late = jnp.swapaxes(term_qkv.astype(BF).reshape(LATE, nz, sub, D), 0, 1)
-    if nz == 4 and nc == 4:
-        grad_full = grad_gather(block_of, early, late, nz, nc, nt)
-    else:
-        grad_full = grad_gather_plain(block_of, early, late, nz, nc)
 
     row_count = half_width // nz
     row_offset = me_t * half_width + me_z * row_count

time: 667 us -> 526 us (0.79)
  Pallas kernels: 164 us -> 330 us
  waiting for transfers between devices: 205 us -> 39.6 us
  starting transfers between devices: 64.1 us -> 11.3 us
  other arithmetic: 59.3 us -> 32.2 us
  local copies, waits for them, and re-layouts: 35.5 us -> 8.86 us
  blocking collectives: 17.7 us -> 0 us
  matrix products: 98.9 us -> 82.6 us
    pallas_call x7 -> x2, Pallas kernels: 164 us -> 330 us  [the longest x1 211 us: backward_attention(): pl.pallas_call(functools.partial(backward_kernel, nz, nc), out_shape=(jax...]
    reduce_scatter x4 -> x1, waiting for transfers between devices: 87 us -> 8.55 us  [early_sum(): lax.psum_scatter(jnp.swapaxes(term, 0, 1).reshape(-1, D), 'context', scat...]
    ppermute x49 -> x7, waiting for transfers between devices: 74.7 us -> 8.26 us  [xor_permute(): return lax.ppermute(value, axis, [(j, j ^ step) for j in range(size)])]
    ppermute x49 -> x7, starting transfers between devices: 53.1 us -> 2.61 us  [xor_permute(): return lax.ppermute(value, axis, [(j, j ^ step) for j in range(size)])]
    all_gather x6 -> x1, waiting for transfers between devices: 38.7 us -> 20.7 us  [per_device(): down_full = lax.all_gather(down_part, 'context', axis=0, tiled=True)]
    all_gather x1 -> x0, blocking collectives: 17.7 us -> none  [two_stage(): part = lax.all_gather(part, 'fsdp', axis=fsdp_axis, tiled=True)]
    another operation x12 -> x0, other arithmetic: 17.3 us -> none  [the longest x6 13 us: per_device(): x_i = jnp.stack([held, other], axis=1).reshape(SEQ, D)]
    unnamed x119 -> x57, local copies, waits for them, and re-layouts: 17.3 us -> 3.41 us
  transfers between devices with their start and end apart: 68 -> 15, of which waited for: 29 -> 7; matrix products, arithmetic and copies ran while one was open for 25% -> 20% of each run, Pallas kernels for 11% -> 0%
where the time goes in v3:
time: 526 us; the launch traced here: 519 us
  Pallas kernels  330 us (63%)
  matrix products  82.6 us (16%)
  waiting for transfers between devices  39.6 us (8%)
  other arithmetic  32.2 us (6%)
  between operations  15 us (3%)
  starting transfers between devices  11.3 us (2%)
  local copies, waits for them, and re-layouts  8.86 us (2%)
    pallas_call x1, Pallas kernels, backward_attention(): pl.pallas_call(functools.partial(backward_kernel, nz, nc), out_shape=(jax...  211 us
    pallas_call x1, Pallas kernels, forward_attention(): pl.pallas_call(functools.partial(forward_kernel, nz, nc), out_shape=(jax....  118 us
    all_gather x1, waiting for transfers between devices, per_device(): down_full = lax.all_gather(down_part, 'context', axis=0, tiled=True)  20.7 us
    dot_general x3, matrix products, dot_tn(): lax.dot_general(a, b, (((0,), (0,)), ((), ())), preferred_element_type=F32)  16.5 us
    dot_general x1, matrix products, per_device(): jnp.einsum('srb,sbc->src', inner_prod, root_right.astype(BF), preferred_e...  11.1 us
    dot_general x1, matrix products, per_device(): jnp.einsum('isd,fd->isf', grad_mlp, down_full, preferred_element_type=F32)  10.8 us
  transfers between devices with their start and end apart: 15, of which 7 were waited for; matrix products, arithmetic and copies ran while one was open for 20% of the time, Pallas kernels for 0%

profile of v3, /device:TPU:0, one launch (start us, length us, event | category | flops | bytes accessed | tf_op | source)
XLA Modules:
  0.0 519.0 jit_solution(3254129448772614466)
XLA Ops:
  7.2 0.9 reduce_sum.135
  8.1 1.5 fusion.48
  9.8 0.8 copy.44.wq_ref
  10.6 0.7 broadcast_in_dim.13.count_ref
  11.3 118.2 %forward_attention.1 = (bf16[3,1408,1024]{2,1,0:T(8,128)(2,1)}, bf16[3,1408,384]{2,1,0:T(8,128)(2,1)}, bf16[3,1408,128]{2,1,0:T(8,128)(2,1)}, f32[3,16,1408]{2,1...) custom-call(f32[3,352,1024]{2,1,0:T(8,128)} %tokens_ref.1, ...), custom_call_target="tpu_custom_call" | custom-call | tf_op jit(solution)/shard_map/forward_attention/pallas_call | solution.py:459
  129.7 2.8 convolution_convert_fusion
  132.6 0.6 collective-permute-start
  133.1 2.5 reduce_sum.142
  135.7 1.5 collective-permute-done
  137.1 5.0 fusion.47
  142.2 0.6 multiply_reduce_fusion.7
  142.8 3.1 copy-done.10
  145.9 8.3 %multiply_convert_fusion = (bf16[3,352,2048]{2,1,0:T(8,128)(2,1)S(1)}, f32[3,352,2048]{2,1,0:T(8,128)}) fusion(bf16[1024,2048]{1,0:T(8,128)(2,1)S(1)} %copy-done.10, f32[3,352,1024]{2,1,0:T(8,128)S(1)} %get-tuple-element.74, f32[1024]{0:T(1024)S(1)} %bitcast.138, f32[3,352]{1,0:T(4,128)S(1)} %add_rsqrt_fusion.1, f32[3,352]{1,0:T(4,128)S(1)} %broadcast_multiply_fusion.5), kind=kOutput, calls=%fused_computation.7 | convolution fusion | flops 4444323840 | bytes 21508352 | tf_op jit(solution)/shard_map/isd,df->isf/dot_general | solution.py:1158
  154.2 6.0 %bitcast_convert_fusion = bf16[2048,1024]{1,0:T(8,128)(2,1)S(1)} fusion(bf16[3,352,2048]{2,1,0:T(8,128)(2,1)S(1)} %get-tuple-element.84, f32[3,352,1024]{2,1,0:T(8,128)S(1)} %bitcast.116, f32[1024]{0:T(1024)S(1)} %bitcast.145), kind=kOutput, calls=%fused_computation.9 | convolution fusion | flops 4433444864 | bytes 12849152 | tf_op jit(solution)/shard_map/dot_general | solution.py:49
  160.3 2.5 copy.45
  162.8 0.6 select_reduce_fusion.slot_blocks
  163.4 20.7 %all-gather.2.cloned.1.call-done = bf16[2048,1024]{1,0:T(8,128)(2,1)} async-done(((bf16[512,1024]{1,0:T(8,128)(2,1)}), bf16[2048,1024]{1,0:T(8,128)(2,1)}) %all-gather.2.cloned.1.call-update) | async-done | bytes 4194320 | tf_op jit(solution)/shard_map/all_gather | solution.py:1134
  184.1 10.8 %fusion.5 = bf16[3,352,2048]{2,1,0:T(8,128)(2,1)S(1)} fusion(f32[3,352,2048]{2,1,0:T(8,128)} %get-tuple-element.85, bf16[2048,1024]{1,0:T(8,128)(2,1)} %all-gather.2.cloned.1.call-done, f32[3,352,1024]{2,1,0:T(8,128)} %param.16, f32[1024]{0:T(1024)S(1)} %bitcast.146), kind=kOutput, calls=%fused_computation.6 | convolution fusion | flops 4452974592 | bytes 21499904 | tf_op jit(solution)/shard_map/isd,fd->isf/dot_general | solution.py:1167
  194.9 4.9 fusion.24
  200.0 7.3 %fusion.27 = bf16[3,352,1024]{2,1,0:T(8,128)(2,1)S(1)} fusion(bf16[3,352,2048]{2,1,0:T(8,128)(2,1)} %copy-done.15, bf16[2048,1024]{1,0:T(8,128)(2,1)S(1)} %copy-done.12), kind=kOutput, calls=%fused_computation.50 | convolution fusion | flops 4430266368 | bytes 10682368 | tf_op jit(solution)/shard_map/isf,fd->isd/dot_general | solution.py:1162
  207.2 0.6 collective-permute-start.1
  207.9 8.0 %bitcast_convert_fusion.1 = bf16[2048,1024]{1,0:T(8,128)(2,1)} fusion(bf16[3,352,2048]{2,1,0:T(8,128)(2,1)S(1)} %copy-done.17, f32[3,352,1024]{2,1,0:T(8,128)S(1)} %bitcast.111, f32[1024]{0:T(1024)S(1)} %bitcast.139, f32[3,352]{1,0:T(4,128)S(1)} %add_rsqrt_fusion.1, f32[3,352]{1,0:T(4,128)S(1)} %broadcast_multiply_fusion.5), kind=kOutput, calls=%fused_computation.10 | convolution fusion | flops 4435607552 | bytes 12857600 | tf_op jit(solution)/shard_map/dot_general | solution.py:49
  215.8 2.0 multiply_reduce_fusion.2
  217.9 6.3 %multiply_reduce_fusion = (f32[1024]{0:T(1024)S(1)}, f32[3,352,1024]{2,1,0:T(8,128)}, f32[1024]{0:T(1024)S(1)}, f32[3,352,1024]{2,1,0:T(8,128)S(1)}) fusion(f32[3,352,1024]{2,1,0:T(8,128)S(1)} %bitcast.118, bf16[3,352,1024]{2,1,0:T(8,128)(2,1)S(1)} %collective-permute-done.1, bf16[3,352,1024]{2,1,0:T(8,128)(2,1)S(1)} %fusion.27, ...), kind=kLoop, calls=%fused_computation.13 | loop fusion | flops 24868864 | bytes 30310912 | tf_op jit(solution)/shard_map/reduce_sum | solution.py:1228
  224.2 4.5 convolution_convert_fusion.1.att_ref
  228.7 2.5 bitcast_convert_fusion.2
  231.2 8.5 %reduce-scatter.2.cloned.1.call-done = bf16[512,1024]{1,0:T(8,128)(2,1)} async-done(((bf16[2048,1024]{1,0:T(8,128)(2,1)}), bf16[512,1024]{1,0:T(8,128)(2,1)}) %reduce-scatter.2.cloned.1.call-update) | async-done | bytes 1048592 | tf_op jit(solution)/shard_map/reduce_scatter | solution.py:1188
  239.8 211.4 %backward_attention.1 = (bf16[3,2,4,4,32,1024]{5,4,3,2,1,0:T(8,128)(2,1)}, bf16[3,352,1536]{2,1,0:T(8,128)(2,1)}, bf16[1024,1536]{1,0:T(8,128)(2,1)}) custom-call(s32[12]{0:T(128)} %select_reduce_fusion.slot_blocks, bf16[3,1408,384]{2,1,0:T(8,128)(2,1)} %get-tuple-element.26.qkv_ref, bf16[3,1408,128]{2,1,0:T(8,128)(2,1)} %get-tuple-element.27.o_ref, ...), custom_call_target="tpu_custom_call" | custom-call | tf_op jit(solution)/shard_map/backward_attention/pallas_call | solution.py:838
  451.1 6.4 %fusion.21 = bf16[3,352,1024]{2,1,0:T(8,128)(2,1)S(1)} fusion(bf16[3,352,1536]{2,1,0:T(8,128)(2,1)} %get-tuple-element.32, bf16[1024,1536]{1,0:T(8,128)(2,1)} %get-tuple-element.33), kind=kOutput, calls=%fused_computation.48 | convolution fusion | flops 3322970112 | bytes 8552448 | tf_op jit(solution)/shard_map/dot_general | solution.py:1213
  457.7 11.1 %multiply_reduce_fusion.8 = (f32[3]{0:T(128)S(1)}, f32[3,128,1024]{2,1,0:T(8,128)}) fusion(f32[3,1024,1024]{2,1,0:T(8,128)} %param.27, bf16[3,1024,1024]{2,1,0:T(8,128)(2,1)} %bitcast.106, f32[3,1,128,1024]{3,2,1,0:T(8,128)} %param.26), kind=kOutput, calls=%fused_computation.60 | convolution fusion | flops 1615331328 | bytes 22020108 | tf_op jit(solution)/shard_map/srb,sbc->src/dot_general | solution.py:1245
  468.8 0.5 collective-permute-start.4
  469.3 2.6 bitcast_convert_fusion.3
  471.9 6.3 %fusion.31 = f32[3,1,128,1024]{3,2,1,0:T(8,128)} fusion(f32[3,1,128,1024]{3,2,1,0:T(8,128)} %param.25, bf16[3,1024,1024]{2,1,0:T(8,128)(2,1)} %bitcast.108, s32[]{:T(128)S(6)} %select_n.12), kind=kOutput, calls=%fused_computation.55 | convolution fusion | flops 806486016 | bytes 10223620 | tf_op jit(solution)/shard_map/sar,sab->srb/dot_general | solution.py:1239
  478.2 3.6 fusion.32
  482.0 3.7 collective-permute-start.5
  485.7 1.5 collective-permute-done.7
  487.3 0.6 collective-permute-done.5
  487.9 1.5 fusion.30
  489.4 4.0 multiply_reduce_fusion.3
  493.5 0.4 collective-permute-start.8
  493.9 3.4 collective-permute-done.8
  497.3 0.4 collective-permute-start.9
  497.7 3.4 collective-permute-done.9
  501.1 2.1 collective-permute-start.12
  503.2 1.8 collective-permute-start.11
  505.0 0.6 collective-permute-start.10
  505.7 4.7 multiply_add_fusion
  510.4 1.4 multiply_subtract_fusion
  (91 shorter events, 1.1 us)
Async XLA Ops:
  7.2 2.4 copy-start
  7.2 176.9 %all-gather.2.cloned.1.call-start = ((), (), s32[]{:S(2)}) async-start(), calls=%async_computation.1 | async-start | bytes 5242880 | tf_op jit(solution)/shard_map/all_gather | solution.py:1134
  129.5 110.3 %reduce-scatter.2.cloned.1.call-start = ((), (), s32[]{:S(2)}) async-start(), calls=%async_computation.2 | async-start | bytes 5242880 | tf_op jit(solution)/shard_map/reduce_scatter | solution.py:1188
  132.6 4.6 collective-permute-start
  142.2 12.0 %copy-start.3 = (f32[3,352,1024]{2,1,0:T(8,128)}, f32[3,352,1024]{2,1,0:T(8,128)S(1)}, u32[]{:S(2)}) copy-start(f32[3,352,1024]{2,1,0:T(8,128)S(1)} %get-tuple-element.74) | copy-start | bytes 12976132
  142.2 3.8 copy-start.10
  142.2 12.0 %slice-start.6 = ((s8[4325376]{0:T(1024)(128)(4,1)}), s8[4194304]{0:T(1024)(128)(4,1)S(1)}, s32[]{:S(2)}) async-start(s8[4325376]{0:T(1024)(128)(4,1)} %bitcast.115), calls=%async_computation.9 | async-start | bytes 8388608
  145.9 8.3 %slice-start.7 = ((s8[4325376]{0:T(1024)(128)(4,1)}), s8[131072]{0:T(1024)(128)(4,1)S(1)}, s32[]{:S(2)}) async-start(s8[4325376]{0:T(1024)(128)(4,1)} %bitcast.115), calls=%async_computation.10 | async-start | bytes 262144
  154.2 6.1 %copy-start.15 = (bf16[3,352,2048]{2,1,0:T(8,128)(2,1)}, bf16[3,352,2048]{2,1,0:T(8,128)(2,1)S(1)}, u32[]{:S(2)}) copy-start(bf16[3,352,2048]{2,1,0:T(8,128)(2,1)S(1)} %get-tuple-element.84) | copy-start | bytes 12976132
  160.3 2.5 copy-start.14
  184.1 10.8 %copy-start.11 = (bf16[1024,2048]{1,0:T(8,128)(2,1)S(1)}, bf16[1024,2048]{1,0:T(8,128)(2,1)}, u32[]{:S(2)}) copy-start(bf16[1024,2048]{1,0:T(8,128)(2,1)} %get-tuple-element.24) | copy-start | bytes 12582916
  194.8 5.0 copy-start.16
  194.9 5.1 copy-start.12
  194.9 12.9 %slice-start.2 = ((s8[4325376]{0:T(1024)(128)(4,1)}), s8[4194304]{0:T(1024)(128)(4,1)S(1)}, s32[]{:S(2)}) async-start(s8[4325376]{0:T(1024)(128)(4,1)} %bitcast.110), calls=%async_computation.5 | async-start | bytes 8388608
  199.8 8.0 %slice-start.3 = ((s8[4325376]{0:T(1024)(128)(4,1)}), s8[131072]{0:T(1024)(128)(4,1)S(1)}, s32[]{:S(2)}) async-start(s8[4325376]{0:T(1024)(128)(4,1)} %bitcast.110), calls=%async_computation.6 | async-start | bytes 262144
  199.9 16.0 %collective-permute-start.2 = (bf16[3,352,1024]{2,1,0:T(8,128)(2,1)S(1)}, bf16[3,352,1024]{2,1,0:T(8,128)(2,1)S(1)}, u32[]{:S(2)}, u32[]{:S(2)}) collective-permute-start(bf16[3,352,1024]{2,1,0:T(8,128)(2,1)S(1)} %fusion.24), channel_id=1, source_target_pairs={{0,1},{1,0},{2,3},{3,2},{4,5},{5,4},{6,7},{7,6},{8,9},{9,8},{10,11... | collective-permute-start | bytes 6488072 | tf_op jit(solution)/shard_map/ppermute | solution.py:907
  199.9 7.9 %copy-start.17 = (bf16[3,352,2048]{2,1,0:T(8,128)(2,1)S(1)}, bf16[3,352,2048]{2,1,0:T(8,128)(2,1)}, u32[]{:S(2)}) copy-start(bf16[3,352,2048]{2,1,0:T(8,128)(2,1)} %copy-done.16) | copy-start | bytes 12976132
  199.9 17.9 %slice-start.8 = ((s8[4325376]{0:T(1024)(128)(4,1)}), s8[4194304]{0:T(1024)(128)(4,1)S(1)}, s32[]{:S(2)}) async-start(s8[4325376]{0:T(1024)(128)(4,1)} %bitcast.117), calls=%async_computation.11 | async-start | bytes 8388608
  207.2 10.6 %collective-permute-start.1 = (bf16[3,352,1024]{2,1,0:T(8,128)(2,1)S(1)}, bf16[3,352,1024]{2,1,0:T(8,128)(2,1)S(1)}, u32[]{:S(2)}, u32[]{:S(2)}) collective-permute-start(bf16[3,352,1024]{2,1,0:T(8,128)(2,1)S(1)} %fusion.27), channel_id=1, source_target_pairs={{0,1},{1,0},{2,3},{3,2},{4,5},{5,4},{6,7},{7,6},{8,9},{9,8},{10,11... | collective-permute-start | bytes 6488072 | tf_op jit(solution)/shard_map/ppermute | solution.py:907
  207.8 10.1 %slice-start.9 = ((s8[4325376]{0:T(1024)(128)(4,1)}), s8[131072]{0:T(1024)(128)(4,1)S(1)}, s32[]{:S(2)}) async-start(s8[4325376]{0:T(1024)(128)(4,1)} %bitcast.117), calls=%async_computation.12 | async-start | bytes 262144
  224.2 4.5 copy-start.4
  224.2 4.5 copy-start.13
  457.6 31.8 %collective-permute-start.3 = (bf16[3,352,1024]{2,1,0:T(8,128)(2,1)S(1)}, bf16[3,352,1024]{2,1,0:T(8,128)(2,1)}, u32[]{:S(2)}, u32[]{:S(2)}) collective-permute-start(bf16[3,352,1024]{2,1,0:T(8,128)(2,1)S(1)} %fusion.21), channel_id=1, source_target_pairs={{0,1},{1,0},{2,3},{3,2},{4,5},{5,4},{6,7},{7,6},{8,9},{9,8},{10,11... | collective-permute-start | bytes 6488072 | tf_op jit(solution)/shard_map/ppermute | solution.py:907
  468.8 13.1 %collective-permute-start.4 = (f32[3]{0:T(128)S(1)}, f32[3]{0:T(128)S(1)}, u32[]{:S(2)}, u32[]{:S(2)}) collective-permute-start(f32[3]{0:T(128)S(1)} %get-tuple-element.86), channel_id=1, source_target_pairs={{0,1},{1,0},{2,3},{3,2},{4,5},{5,4},{6,7},{7,6},{8,9},{9,8},{10,11... | collective-permute-start | bytes 44 | tf_op jit(solution)/shard_map/ppermute | solution.py:907
  469.3 8.9 %copy-start.2 = (bf16[3,2,4,4,32,1024]{5,4,3,2,1,0:T(8,128)(2,1)S(1)}, bf16[3,2,4,4,32,1024]{5,4,3,2,1,0:T(8,128)(2,1)}, u32[]{:S(2)}) copy-start(bf16[3,2,4,4,32,1024]{5,4,3,2,1,0:T(8,128)(2,1)} %get-tuple-element.34) | copy-start | bytes 18874372
  469.3 8.9 %copy-start.6 = (f32[3,1,128,1024]{3,2,1,0:T(8,128)S(1)}, f32[3,1,128,1024]{3,2,1,0:T(8,128)}, u32[]{:S(2)}) copy-start(f32[3,1,128,1024]{3,2,1,0:T(8,128)} %param.24) | copy-start | bytes 4718596
  471.9 17.4 %slice-start = ((s8[4325376]{0:T(1024)(128)(4,1)}), s8[4194304]{0:T(1024)(128)(4,1)S(1)}, s32[]{:S(2)}) async-start(s8[4325376]{0:T(1024)(128)(4,1)} %bitcast.104), calls=%async_computation.3 | async-start | bytes 8388608
  478.2 9.6 %copy-start.5 = (f32[3,128,1024]{2,1,0:T(8,128)S(1)}, f32[3,128,1024]{2,1,0:T(8,128)}, u32[]{:S(2)}) copy-start(f32[3,128,1024]{2,1,0:T(8,128)} %get-tuple-element.87) | copy-start | bytes 4718596
  478.2 9.6 %copy-start.7 = (f32[3,1,128,1024]{3,2,1,0:T(8,128)S(1)}, f32[3,1,128,1024]{3,2,1,0:T(8,128)}, u32[]{:S(2)}) copy-start(f32[3,1,128,1024]{3,2,1,0:T(8,128)} %param.28) | copy-start | bytes 4718596
  478.2 11.1 %slice-start.1 = ((s8[4325376]{0:T(1024)(128)(4,1)}), s8[131072]{0:T(1024)(128)(4,1)S(1)}, s32[]{:S(2)}) async-start(s8[4325376]{0:T(1024)(128)(4,1)} %bitcast.104), calls=%async_computation.4 | async-start | bytes 262144
  481.8 7.5 %copy-start.8 = (f32[1,1024]{1,0:T(1,128)S(1)}, f32[1,1024]{1,0:T(1,128)}, u32[]{:S(2)}) copy-start(f32[1,1024]{1,0:T(1,128)} %get-tuple-element.81.gain_ref) | copy-start | bytes 12292
  481.9 5.4 %collective-permute-start.7 = (f32[3]{0:T(128)S(1)}, f32[3]{0:T(128)S(1)}, u32[]{:S(2)}, u32[]{:S(2)}) collective-permute-start(f32[3]{0:T(128)S(1)} %add.127), channel_id=1, source_target_pairs={{0,8},{8,16},{16,24},{24,0},{1,9},{9,17},{17,25},{25,1},{2,10},{10... | collective-permute-start | bytes 44 | tf_op jit(solution)/shard_map/ppermute | solution.py:943
  481.9 5.3 %collective-permute-start.6 = (f32[3]{0:T(128)S(1)}, f32[3]{0:T(128)S(1)}, u32[]{:S(2)}, u32[]{:S(2)}) collective-permute-start(f32[3]{0:T(128)S(1)} %add.127), channel_id=1, source_target_pairs={{0,16},{8,24},{16,0},{24,8},{1,17},{9,25},{17,1},{25,9},{2,18},{10... | collective-permute-start | bytes 44 | tf_op jit(solution)/shard_map/ppermute | solution.py:943
  482.0 5.8 %collective-permute-start.5 = (f32[3]{0:T(128)S(1)}, f32[3]{0:T(128)S(1)}, u32[]{:S(2)}, u32[]{:S(2)}) collective-permute-start(f32[3]{0:T(128)S(1)} %add.127), channel_id=1, source_target_pairs={{0,24},{8,0},{16,8},{24,16},{1,25},{9,1},{17,9},{25,17},{2,26},{10... | collective-permute-start | bytes 44 | tf_op jit(solution)/shard_map/ppermute | solution.py:943
  487.8 17.8 %slice-start.4 = ((s8[4325376]{0:T(1024)(128)(4,1)}), s8[4194304]{0:T(1024)(128)(4,1)S(1)}, s32[]{:S(2)}) async-start(s8[4325376]{0:T(1024)(128)(4,1)} %bitcast.112), calls=%async_computation.7 | async-start | bytes 8388608
  489.4 16.3 %slice-start.5 = ((s8[4325376]{0:T(1024)(128)(4,1)}), s8[131072]{0:T(1024)(128)(4,1)S(1)}, s32[]{:S(2)}) async-start(s8[4325376]{0:T(1024)(128)(4,1)} %bitcast.112), calls=%async_computation.8 | async-start | bytes 262144
  493.5 3.8 collective-permute-start.8
  497.3 3.8 collective-permute-start.9
  501.1 9.3 %copy-start.9 = (f32[4,64]{1,0:T(4,128)S(1)}, f32[4,64]{1,0:T(4,128)}, u32[]{:S(2)}) copy-start(f32[4,64]{1,0:T(4,128)} %param.29) | copy-start | bytes 3076
  501.1 9.2 %collective-permute-start.12 = (f32[4,1024]{1,0:T(4,128)S(1)}, f32[4,1024]{1,0:T(4,128)S(1)}, u32[]{:S(2)}, u32[]{:S(2)}) collective-permute-start(f32[4,1024]{1,0:T(4,128)S(1)} %fusion.61), channel_id=1, source_target_pairs={{0,8},{8,16},{16,24},{24,0},{1,9},{9,17},{17,25},{25,1},{2,10},{10... | collective-permute-start | bytes 49160 | tf_op jit(solution)/shard_map/ppermute | solution.py:943
  503.2 7.2 %collective-permute-start.11 = (f32[4,1024]{1,0:T(4,128)S(1)}, f32[4,1024]{1,0:T(4,128)S(1)}, u32[]{:S(2)}, u32[]{:S(2)}) collective-permute-start(f32[4,1024]{1,0:T(4,128)S(1)} %fusion.61), channel_id=1, source_target_pairs={{0,16},{8,24},{16,0},{24,8},{1,17},{9,25},{17,1},{25,9},{2,18},{10... | collective-permute-start | bytes 49160 | tf_op jit(solution)/shard_map/ppermute | solution.py:943
  505.0 5.4 %collective-permute-start.10 = (f32[4,1024]{1,0:T(4,128)S(1)}, f32[4,1024]{1,0:T(4,128)S(1)}, u32[]{:S(2)}, u32[]{:S(2)}) collective-permute-start(f32[4,1024]{1,0:T(4,128)S(1)} %fusion.61), channel_id=1, source_target_pairs={{0,24},{8,0},{16,8},{24,16},{1,25},{9,1},{17,9},{25,17},{2,26},{10... | collective-permute-start | bytes 49160 | tf_op jit(solution)/shard_map/ppermute | solution.py:943
  505.7 6.1 %copy-start.1 = (bf16[256,3,512]{2,0,1:T(8,128)(2,1)S(1)}, bf16[256,3,512]{2,0,1:T(8,128)(2,1)}, u32[]{:S(2)}) copy-start(bf16[256,3,512]{2,0,1:T(8,128)(2,1)} %param.18) | copy-start | bytes 2359300
Sparse Core Ops, SparseCore 0:
  129.6 54.4 all-gather.1
  187.0 52.6 reduce-scatter.1

commit v4 on v3

--- a/solution.py
+++ b/solution.py
@@ -318,6 +318,43 @@
         return [local_copy] + [go(src, dst, peer) for peer in z_peers]
 
     cols, hid, depth_o = wout_ref.shape[0] // nc, wup_ref.shape[1] // nc, wout_ref.shape[1]
+
+    def x_piece(i):
+        def at(member, part):
+            rows = span(member * local_len + me_t * half, half)
+            if part is None:
+                return x_all.at[i, rows]
+            return x_all.at[i, rows, pl.ds(part * (D // 2), D // 2)]
+
+        return at
+
+    swaps = [[] for _ in range(images)]
+    near, far = [], []
+
+    def swap(i, member, part=None):
+        piece = x_piece(i)(member, part)
+        swaps[i].append(go(piece, piece, core))
+
+    def normalize(i):
+        local.wait(token_in[i])
+        value = tok[i]
+        centred = value - jnp.mean(value, axis=-1, keepdims=True)
+        inv_std = lax.rsqrt(jnp.mean(centred * centred, axis=-1, keepdims=True) + 1e-06)
+        x_all[i, span(me_c * local_len + me_t * half, half)] = (
+            centred * inv_std * gain_ref[...]
+        ).astype(BF)
+
+    def send_near(i):
+        near.append(spread_plane(go, x_piece(i), me_c))
+        swap(i, me_c)
+
+    def send_far(i):
+        far.append(spread_plane_on(go, x_piece(i), me_c, near[i]))
+        swap(i, me_c ^ 1)
+        swap(i, me_c ^ 2)
+
+    normalize(0)
+    send_near(0)
     out_in = to_line(
         wout_ref.at[span(me_c * cols, cols)],
         out_full.at[span(me_c * cols, cols), span(me_z * depth_o, depth_o)],
@@ -327,41 +364,14 @@
         up_full.at[span(me_z * depth, depth), span(me_c * hid, hid)],
     )
     down_in = to_line(
-        wdown_ref.at[span(me_c * hid, hid)], down_part.at[:, span(me_z * depth_o, depth_o)]
+        wdown_ref.at[span(me_c * hid, hid)],
+        down_part.at[:, span(me_z * depth_o, depth_o)],
     )
-
-    def x_piece(i):
-        def at(member, part):
-            rows = span(member * local_len + me_t * half, half)
-            if part is None:
-                return x_all.at[i, rows]
-            return x_all.at[i, rows, pl.ds(part * (D // 2), D // 2)]
-
-        return at
-
-    swaps = [[] for _ in range(images)]
-
-    def swap(i, member, part=None):
-        piece = x_piece(i)(member, part)
-        swaps[i].append(go(piece, piece, core))
-
-    near = []
-    for i in range(images):
-        local.wait(token_in[i])
-        value = tok[i]
-        centred = value - jnp.mean(value, axis=-1, keepdims=True)
-        inv_std = lax.rsqrt(jnp.mean(centred * centred, axis=-1, keepdims=True) + 1e-06)
-        x_all[i, span(me_c * local_len + me_t * half, half)] = (
-            centred * inv_std * gain_ref[...]
-        ).astype(BF)
-        near.append(spread_plane(go, x_piece(i), me_c))
-        swap(i, me_c)
-    far = []
-    for i in range(images):
-        far.append(spread_plane_on(go, x_piece(i), me_c, near[i]))
-        swap(i, me_c ^ 1)
-        swap(i, me_c ^ 2)
-
+    normalize(1)
+    send_near(1)
+    normalize(2)
+    send_far(0)
+    send_near(2)
     local.wait(wq_own)
     for move in wq_in:
         move.wait_recv()
@@ -405,10 +415,10 @@
             qkv[i, rows] = dot_nn(x_all[i, rows], wq[...]).astype(BF)
 
         local.start(qkv.at[i], qkv_out.at[i])
+        if i == 0:
+            send_far(1)
         bias = jnp.where(place < cnt_out[i : i + 1, 0:1], 0.0, -1e30)
-
-        @pl.loop(0, nc)
-        def _(chunk):
+        def attend(chunk):
             rows = span(chunk * local_len, local_len)
             q = qkv[i, rows, 0:128] * SCALE
             k = qkv[i, :, 128:256]
@@ -425,6 +435,14 @@
             o_all[i, rows] = jnp.where(first, outs[0], outs[1]).astype(BF)
             lse_all[rows] = jnp.where(first, sums[0], sums[1])
 
+        pl.loop(0, nc // 2)(attend)
+        if i == 0:
+            send_far(2)
+            out_near = weight_plane(out_in, out_piece)
+        if i == images - 1:
+            out_far = spread_plane_on(go, out_piece, me_c, out_near)
+        pl.loop(nc // 2, nc)(attend)
+
         mine = att_out.at[i, :, span(me_c * 128, 128)]
         for k in range(1, nc):
             att_in.append(
@@ -437,11 +455,8 @@
             lse_out[i, 8 * head : 8 * head + 8, :] = jnp.broadcast_to(
                 sums_t[HD * head : HD * head + 1], (8, seq)
             )
-        if i == 0:
-            out_near = weight_plane(out_in, out_piece)
-        if i == images - 1:
+        if i == 1:
             up_near = weight_plane(up_in, up_piece)
-            out_far = spread_plane_on(go, out_piece, me_c, out_near)
     up_far = spread_plane_on(go, up_piece, me_c, up_near)
     for move in att_in + out_far + up_far + down_in[1:]:
         move.wait_recv()
@@ -494,7 +509,6 @@
 def backward_kernel(
     nz,
     nc,
-    slot_blocks,
     qkv_ref,
     o_ref,
     lse_ref,
@@ -505,8 +519,9 @@
     down_ref,
     x_ref,
     wq_ref,
-    out_ref,
-    tok_out,
+    early_ref,
+    late_out,
+    heads_out,
     wq_out,
     grad,
     heads,
@@ -523,22 +538,20 @@
     far_in,
     mine_ref,
     zpart_ref,
-    early_ref,
+    zsend_ref,
+    znext_ref,
     late_ref,
     lpart_ref,
-    place_ref,
-    g_ref,
-    l_ref,
+    lsend_ref,
+    lnext_ref,
     send,
     recv,
     local_sems,
 ):
     me_z, me_c, me_t = (lax.axis_index(a) for a in ("fsdp", "context", "tensor"))
     images, local_len = att_ref.shape[:2]
-    slots = out_ref.shape[0]
     x_c, y_c, far_c = me_c ^ 1, me_c ^ 2, me_c ^ 3
-    core, x_near, y_near = {"tensor": 1 - me_t}, {"context": x_c}, {"context": y_c}
-    above, below = {"fsdp": me_z + 1}, {"fsdp": me_z - 1}
+    x_near, y_near = {"context": x_c}, {"context": y_c}
     z_peers = [{"fsdp": lax.rem(me_z + k, nz)} for k in range(1, nz)]
     c_peers = [{"context": me_c ^ k} for k in range(1, nc)]
     left, right = pl.ds(0, D // 2), pl.ds(D // 2, D // 2)
@@ -555,8 +568,11 @@
         own_in.append(local.start(ref.at[block, me_c], own_ref.at[index]))
         far_own.append(local.start(ref.at[block, y_c, :, :, left], far_y.at[index]))
         far_own.append(local.start(ref.at[block, x_c, :, :, right], far_x.at[index]))
-    mine_in = local.start(down_ref.at[:, me_z], mine_ref)
-    greet(z_peers + c_peers + [core])
+    mine_in = [
+        local.start(down_ref.at[:, me_z], mine_ref.at[0]),
+        local.start(down_ref.at[:, me_z ^ 2], mine_ref.at[1]),
+    ]
+    greet(z_peers + c_peers)
     moves = Moves(send, recv)
     sent = []
 
@@ -567,7 +583,8 @@
         return move
 
     grad_in = []
-    for i in range(images):
+
+    def send_grad(i):
         here = grad.at[i, span(me_c * local_len, local_len)]
         grad_in.append(
             [local.start(att_ref.at[i, :, span(me_c * 128, 128)], here)]
@@ -576,8 +593,11 @@
                 for k in range(1, nc)
             ]
         )
+
     near = []
-    for index, (ref, block) in enumerate(terms):
+
+    def send_term(index):
+        ref, block = terms[index]
         near.append(
             [
                 go(ref.at[block, x_c, :, :, left], near_in.at[index, 0], x_near),
@@ -586,21 +606,32 @@
                 go(ref.at[block, far_c, :, :, right], near_in.at[index, 3], y_near),
             ]
         )
-    down_in = [
-        go(
-            down_ref.at[:, lax.rem(me_z + k, nz)],
-            zpart_ref.at[k - 1, pl.ds(len(terms), downs)],
-            z_peers[k - 1],
-        )
-        for k in range(1, nz)
-    ]
+
+    send_grad(0)
+    send_term(0)
+    send_term(1)
+    send_grad(1)
     width = wq_ref.shape[1]
-
-    def wq_piece(member, part):
-        at = span(member * width, width)
-        return wq_out.at[:, at] if part is None else wq_out.at[pl.ds(part * (D // 2), D // 2), at]
-
-    wq_own = local.start(wq_ref, wq_piece(me_c, None))
+    wq_here = wq_out.at[:, span(me_c * width, width)]
+    local.start(wq_ref, wq_here)
+    z_pair, z_next = {"fsdp": me_z ^ 1}, {"fsdp": me_z ^ 2}
+
+    def halve(ref, low, count, at):
+        blocks = pl.ds(low, count)
+        return [
+            go(ref.at[blocks, me_z ^ 1], zpart_ref.at[0, pl.ds(at, count)], z_pair),
+            go(ref.at[blocks, me_z ^ 3], zpart_ref.at[1, pl.ds(at, count)], z_pair),
+        ]
+
+    def halve_on(moves_in, own, count, at):
+        for move in moves_in:
+            move.wait_recv()
+        for block in range(count):
+            zsend_ref[at + block] = own(block) + zpart_ref[1, at + block]
+        blocks = pl.ds(at, count)
+        return go(zsend_ref.at[blocks], znext_ref.at[blocks], z_next)
+
+    down_in = halve(down_ref, 0, downs, len(terms))
     first = lax.broadcasted_iota(jnp.int32, (local_len, 128), 1) < HD
     place = lax.broadcasted_iota(jnp.int32, (local_len, 128), 0)
     weight_ref[...] = jnp.zeros_like(weight_ref)
@@ -616,6 +647,12 @@
         first_far = go(far_y.at[index], far_in.at[index, 0], y_near)
         far_x[index] += near_in[index, 3]
         far_moves.append((first_far, go(far_x.at[index], far_in.at[index, 1], x_near)))
+
+    def sum_end(index):
+        for move in far_moves[index]:
+            move.wait_recv()
+        own_ref[index, :, :, left] += near_in[index, 0] + far_in[index, 0]
+        own_ref[index, :, :, right] += near_in[index, 2] + far_in[index, 1]
 
     for i in range(images):
         for copy in held[i]:
@@ -632,8 +669,7 @@
         dq_ref[...] = jnp.zeros_like(dq_ref)
         real = cnt_ref[i : i + 1, :]
 
-        @pl.loop(0, nc)
-        def _(chunk):
+        def attend(chunk):
             rows = span(chunk * local_len, local_len)
             q = qkv[i, :, 0:128]
             k = qkv[i, rows, 128:256] * SCALE
@@ -655,6 +691,19 @@
             heads[i, rows, 128:256] = jnp.where(first, dks[0], dks[1]).astype(BF)
             heads[i, rows, 256:384] = jnp.where(first, dvs[0], dvs[1]).astype(BF)
 
+        pl.loop(0, nc // 2)(attend)
+        if i == 0:
+            sum_step(0)
+            send_term(2)
+        if i == 1:
+            sum_step(2)
+            send_term(4)
+        if i == 2:
+            sum_step(3)
+            for index in range(3):
+                sum_end(index)
+            group_a = halve(own_ref, 0, 3, 0)
+        pl.loop(nc // 2, nc)(attend)
         heads[i, :, 0:128] = dq_ref[...].astype(BF)
         local.wait(x_in[i])
 
@@ -663,187 +712,74 @@
             rows = span(chunk * local_len, local_len)
             weight_ref[...] += dot_tn(heads[i, rows], x_all[i % 2, rows])
 
+        local.start(heads.at[i], heads_out.at[i])
         if i + 2 < images:
             x_in.append(local.start(x_ref.at[i + 2], x_all.at[i % 2]))
-        if i == 1:
-            for index in range(3):
-                sum_step(index)
+        if i == 0:
+            for copy in mine_in:
+                local.wait(copy)
+            down_next = halve_on(down_in, lambda b: mine_ref[1, b], downs, len(terms))
+            sum_step(1)
+            send_grad(2)
+            send_term(3)
     sub = late_ref.shape[2]
     for z in range(nz):
         for j in range(LATE):
             late_ref[z, j] = weight_ref[pl.ds(j * 128 + z * sub, sub)].astype(BF)
     late_in = [
-        go(late_ref.at[lax.rem(me_z + k, nz)], lpart_ref.at[k - 1], z_peers[k - 1])
-        for k in range(1, nz)
+        go(late_ref.at[me_z ^ 1], lpart_ref.at[0], z_pair),
+        go(late_ref.at[me_z ^ 3], lpart_ref.at[1], z_pair),
     ]
+    sum_step(4)
+    wq_in = [go(wq_ref, wq_here, x_near), go(wq_ref, wq_here, y_near)]
+    next_in = [down_next, halve_on(group_a, lambda b: own_ref[b, me_z ^ 2], 3, 0)]
     for index in range(3, len(terms)):
-        sum_step(index)
-    for index in range(len(terms)):
-        for move in far_moves[index]:
-            move.wait_recv()
-        own_ref[index, :, :, left] += near_in[index, 0] + far_in[index, 0]
-        own_ref[index, :, :, right] += near_in[index, 2] + far_in[index, 1]
-    zterm_in = [
-        go(
-            own_ref.at[:, lax.rem(me_z + k, nz)],
-            zpart_ref.at[k - 1, pl.ds(0, len(terms))],
-            z_peers[k - 1],
-        )
-        for k in range(1, nz)
-    ]
-
-    swapped = []
-
-    def swap(ref, member, z, cond=None, columns=None):
-        piece = ref.at[:, me_t, member, z]
-        if columns is not None:
-            piece = ref.at[:, me_t, member, z, :, columns]
-        swapped.append(go(piece, piece, core, cond=cond, recv_cond=cond))
-
-    def along_fsdp(ref, member):
-        own = ref.at[:, me_t, member, me_z]
-        return [
-            go(own, own, above, cond=me_z < nz - 1, recv_cond=me_z > 0),
-            go(own, own, below, cond=me_z > 0, recv_cond=me_z < nz - 1),
-        ]
-
-    def onward(ref, member, last, hop):
-        up_z, down_z = me_z - hop, me_z + hop
-        last[0].wait_recv()
-        up = down = None
-        if hop < nz - 1:
-            piece = ref.at[:, me_t, member, up_z]
-            cond = jnp.logical_and(me_z < nz - 1, up_z >= 0)
-            up = go(piece, piece, above, cond=cond, recv_cond=up_z - 1 >= 0)
-        last[1].wait_recv()
-        if hop < nz - 1:
-            piece = ref.at[:, me_t, member, down_z]
-            cond = jnp.logical_and(me_z > 0, down_z <= nz - 1)
-            down = go(piece, piece, below, cond=cond, recv_cond=down_z + 1 <= nz - 1)
-        return [up, down], [(up_z, up_z >= 0), (down_z, down_z <= nz - 1)]
-
-    total = late_ref[me_z].astype(F32)
-    for k in range(1, nz):
-        late_in[k - 1].wait_recv()
-        total = total + lpart_ref[k - 1].astype(F32)
-    l_ref[:, me_t, me_c, me_z] = total.astype(BF)
-    late_line = along_fsdp(l_ref, me_c)
-    near = []
-
-    def spread(z, cond=None):
-        piece = l_ref.at[:, me_t, me_c, z]
-        near.append(
-            (
-                z,
-                cond,
-                go(piece, piece, x_near, cond=cond, recv_cond=cond),
-                go(piece, piece, y_near, cond=cond, recv_cond=cond),
-            )
-        )
-        swap(l_ref, me_c, z, cond)
-
-    for move in down_in + zterm_in:
+        sum_end(index)
+    group_b = halve(own_ref, 3, len(terms) - 3, 3)
+    for move in late_in:
         move.wait_recv()
-    local.wait(mine_in)
+    lsend_ref[...] = late_ref[me_z ^ 2] + lpart_ref[1]
+    late_next = go(lsend_ref, lnext_ref, z_next)
+    next_in.append(
+        halve_on(group_b, lambda b: own_ref[3 + b, me_z ^ 2], len(terms) - 3, 3)
+    )
+    late_next.wait_recv()
+    total = late_ref[me_z].astype(F32) + lpart_ref[0].astype(F32) + lnext_ref[...].astype(F32)
+    late_out[...] = total.astype(BF)
+    for move in next_in:
+        move.wait_recv()
     for block in range(EARLY):
         if block < len(terms):
             total = own_ref[block, me_z].astype(F32)
         else:
-            total = mine_ref[block - len(terms)].astype(F32)
-        for k in range(1, nz):
-            total = total + zpart_ref[k - 1, block].astype(F32)
+            total = mine_ref[0, block - len(terms)].astype(F32)
+        total = total + zpart_ref[0, block].astype(F32) + znext_ref[block].astype(F32)
         early_ref[block] = total.astype(BF)
-    for slot in range(NBLK):
-        block = jnp.clip(slot_blocks[slot] - LATE, 0, EARLY - 1)
-        place_ref[slot] = early_ref[block]
-    placed = []
-    for k in range(1, nc):
-        theirs = place_ref.at[pl.ds((me_c ^ k) * slots, slots)]
-        placed.append(go(theirs, g_ref.at[:, me_t, me_c, me_z], c_peers[k - 1]))
-    for slot in range(slots):
-        g_ref[slot, me_t, me_c, me_z] = place_ref[me_c * slots + slot]
-    lines = {}
-    for k in range(nc):
-        member = me_c ^ k
-        if k > 0:
-            placed[k - 1].wait_recv()
-        lines[k] = along_fsdp(g_ref, member)
-        swap(g_ref, member, me_z)
-    tok_in = []
-    for i in range(images):
-        there = tok_out.at[i, :, span(me_c * 384, 384)]
-        for k in range(1, nc):
-            tok_in.append(
-                go(heads.at[i, span((me_c ^ k) * local_len, local_len)], there, c_peers[k - 1])
-            )
-        local.start(heads.at[i, span(me_c * local_len, local_len)], there)
-    spread(me_z)
-    local.wait(wq_own)
-    wq_near = spread_plane(go, wq_piece, me_c)
-    far = []
-    done = 0
-
-    def spread_on():
-        nonlocal done
-        for z, cond, x_move, y_move in near[done:]:
-            x_move.wait_recv()
-            piece = l_ref.at[:, me_t, x_c, z, :, left]
-            far.append((z, cond, left, go(piece, piece, y_near, cond=cond, recv_cond=cond)))
-            swap(l_ref, x_c, z, cond)
-            y_move.wait_recv()
-            piece = l_ref.at[:, me_t, y_c, z, :, right]
-            far.append((z, cond, right, go(piece, piece, x_near, cond=cond, recv_cond=cond)))
-            swap(l_ref, y_c, z, cond)
-        done = len(near)
-
-    for hop in range(1, nz):
-        late_line, here = onward(l_ref, me_c, late_line, hop)
-        for z, cond in here:
-            spread(z, cond)
-        for k in range(nc):
-            member = me_c ^ k
-            lines[k], here = onward(g_ref, member, lines[k], hop)
-            for z, cond in here:
-                swap(g_ref, member, z, cond)
-        spread_on()
-    wq_far = spread_plane_on(go, wq_piece, me_c, wq_near)
-    for z, cond, columns, move in far:
+    for move in wq_in:
         move.wait_recv()
-        swap(l_ref, far_c, z, cond, columns)
-    for move in swapped:
-        move.wait_recv()
-    for move in tok_in + wq_far:
-        move.wait_recv()
+    local.finish()
     for move in sent:
         move.wait_send()
-    for slot in range(slots):
-        block = slot_blocks[me_c * slots + slot]
-        late = l_ref[jnp.clip(block, 0, LATE - 1)]
-        g_ref[slot] = jnp.where(block < LATE, late, g_ref[slot])
-        local.start(g_ref.at[slot], out_ref.at[slot])
-    local.finish()
 
 
 def backward_attention(
-    block_of, qkv, o_heads, lse, grad_att, counts, term_out, term_up, down, x_all, wq, nz, nc, nt
+    qkv, o_heads, lse, grad_att, counts, term_out, term_up, down, x_all, wq, nz, nc
 ):
     images, seq = qkv.shape[:2]
     local_len = seq // nc
     sub = term_up.shape[3]
-    slots = NBLK // nc
     terms = 1 + term_up.shape[0]
     any_ = pl.BlockSpec(memory_space=pl.ANY)
     vmem = pl.BlockSpec(memory_space=pltpu.VMEM)
-    shape = (slots, nt, nc, nz, sub, D)
-    out, tok, wq_all = pl.pallas_call(
+    return pl.pallas_call(
         functools.partial(backward_kernel, nz, nc),
         out_shape=(
-            jax.ShapeDtypeStruct(shape, BF),
-            jax.ShapeDtypeStruct((images, local_len, nc * 384), BF),
+            jax.ShapeDtypeStruct((EARLY, sub, D), BF),
+            jax.ShapeDtypeStruct((LATE, sub, D), BF),
+            jax.ShapeDtypeStruct((images, seq, 384), BF),
             jax.ShapeDtypeStruct((D, nc * 384), BF),
         ),
         in_specs=[
-            pl.BlockSpec(memory_space=pltpu.SMEM),
             any_,
             any_,
             vmem,
@@ -855,7 +791,7 @@
             any_,
             any_,
         ],
-        out_specs=(any_, any_, any_),
+        out_specs=(vmem, vmem, any_, any_),
         scratch_shapes=[
             pltpu.VMEM((images, seq, 128), BF),
             pltpu.VMEM((images, seq, 384), BF),
@@ -870,14 +806,14 @@
             pltpu.VMEM((terms, nz, sub, D // 2), BF),
             pltpu.VMEM((terms, 4, nz, sub, D // 2), BF),
             pltpu.VMEM((terms, 2, nz, sub, D // 2), BF),
-            pltpu.VMEM((EARLY - terms, sub, D), BF),
-            pltpu.VMEM((nz - 1, EARLY, sub, D), BF),
+            pltpu.VMEM((2, EARLY - terms, sub, D), BF),
+            pltpu.VMEM((2, EARLY, sub, D), BF),
+            pltpu.VMEM((EARLY, sub, D), BF),
             pltpu.VMEM((EARLY, sub, D), BF),
             pltpu.VMEM((nz, LATE, sub, D), BF),
-            pltpu.VMEM((nz - 1, LATE, sub, D), BF),
-            pltpu.VMEM((NBLK, sub, D), BF),
-            pltpu.VMEM(shape, BF),
-            pltpu.VMEM((LATE, nt, nc, nz, sub, D), BF),
+            pltpu.VMEM((2, LATE, sub, D), BF),
+            pltpu.VMEM((LATE, sub, D), BF),
+            pltpu.VMEM((LATE, sub, D), BF),
             pltpu.SemaphoreType.DMA((256,)),
             pltpu.SemaphoreType.DMA((256,)),
             pltpu.SemaphoreType.DMA((64,)),
@@ -887,7 +823,6 @@
         ),
         name="backward_attention",
     )(
-        block_of,
         qkv,
         o_heads,
         lse,
@@ -899,7 +834,409 @@
         x_all,
         wq,
     )
-    return out.reshape(slots, D, D), tok, wq_all
+
+
+def tail_kernel(
+    nz,
+    nc,
+    token_count,
+    slot_blocks,
+    early_ref,
+    late_ref,
+    heads_ref,
+    wq_ref,
+    tokens_ref,
+    mid_ref,
+    gain_ref,
+    gains_ref,
+    rl_ref,
+    rr_ref,
+    sl_ref,
+    sr_ref,
+    ms_ref,
+    tokens_out,
+    gain_out,
+    grad_out,
+    left_out,
+    right_out,
+    weight_out,
+    tok,
+    wq,
+    x_buf,
+    mid_buf,
+    part,
+    part_in,
+    rl,
+    rr,
+    sl,
+    sr,
+    ms,
+    update,
+    square,
+    square_in,
+    gain_sum,
+    gain_in,
+    place_ref,
+    g_ref,
+    l_ref,
+    g_all,
+    send,
+    recv,
+    local_sems,
+):
+    me_z, me_c, me_t = (lax.axis_index(a) for a in ("fsdp", "context", "tensor"))
+    images, local_len = tokens_ref.shape[:2]
+    slots = g_ref.shape[0]
+    x_c, y_c, far_c = me_c ^ 1, me_c ^ 2, me_c ^ 3
+    core, x_near, y_near = {"tensor": 1 - me_t}, {"context": x_c}, {"context": y_c}
+    above, below = {"fsdp": me_z + 1}, {"fsdp": me_z - 1}
+    c_peers = [{"context": me_c ^ k} for k in range(1, nc)]
+    group = [
+        {"fsdp": me_z ^ (k // 2), "tensor": me_t ^ (k % 2)} for k in range(1, 2 * nz)
+    ]
+    rows_group = [(me_z ^ (k // nc), me_c ^ (k % nc)) for k in range(1, nz * nc)]
+    others = [{"fsdp": z, "context": c} for z, c in rows_group[nc - 1 :] ]
+    diagonal = [d for k, d in enumerate(others) if (k + nc) % nc]
+    left, right = pl.ds(0, D // 2), pl.ds(D // 2, D // 2)
+    local = Local(local_sems)
+    width = wq.shape[1] // nc
+    wq_in = [
+        local.start(wq_ref.at[:, span(m * width, width)], wq.at[:, span(m * width, width)])
+        for m in (me_c, x_c, y_c)
+    ]
+    x_in = [local.start(tokens_ref.at[i], x_buf.at[i]) for i in range(images)]
+    mid_in = [local.start(mid_ref.at[i], mid_buf.at[i]) for i in range(images)]
+    state_in = [
+        local.start(a, b) for a, b in ((rl_ref, rl), (sl_ref, sl), (sr_ref, sr), (ms_ref, ms))
+    ]
+    rr_in = [local.start(rr_ref.at[0], rr)]
+    for slot in range(NBLK):
+        block = jnp.clip(slot_blocks[slot] - LATE, 0, EARLY - 1)
+        place_ref[slot] = early_ref[block]
+    l_ref[:, me_t, me_c, me_z] = late_ref[...]
+    for slot in range(slots):
+        g_ref[slot, me_t, me_c, me_z] = place_ref[me_c * slots + slot]
+    greet(group + c_peers + diagonal)
+    moves = Moves(send, recv)
+    sent = []
+
+    def go(*args, **kw):
+        move = moves.make(*args, **kw)
+        move.start()
+        sent.append(move)
+        return move
+
+    placed = []
+    for k in range(1, nc):
+        theirs = place_ref.at[pl.ds((me_c ^ k) * slots, slots)]
+        placed.append(go(theirs, g_ref.at[:, me_t, me_c, me_z], c_peers[k - 1]))
+
+    swapped = []
+
+    def swap(piece, cond=None):
+        swapped.append(go(piece, piece, core, cond=cond, recv_cond=cond))
+
+    def along_fsdp(at):
+        own = at(me_z)
+        return [
+            go(own, own, above, cond=me_z < nz - 1, recv_cond=me_z > 0),
+            go(own, own, below, cond=me_z > 0, recv_cond=me_z < nz - 1),
+        ]
+
+    def onward(at, last, hop):
+        up_z, down_z = me_z - hop, me_z + hop
+        last[0].wait_recv()
+        up = down = None
+        if hop < nz - 1:
+            piece = at(up_z)
+            cond = jnp.logical_and(me_z < nz - 1, up_z >= 0)
+            up = go(piece, piece, above, cond=cond, recv_cond=up_z - 1 >= 0)
+        last[1].wait_recv()
+        if hop < nz - 1:
+            piece = at(down_z)
+            cond = jnp.logical_and(me_z > 0, down_z <= nz - 1)
+            down = go(piece, piece, below, cond=cond, recv_cond=down_z + 1 <= nz - 1)
+        return [up, down], [(up_z, up_z >= 0), (down_z, down_z <= nz - 1)]
+
+    def late_at(member):
+        return lambda z: l_ref.at[:, me_t, member, z]
+
+    def slot_at(slot):
+        return lambda z: g_ref.at[slot, me_t, :, z]
+
+    late_line = along_fsdp(late_at(me_c))
+    near, far = [], []
+
+    def spread(z, cond=None):
+        piece = late_at(me_c)(z)
+        near.append(
+            (
+                z,
+                cond,
+                go(piece, piece, x_near, cond=cond, recv_cond=cond),
+                go(piece, piece, y_near, cond=cond, recv_cond=cond),
+            )
+        )
+        swap(piece, cond)
+
+    def spread_on(entry):
+        z, cond, x_move, y_move = entry
+        x_move.wait_recv()
+        piece = l_ref.at[:, me_t, x_c, z, :, left]
+        first = go(piece, piece, y_near, cond=cond, recv_cond=cond)
+        swap(late_at(x_c)(z), cond)
+        y_move.wait_recv()
+        piece = l_ref.at[:, me_t, y_c, z, :, right]
+        second = go(piece, piece, x_near, cond=cond, recv_cond=cond)
+        swap(late_at(y_c)(z), cond)
+        far.append((z, cond, left, first))
+        far.append((z, cond, right, second))
+
+    spread(me_z)
+    tok_in = []
+
+    def send_tok(i):
+        there = tok.at[i, :, span(me_c * 384, 384)]
+        tok_in.append(
+            [local.start(heads_ref.at[i, span(me_c * local_len, local_len)], there)]
+            + [
+                go(
+                    heads_ref.at[i, span((me_c ^ k) * local_len, local_len)],
+                    there,
+                    c_peers[k - 1],
+                )
+                for k in range(1, nc)
+            ]
+        )
+    lines = []
+
+    def slot_line(slot):
+        lines.append(along_fsdp(slot_at(slot)))
+        swap(slot_at(slot)(me_z))
+
+    def late_on(hop):
+        nonlocal late_line
+        late_line, here = onward(late_at(me_c), late_line, hop)
+        for z, cond in here:
+            spread(z, cond)
+
+    half_rows = D // 2
+    for copy in wq_in[1:]:
+        local.wait(copy)
+    late_on(1)
+    for move in placed:
+        move.wait_recv()
+    slot_line(0)
+    spread_on(near[0])
+    late_on(2)
+    slot_line(1)
+    slot_line(2)
+    for entry in near[1:3]:
+        spread_on(entry)
+    send_tok(0)
+    late_on(3)
+    for entry in near[3:5]:
+        spread_on(entry)
+    x_rows = wq.at[pl.ds(0, half_rows), span(x_c * width, width)]
+    y_rows = wq.at[pl.ds(half_rows, half_rows), span(y_c * width, width)]
+    wq_far = [go(x_rows, x_rows, y_near), go(y_rows, y_rows, x_near)]
+
+    part_moves = []
+    gain_out[...] = jnp.zeros_like(gain_out)
+    square[...] = jnp.zeros_like(square)
+
+    def project(i):
+        local.wait(tok_in[i][0])
+        for move in tok_in[i][1:]:
+            move.wait_recv()
+        part[i] = dot_nt(tok[i], wq[...]).astype(BF)
+        part_moves.append(go(part.at[i], part_in.at[i], core))
+
+    def norm_backward(i):
+        part_moves[i].wait_recv()
+        local.wait(x_in[i])
+        local.wait(mid_in[i])
+
+        @pl.loop(0, 2)
+        def _(step):
+            rows = span(step * (local_len // 2), local_len // 2)
+            value = x_buf[i, rows]
+            centred = value - jnp.mean(value, axis=-1, keepdims=True)
+            inv_std = lax.rsqrt(jnp.mean(centred * centred, axis=-1, keepdims=True) + 1e-06)
+            normed = centred * inv_std
+            grad = part[i, rows].astype(F32) + part_in[i, rows].astype(F32)
+            scaled = grad * gain_ref[...]
+            inner = (
+                scaled
+                - jnp.mean(scaled, axis=-1, keepdims=True)
+                - normed * jnp.mean(scaled * normed, axis=-1, keepdims=True)
+            )
+            mid_buf[i, rows] += inner * inv_std
+            gain_out[0:1, :] += jnp.sum(grad * normed, axis=0, keepdims=True)
+
+        local.start(mid_buf.at[i], tokens_out.at[i])
+
+    def slots_on(hop):
+        for slot in range(slots):
+            lines[slot], here = onward(slot_at(slot), lines[slot], hop)
+            for z, cond in here:
+                swap(slot_at(slot)(z), cond)
+
+    slots_on(1)
+    for entry in near[5:]:
+        spread_on(entry)
+    for i in range(1, images):
+        send_tok(i)
+    for z, cond, columns, move in far:
+        move.wait_recv()
+        swap(l_ref.at[:, me_t, far_c, z, :, columns], cond)
+    local.wait(wq_in[0])
+    for move in wq_far:
+        move.wait_recv()
+    project(0)
+    slots_on(2)
+    for i in range(1, images):
+        project(i)
+    for i in range(images):
+        norm_backward(i)
+    gain_sum[...] = gains_ref[...]
+    gain_sum[0:1, :] = gain_out[0:1, :]
+    gain_moves = []
+    for k, (z, c) in enumerate(rows_group):
+        theirs = span((z * nc + c) // 2 * 128, 128)
+        gain_moves.append(
+            go(gain_sum.at[:, theirs], gain_in.at[k], {"fsdp": z, "context": c})
+        )
+    slots_on(3)
+    for move in swapped:
+        move.wait_recv()
+    for copy in state_in:
+        local.wait(copy)
+    offset = me_t * (D // 2) + me_z * rl.shape[1]
+    mine = span(offset, rl.shape[1])
+    for slot in range(slots):
+        block = slot_blocks[me_c * slots + slot]
+        late = l_ref[jnp.clip(block, 0, LATE - 1)]
+        g_all[...] = jnp.where(block < LATE, late, g_ref[slot]).reshape(D, D)
+        rows = g_all[mine, :]
+        grad_out[slot] = rows.astype(F32)
+        left_out[slot] = 0.5 * sl[slot] + 0.5 / token_count * dot_nt(rows, g_all[...])
+        right_out[slot] = 0.5 * sr[slot] + 0.5 / token_count * dot_tn(g_all[:, mine], g_all[...])
+        inner = dot_nn(rl[slot].astype(BF), g_all[...]).astype(BF)
+        local.wait(rr_in[slot])
+        update[slot] = dot_nn(inner, rr[...].astype(BF))
+        if slot + 1 < slots:
+            rr_in.append(local.start(rr_ref.at[slot + 1], rr))
+        total = jnp.sum(update[slot] * update[slot], axis=0, keepdims=True)
+        total = jnp.sum(total, axis=1, keepdims=True)
+        square[slot : slot + 1, :] = jnp.broadcast_to(total, (1, 128))
+    square_moves = [
+        go(square, square_in.at[k], group[k]) for k in range(len(group))
+    ]
+    for move in square_moves:
+        move.wait_recv()
+    for slot in range(slots):
+        total = square[slot : slot + 1, 0:1]
+        for k in range(len(group)):
+            total = total + square_in[k, slot : slot + 1, 0:1]
+        weight_out[slot] = ms[slot] - lax.rsqrt(total / (D * D) + 1e-06) * update[slot]
+    total = gain_sum[:, span((me_z * nc + me_c) // 2 * 128, 128)]
+    for k, move in enumerate(gain_moves):
+        move.wait_recv()
+        total = total + gain_in[k]
+    gain_out[:, 0:128] = total
+    local.finish()
+    for move in sent:
+        move.wait_send()
+
+
+def tail(
+    block_of,
+    early,
+    late,
+    grad_heads,
+    wq_all,
+    tokens,
+    grad_middle,
+    gain,
+    gain_terms,
+    root_left,
+    root_right,
+    stat_left,
+    stat_right,
+    master,
+    token_count,
+    nz,
+    nc,
+    nt,
+):
+    images, local_len = tokens.shape[:2]
+    sub = early.shape[1]
+    slots, row_count = root_left.shape[:2]
+    any_ = pl.BlockSpec(memory_space=pl.ANY)
+    vmem = pl.BlockSpec(memory_space=pltpu.VMEM)
+    state = jax.ShapeDtypeStruct((slots, row_count, D), F32)
+    shape = (slots, nt, nc, nz, sub, D)
+    return pl.pallas_call(
+        functools.partial(tail_kernel, nz, nc, token_count),
+        out_shape=(
+            jax.ShapeDtypeStruct((images, local_len, D), F32),
+            jax.ShapeDtypeStruct((8, D), F32),
+            state,
+            state,
+            state,
+            state,
+        ),
+        in_specs=[pl.BlockSpec(memory_space=pltpu.SMEM), vmem, vmem]
+        + [any_] * 4
+        + [vmem, vmem]
+        + [any_] * 5,
+        out_specs=(any_, vmem, vmem, vmem, vmem, vmem),
+        scratch_shapes=[
+            pltpu.VMEM((images, local_len, nc * 384), BF),
+            pltpu.VMEM((D, nc * 384), BF),
+            pltpu.VMEM((images, local_len, D), F32),
+            pltpu.VMEM((images, local_len, D), F32),
+            pltpu.VMEM((images, local_len, D), BF),
+            pltpu.VMEM((images, local_len, D), BF),
+            pltpu.VMEM((slots, row_count, D), F32),
+            pltpu.VMEM((D, D), F32),
+            pltpu.VMEM((slots, row_count, D), F32),
+            pltpu.VMEM((slots, row_count, D), F32),
+            pltpu.VMEM((slots, row_count, D), F32),
+            pltpu.VMEM((slots, row_count, D), F32),
+            pltpu.VMEM((8, 128), F32),
+            pltpu.VMEM((2 * nz - 1, 8, 128), F32),
+            pltpu.VMEM((8, D), F32),
+            pltpu.VMEM((nz * nc - 1, 8, 128), F32),
+            pltpu.VMEM((NBLK, sub, D), BF),
+            pltpu.VMEM(shape, BF),
+            pltpu.VMEM((LATE, nt, nc, nz, sub, D), BF),
+            pltpu.VMEM((D, D), BF),
+            pltpu.SemaphoreType.DMA((160,)),
+            pltpu.SemaphoreType.DMA((160,)),
+            pltpu.SemaphoreType.DMA((32,)),
+        ],
+        compiler_params=pltpu.CompilerParams(
+            collective_id=3, has_side_effects=True, vmem_limit_bytes=61 << 20
+        ),
+        name="tail",
+    )(
+        block_of,
+        early,
+        late,
+        grad_heads,
+        wq_all,
+        tokens,
+        grad_middle,
+        gain,
+        gain_terms,
+        root_left,
+        root_right,
+        stat_left,
+        stat_right,
+        master,
+    )
 
 
 def xor_permute(value, axis, step):
@@ -1112,7 +1449,7 @@
     hidden = w_up.shape[1]
     up_blocks = hidden // half_width
     cols = half_width // nc
-    fast = nz == 4 and nc == 4
+    fast = nz == 4 and nc == 4 and nt == 2 and images == 3
     if fast:
         wq_part = lax.dynamic_slice_in_dim(w_qkv, me_c * cols, cols, 2).reshape(-1, 3 * cols)
         counts = jnp.pad(jnp.sum(key_mask, axis=1), (0, 8 - images))
@@ -1192,27 +1529,34 @@
     term_out = early_term(attended, grad_branch)
     term_up = early_term(grad_pre, normed2_low)
     down = early_sum(early_term(act_low, grad_mlp))
+    tokens_all = images * nz * SEQ
+    grad_gain3 = jnp.sum(grad_middle * branch_attn, axis=(0, 1))
+    grad_gain4 = jnp.sum(cotangent * branch_mlp, axis=(0, 1))
+    blank = jnp.zeros_like(grad_gain2)
+    gain_terms = jnp.stack([blank, grad_gain2, grad_gain3, grad_gain4] + [blank] * 4, axis=0)
     if fast:
-        grad_full, grad_tok, wq_all = backward_attention(
+        early, late, grad_heads, wq_all = backward_attention(
+            qkv, out_heads, log_sums, grad_att, counts, term_out, term_up, down, x_all, wq, nz, nc
+        )
+        grad_tokens, gain_sum, grad_mine, left_new, right_new, weight_new = tail(
             block_of,
-            qkv,
-            out_heads,
-            log_sums,
-            grad_att,
-            counts,
-            term_out,
-            term_up,
-            down,
-            x_all,
-            wq,
+            early,
+            late,
+            grad_heads,
+            wq_all,
+            tokens,
+            grad_middle,
+            gains[0:1],
+            gain_terms,
+            root_left[:, 0],
+            root_right,
+            stat_left[:, 0],
+            stat_right[:, 0],
+            master[:, 0],
+            tokens_all,
             nz,
             nc,
             nt,
-        )
-        grad_n1 = sum_tensor(
-            lax.dot_general(
-                grad_tok, wq_all, (((2,), (1,)), ((), ())), preferred_element_type=F32
-            )
         )
     else:
         early = jnp.concatenate([early_sum(term_out), early_sum(term_up), down], axis=0)
@@ -1222,43 +1566,46 @@
         term_qkv = jnp.einsum("isk,isd->kd", grad_heads, x_all, preferred_element_type=F32)
         late = jnp.swapaxes(term_qkv.astype(BF).reshape(LATE, nz, sub, D), 0, 1)
         grad_full = grad_gather_plain(block_of, early, late, nz, nc)
-    input_part, grad_gain1 = norm_back(grad_n1, gains[0], normed1, inv_std1)
-    grad_tokens = grad_middle + input_part
-    grad_gain3 = jnp.sum(grad_middle * branch_attn, axis=(0, 1))
-    grad_gain4 = jnp.sum(cotangent * branch_mlp, axis=(0, 1))
-    gain_terms = jnp.stack([grad_gain1, grad_gain2, grad_gain3, grad_gain4], axis=0)
-
-    row_count = half_width // nz
-    row_offset = me_t * half_width + me_z * row_count
-    tokens_all = images * nz * SEQ
-    grad_mine = lax.dynamic_slice_in_dim(grad_full, row_offset, row_count, 1)
-    left_new = 0.5 * stat_left[:, 0] + 0.5 / tokens_all * jnp.einsum(
-        "sra,sba->srb", grad_mine, grad_full, preferred_element_type=F32
-    )
-    grad_cols = lax.dynamic_slice_in_dim(grad_full, row_offset, row_count, 2)
-    right_new = 0.5 * stat_right[:, 0] + 0.5 / tokens_all * jnp.einsum(
-        "sar,sab->srb", grad_cols, grad_full, preferred_element_type=F32
-    )
-    inner_prod = jnp.einsum(
-        "sra,sab->srb", root_left[:, 0].astype(BF), grad_full, preferred_element_type=F32
-    ).astype(BF)
-    update = jnp.einsum(
-        "srb,sbc->src", inner_prod, root_right.astype(BF), preferred_element_type=F32
-    )
-    square_sum = jnp.sum(update * update, axis=(1, 2))
-    square_sum = sum_fsdp(square_sum + xor_permute(square_sum, "tensor", 1))
-    factor = lax.rsqrt(square_sum / (D * D) + 1e-06)
-    weight_new = master[:, 0] - factor[:, None, None] * update
-
-    gain_sum = gain_terms
-    step = 1
-    while step < nc:
-        gain_sum = gain_sum + xor_permute(gain_sum, "context", step)
-        step *= 2
-    gain_sum = sum_fsdp(gain_sum)
+        input_part, grad_gain1 = norm_back(grad_n1, gains[0], normed1, inv_std1)
+        grad_tokens = grad_middle + input_part
+        row_count = half_width // nz
+        row_offset = me_t * half_width + me_z * row_count
+        grad_mine = lax.dynamic_slice_in_dim(grad_full, row_offset, row_count, 1)
+        left_new = 0.5 * stat_left[:, 0] + 0.5 / tokens_all * jnp.einsum(
+            "sra,sba->srb", grad_mine, grad_full, preferred_element_type=F32
+        )
+        grad_cols = lax.dynamic_slice_in_dim(grad_full, row_offset, row_count, 2)
+        right_new = 0.5 * stat_right[:, 0] + 0.5 / tokens_all * jnp.einsum(
+            "sar,sab->srb", grad_cols, grad_full, preferred_element_type=F32
+        )
+        inner_prod = jnp.einsum(
+            "sra,sab->srb", root_left[:, 0].astype(BF), grad_full, preferred_element_type=F32
+        ).astype(BF)
+        update = jnp.einsum(
+            "srb,sbc->src", inner_prod, root_right.astype(BF), preferred_element_type=F32
+        )
+        square_sum = jnp.sum(update * update, axis=(1, 2))
+        square_sum = sum_fsdp(square_sum + xor_permute(square_sum, "tensor", 1))
+        factor = lax.rsqrt(square_sum / (D * D) + 1e-06)
+        weight_new = master[:, 0] - factor[:, None, None] * update
+
+        gain_terms = gain_terms[:4].at[0].set(grad_gain1)
+        gain_sum = gain_terms
+        step = 1
+        while step < nc:
+            gain_sum = gain_sum + xor_permute(gain_sum, "context", step)
+            step *= 2
+        gain_sum = sum_fsdp(gain_sum)
+
     share_width = gain_state.shape[1]
     gain_index = lax.axis_index(("fsdp", "context"))
-    gain_grad = lax.dynamic_slice_in_dim(gain_sum, gain_index * share_width, share_width, 1)
+    if fast:
+        at = lax.rem(gain_index * share_width, 128)
+        gain_grad = lax.dynamic_slice(gain_sum, (0, at), (4, share_width))
+    else:
+        gain_grad = lax.dynamic_slice_in_dim(
+            gain_sum, gain_index * share_width, share_width, 1
+        )
     gain_mine = lax.dynamic_slice_in_dim(gains, gain_index * share_width, share_width, 1)
     state_new = 0.5 * gain_state + 0.5 * gain_grad * gain_grad / tokens_all
     gain_new = gain_mine - 0.1 * gain_grad * lax.rsqrt(tokens_all * state_new)

time: 526 us -> 466 us (0.89)
  Pallas kernels: 330 us -> 307 us
  matrix products: 82.6 us -> 60.9 us
  other arithmetic: 32.2 us -> 20.6 us
  starting transfers between devices: 11.3 us -> 0.94 us
  local copies, waits for them, and re-layouts: 8.86 us -> 19.2 us
  waiting for transfers between devices: 39.6 us -> 33.3 us
    pallas_call x1, Pallas kernels: 211 us -> 92.5 us  [backward_attention(): pl.pallas_call(functools.partial(backward_kernel, nz, nc), out_shape=(jax...]
    pallas_call x0 -> x1, Pallas kernels: none -> 108 us  [tail(): pl.pallas_call(functools.partial(tail_kernel, nz, nc, token_count), out_s...]
    dot_general x4 -> x0, matrix products: 27.5 us -> none  [the longest x1 11.1 us: per_device(): jnp.einsum('srb,sbc->src', inner_prod, root_right.astype(BF), preferred_e...]
    pallas_call x1, Pallas kernels: 118 us -> 106 us  [forward_attention(): pl.pallas_call(functools.partial(forward_kernel, nz, nc), out_shape=(jax....]
    unnamed x57 -> x50, local copies, waits for them, and re-layouts: 3.41 us -> 13.1 us
    reduce_scatter x1, waiting for transfers between devices: 8.55 us -> 0.01 us  [early_sum(): lax.psum_scatter(jnp.swapaxes(term, 0, 1).reshape(-1, D), 'context', scat...]
    all_gather x1, waiting for transfers between devices: 20.7 us -> 29.1 us  [per_device(): down_full = lax.all_gather(down_part, 'context', axis=0, tiled=True)]
    ppermute x6 -> x0, starting transfers between devices: 8.38 us -> none  [sum_fsdp(): lax.ppermute(value, 'fsdp', [(j, (j - k) % size) for j in range(size)])]
  transfers between devices with their start and end apart: 15 -> 5, of which waited for: 7 -> 2; matrix products, arithmetic and copies ran while one was open for 20% -> 18% of each run, Pallas kernels for 0% -> 0%
where the time goes in v4:
time: 466 us; the launch traced here: 457 us
  Pallas kernels  307 us (66%)
  matrix products  60.9 us (13%)
  waiting for transfers between devices  33.3 us (7%)
  other arithmetic  20.6 us (4%)
  local copies, waits for them, and re-layouts  19.2 us (4%)
  between operations  14.5 us (3%)
    pallas_call x1, Pallas kernels, tail(): pl.pallas_call(functools.partial(tail_kernel, nz, nc, token_count), out_s...  108 us
    pallas_call x1, Pallas kernels, forward_attention(): pl.pallas_call(functools.partial(forward_kernel, nz, nc), out_shape=(jax....  106 us
    pallas_call x1, Pallas kernels, backward_attention(): pl.pallas_call(functools.partial(backward_kernel, nz, nc), out_shape=(jax...  92.5 us
    all_gather x1, waiting for transfers between devices, per_device(): down_full = lax.all_gather(down_part, 'context', axis=0, tiled=True)  29.1 us
    dot_general x3, matrix products, dot_tn(): lax.dot_general(a, b, (((0,), (0,)), ((), ())), preferred_element_type=F32)  19.8 us
    unnamed x50, local copies, waits for them, and re-layouts  13.1 us
    dot_general x1, matrix products, per_device(): jnp.einsum('isd,fd->isf', grad_mlp, down_full, preferred_element_type=F32)  10.8 us
  transfers between devices with their start and end apart: 5, of which 2 were waited for; matrix products, arithmetic and copies ran while one was open for 18% of the time, Pallas kernels for 0%

profile of v4, /device:TPU:0, one launch (start us, length us, event | category | flops | bytes accessed | tf_op | source)
XLA Modules:
  0.0 457.0 jit_solution(16683316748834268409)
XLA Ops:
  7.2 0.0 copy-start
  7.2 0.0 all-gather.2.cloned.1.call-start
  7.2 0.9 reduce_sum.81
  8.1 1.5 fusion.27
  9.6 0.1 copy.44
  9.8 0.8 copy.38.wq_ref
  10.6 0.7 broadcast_in_dim.10.count_ref
  11.3 106.5 %forward_attention.1 = (bf16[3,1408,1024]{2,1,0:T(8,128)(2,1)}, bf16[3,1408,384]{2,1,0:T(8,128)(2,1)}, bf16[3,1408,128]{2,1,0:T(8,128)(2,1)}, f32[3,16,1408]{2,1...) custom-call(f32[3,352,1024]{2,1,0:T(8,128)} %tokens_ref.3, ...), custom_call_target="tpu_custom_call" | custom-call | tf_op jit(solution)/shard_map/forward_attention/pallas_call | solution.py:474
  117.8 0.0 all-gather.2.cloned.1.call-update
  117.8 0.0 reduce-scatter.2.cloned.1.call-start
  117.8 2.8 convolution_convert_fusion
  120.7 0.2 collective-permute-start
  120.9 4.2 collective-permute-done
  125.0 4.0 fusion.26
  129.0 0.0 copy-done.4
  129.0 0.0 copy-start.2
  129.1 0.0 slice-start.2
  129.1 0.6 multiply_reduce_fusion.4
  129.7 3.2 copy-done.11
  132.9 8.3 %multiply_convert_fusion = (bf16[3,352,2048]{2,1,0:T(8,128)(2,1)S(1)}, f32[3,352,2048]{2,1,0:T(8,128)}) fusion(bf16[1024,2048]{1,0:T(8,128)(2,1)S(1)} %copy-done.11, f32[3,352,1024]{2,1,0:T(8,128)S(1)} %get-tuple-element.85, f32[1024]{0:T(1024)S(1)} %bitcast.81, f32[3,352]{1,0:T(4,128)S(1)} %add_rsqrt_fusion, f32[3,352]{1,0:T(4,128)S(1)} %broadcast_multiply_fusion.2), kind=kOutput, calls=%fused_computation.7 | convolution fusion | flops 4444323840 | bytes 21508352 | tf_op jit(solution)/shard_map/isd,df->isf/dot_general | solution.py:1495
  141.2 6.0 %bitcast_convert_fusion = bf16[2048,1024]{1,0:T(8,128)(2,1)S(1)} fusion(bf16[3,352,2048]{2,1,0:T(8,128)(2,1)S(1)} %get-tuple-element.94, f32[3,352,1024]{2,1,0:T(8,128)S(1)} %bitcast.67, f32[1024]{0:T(1024)S(1)} %bitcast.91), kind=kOutput, calls=%fused_computation.9 | convolution fusion | flops 4433444864 | bytes 12849152 | tf_op jit(solution)/shard_map/dot_general | solution.py:49
  147.3 2.5 copy.39
  149.7 0.0 reduce-scatter.2.cloned.1.call-update
  149.8 29.1 %all-gather.2.cloned.1.call-done = bf16[2048,1024]{1,0:T(8,128)(2,1)} async-done(((bf16[512,1024]{1,0:T(8,128)(2,1)}), bf16[2048,1024]{1,0:T(8,128)(2,1)}) %all-gather.2.cloned.1.call-update) | async-done | bytes 4194320 | tf_op jit(solution)/shard_map/all_gather | solution.py:1471
  178.9 10.8 %fusion.5 = bf16[3,352,2048]{2,1,0:T(8,128)(2,1)S(1)} fusion(f32[3,352,2048]{2,1,0:T(8,128)} %get-tuple-element.95, bf16[2048,1024]{1,0:T(8,128)(2,1)} %all-gather.2.cloned.1.call-done, f32[3,352,1024]{2,1,0:T(8,128)} %param.16, f32[1024]{0:T(1024)S(1)} %bitcast.92), kind=kOutput, calls=%fused_computation.6 | convolution fusion | flops 4452974592 | bytes 21499904 | tf_op jit(solution)/shard_map/isd,fd->isf/dot_general | solution.py:1504
  189.7 6.0 %fusion.15 = bf16[3,352,1024]{2,1,0:T(8,128)(2,1)} fusion(bf16[3,352,2048]{2,1,0:T(8,128)(2,1)S(1)} %fusion.5, bf16[1024,2048]{1,0:T(8,128)(2,1)S(1)} %copy-done.12), kind=kOutput, calls=%fused_computation.36 | convolution fusion | flops 4430266368 | bytes 10682368 | tf_op jit(solution)/shard_map/isf,df->isd/dot_general | solution.py:1507
  195.6 0.0 collective-permute-start.2
  195.6 0.0 slice-start
  195.7 8.2 %fusion.18 = bf16[3,352,1024]{2,1,0:T(8,128)(2,1)} fusion(bf16[3,352,2048]{2,1,0:T(8,128)(2,1)} %copy-done.16, bf16[2048,1024]{1,0:T(8,128)(2,1)S(1)} %copy-done.13), kind=kOutput, calls=%fused_computation.37 | convolution fusion | flops 4430266368 | bytes 10682368 | tf_op jit(solution)/shard_map/isf,fd->isd/dot_general | solution.py:1499
  203.9 0.7 collective-permute-start.1
  204.6 0.6 select_reduce_fusion.slot_blocks
  205.2 11.2 %bitcast_convert_fusion.1 = bf16[2048,1024]{1,0:T(8,128)(2,1)} fusion(bf16[3,352,2048]{2,1,0:T(8,128)(2,1)} %copy-done.17, f32[3,352,1024]{2,1,0:T(8,128)} %copy-done.2, f32[1024]{0:T(1024)S(1)} %bitcast.82, f32[3,352]{1,0:T(4,128)S(1)} %add_rsqrt_fusion, f32[3,352]{1,0:T(4,128)S(1)} %broadcast_multiply_fusion.2), kind=kOutput, calls=%fused_computation.10 | convolution fusion | flops 4435607552 | bytes 12857600 | tf_op jit(solution)/shard_map/dot_general | solution.py:49
  216.3 0.0 collective-permute-done.2
  216.4 4.4 multiply_reduce_fusion.2
  220.8 0.0 collective-permute-done.1
  220.8 8.8 %multiply_reduce_fusion = (f32[1024]{0:T(1024)S(1)}, f32[3,352,1024]{2,1,0:T(8,128)}, f32[1024]{0:T(1024)S(1)}, f32[3,352,1024]{2,1,0:T(8,128)}) fusion(f32[3,352,1024]{2,1,0:T(8,128)} %param.16, bf16[3,352,1024]{2,1,0:T(8,128)(2,1)} %collective-permute-done.1, bf16[3,352,1024]{2,1,0:T(8,128)(2,1)} %fusion.18, f32[3,352,1024]{2,1,0:T(8,128)S(1)} %bitcast.64, ...), kind=kLoop, calls=%fused_computation.11 | loop fusion | flops 24868864 | bytes 30310912 | tf_op jit(solution)/shard_map/reduce_sum | solution.py:1534
  229.6 0.7 stack.19.gains_ref
  230.3 5.1 %convolution_convert_fusion.1.att_ref = bf16[3,352,512]{2,1,0:T(8,128)(2,1)} fusion(bf16[512,1024]{1,0:T(8,128)(2,1)} %get-tuple-element.30, f32[3,352,1024]{2,1,0:T(8,128)} %get-tuple-element.89.mid_ref, f32[1024]{0:T(1024)S(1)} %bitcast.89), kind=kOutput, calls=%fused_computation.39 | convolution fusion | flops 1109999616 | bytes 6459392 | tf_op jit(solution)/shard_map/isd,hd->ish/dot_general | solution.py:1512
  235.3 2.6 bitcast_convert_fusion.2
  237.9 92.5 %backward_attention.1 = (bf16[9,32,1024]{2,1,0:T(8,128)(2,1)}, bf16[3,32,1024]{2,1,0:T(8,128)(2,1)}, bf16[3,1408,384]{2,1,0:T(8,128)(2,1)}, bf16[1024,1536]{1,0:T(8,128)(2,1)}) custom-call(bf16[3,1408,384]{2,1,0:T(8,128)(2,1)} %get-tuple-element.33.qkv_ref, bf16[3,1408,128]{2,1,0:T(8,128)(2,1)} %get-tuple-element.34.o_ref, ...), custom_call_target="tpu_custom_call" | custom-call | tf_op jit(solution)/shard_map/backward_attention/pallas_call | solution.py:774
  330.5 0.0 copy-start.10
  330.5 108.4 %tail.1 = (f32[3,352,1024]{2,1,0:T(8,128)}, f32[8,1024]{1,0:T(8,128)}, f32[3,128,1024]{2,1,0:T(8,128)}, f32[3,128,1024]{2,1,0:T(8,128)}, f32[3,128,1024]{2,1,0:T(8,128)}, /*index=5*/f32[3,128,1024]{2,1,0:T(8,128)}) custom-call(s32[12]{0:T(128)} %select_reduce_fusion.slot_blocks, bf16[9,32,1024]{2,1,0:T(8,128)(2,1)} %get-tuple-element.39.early_ref, ...), custom_call_target="tpu_custom_call" | custom-call | tf_op jit(solution)/shard_map/tail/pallas_call | solution.py:1180
  438.9 1.4 multiply_subtract_fusion
  440.2 5.1 %copy.50 = f32[3,352,1024]{2,1,0:T(8,128)} copy(f32[3,352,1024]{2,1,0:T(8,128)} %get-tuple-element.108) | data formatting | bytes 8650752
  445.3 1.1 copy.51
  446.5 1.1 copy.52
  447.6 1.1 copy.53
  448.8 1.1 copy.54
  (47 shorter events, 0.1 us)
Async XLA Ops:
  7.2 2.4 copy-start
  7.2 171.7 %all-gather.2.cloned.1.call-start = ((), (), s32[]{:S(2)}) async-start(), calls=%async_computation.1 | async-start | bytes 5242880 | tf_op jit(solution)/shard_map/all_gather | solution.py:1471
  117.8 120.1 %reduce-scatter.2.cloned.1.call-start = ((), (), s32[]{:S(2)}) async-start(), calls=%async_computation.2 | async-start | bytes 5242880 | tf_op jit(solution)/shard_map/reduce_scatter | solution.py:1525
  120.7 4.3 collective-permute-start
  125.0 4.0 copy-start.4
  129.0 12.2 %copy-start.2 = (f32[3,352,1024]{2,1,0:T(8,128)}, f32[3,352,1024]{2,1,0:T(8,128)S(1)}, u32[]{:S(2)}) copy-start(f32[3,352,1024]{2,1,0:T(8,128)S(1)} %get-tuple-element.85) | copy-start | bytes 12976132
  129.0 3.9 copy-start.11
  129.1 12.1 %slice-start.2 = ((s8[4325376]{0:T(1024)(128)(4,1)}), s8[4194304]{0:T(1024)(128)(4,1)S(1)}, s32[]{:S(2)}) async-start(s8[4325376]{0:T(1024)(128)(4,1)} %bitcast.66), calls=%async_computation.5 | async-start | bytes 8388608
  132.9 8.3 %slice-start.3 = ((s8[4325376]{0:T(1024)(128)(4,1)}), s8[131072]{0:T(1024)(128)(4,1)S(1)}, s32[]{:S(2)}) async-start(s8[4325376]{0:T(1024)(128)(4,1)} %bitcast.66), calls=%async_computation.6 | async-start | bytes 262144
  141.2 6.1 %copy-start.16 = (bf16[3,352,2048]{2,1,0:T(8,128)(2,1)}, bf16[3,352,2048]{2,1,0:T(8,128)(2,1)S(1)}, u32[]{:S(2)}) copy-start(bf16[3,352,2048]{2,1,0:T(8,128)(2,1)S(1)} %get-tuple-element.94) | copy-start | bytes 12976132
  178.9 10.8 %copy-start.12 = (bf16[1024,2048]{1,0:T(8,128)(2,1)S(1)}, bf16[1024,2048]{1,0:T(8,128)(2,1)}, u32[]{:S(2)}) copy-start(bf16[1024,2048]{1,0:T(8,128)(2,1)} %get-tuple-element.31) | copy-start | bytes 12582916
  189.7 6.0 %copy-start.17 = (bf16[3,352,2048]{2,1,0:T(8,128)(2,1)}, bf16[3,352,2048]{2,1,0:T(8,128)(2,1)S(1)}, u32[]{:S(2)}) copy-start(bf16[3,352,2048]{2,1,0:T(8,128)(2,1)S(1)} %fusion.5) | copy-start | bytes 12976132
  189.7 6.0 %copy-start.13 = (bf16[2048,1024]{1,0:T(8,128)(2,1)S(1)}, bf16[2048,1024]{1,0:T(8,128)(2,1)}, u32[]{:S(2)}) copy-start(bf16[2048,1024]{1,0:T(8,128)(2,1)} %all-gather.2.cloned.1.call-done) | copy-start | bytes 12582916
  195.6 8.9 %copy-start.15 = (s32[12]{0:T(128)S(1)}, s32[12]{0:T(128)}, u32[]{:S(2)}) copy-start(s32[12]{0:T(128)} %param.23) | copy-start | bytes 148
  195.6 20.7 %collective-permute-start.2 = (bf16[3,352,1024]{2,1,0:T(8,128)(2,1)}, bf16[3,352,1024]{2,1,0:T(8,128)(2,1)}, u32[]{:S(2)}, u32[]{:S(2)}) collective-permute-start(bf16[3,352,1024]{2,1,0:T(8,128)(2,1)} %fusion.15), channel_id=1, source_target_pairs={{0,1},{1,0},{2,3},{3,2},{4,5},{5,4},{6,7},{7,6},{8,9},{9,8},{10,11... | collective-permute-start | bytes 6488072 | tf_op jit(solution)/shard_map/ppermute | solution.py:1244
  195.6 20.7 %slice-start = ((s8[4325376]{0:T(1024)(128)(4,1)}), s8[131072]{0:T(1024)(128)(4,1)S(1)}, s32[]{:S(2)}) async-start(s8[4325376]{0:T(1024)(128)(4,1)} %bitcast.63), calls=%async_computation.3 | async-start | bytes 262144
  203.9 16.9 %collective-permute-start.1 = (bf16[3,352,1024]{2,1,0:T(8,128)(2,1)}, bf16[3,352,1024]{2,1,0:T(8,128)(2,1)}, u32[]{:S(2)}, u32[]{:S(2)}) collective-permute-start(bf16[3,352,1024]{2,1,0:T(8,128)(2,1)} %fusion.18), channel_id=1, source_target_pairs={{0,1},{1,0},{2,3},{3,2},{4,5},{5,4},{6,7},{7,6},{8,9},{9,8},{10,11... | collective-permute-start | bytes 6488072 | tf_op jit(solution)/shard_map/ppermute | solution.py:1244
  205.2 11.2 %slice-start.1 = ((s8[4325376]{0:T(1024)(128)(4,1)}), s8[4194304]{0:T(1024)(128)(4,1)S(1)}, s32[]{:S(2)}) async-start(s8[4325376]{0:T(1024)(128)(4,1)} %bitcast.63), calls=%async_computation.4 | async-start | bytes 8388608
  216.3 4.5 copy-start.5
  229.6 5.8 %copy-start.14 = (bf16[3,352,512]{2,1,0:T(8,128)(2,1)S(1)}, bf16[3,352,512]{2,1,0:T(8,128)(2,1)}, u32[]{:S(2)}) copy-start(bf16[3,352,512]{2,1,0:T(8,128)(2,1)} %get-tuple-element.29) | copy-start | bytes 3244036
  230.3 5.1 %copy-start.3 = (f32[3,352,1024]{2,1,0:T(8,128)S(1)}, f32[3,352,1024]{2,1,0:T(8,128)}, u32[]{:S(2)}) copy-start(f32[3,352,1024]{2,1,0:T(8,128)} %get-tuple-element.89.mid_ref) | copy-start | bytes 12976132
  330.5 108.4 %copy-start.10 = (f32[4,64]{1,0:T(4,128)S(1)}, f32[4,64]{1,0:T(4,128)}, u32[]{:S(2)}) copy-start(f32[4,64]{1,0:T(4,128)} %param.29) | copy-start | bytes 3076
  440.2 5.1 %copy-start.9 = (f32[3,128,1024]{2,1,0:T(8,128)S(1)}, f32[3,128,1024]{2,1,0:T(8,128)}, u32[]{:S(2)}) copy-start(f32[3,128,1024]{2,1,0:T(8,128)} %get-tuple-element.44) | copy-start | bytes 4718596
  440.2 6.2 %copy-start.8 = (f32[3,128,1024]{2,1,0:T(8,128)S(1)}, f32[3,128,1024]{2,1,0:T(8,128)}, u32[]{:S(2)}) copy-start(f32[3,128,1024]{2,1,0:T(8,128)} %get-tuple-element.45) | copy-start | bytes 4718596
  445.3 2.3 copy-start.7
  445.3 3.4 copy-start.6
  445.3 4.6 %copy-start.1 = (bf16[256,3,512]{2,0,1:T(8,128)(2,1)S(1)}, bf16[256,3,512]{2,0,1:T(8,128)(2,1)}, u32[]{:S(2)}) copy-start(bf16[256,3,512]{2,0,1:T(8,128)(2,1)} %param.18) | copy-start | bytes 2359300
Sparse Core Ops, SparseCore 0:
  117.9 60.8 all-gather.1
  181.8 52.6 reduce-scatter.1
